TPU v7x, 32 devices: a whole 2x2x4 slice. The times are simulated.
32 devices in a mesh: fsdp: 8 (over z, x), dp: 4 (over y, core).
Axes of the slice: x: 2, y: 2, z: 4, core: 2. Of those that a mesh axis runs over, the one named last changes fastest.
Arguments:
- hidden: bfloat16 [2, 32, 384, 1536], P(None, ('fsdp', 'dp')), may hold values from -6 to 6
- teacher: bfloat16 [2, 32, 384, 1536], P(None, ('fsdp', 'dp')), may hold values from -6 to 6
- cotangent: bfloat16 [2, 32, 384, 1536], P(None, ('fsdp', 'dp')), may hold values from -6.3329935e-07 to 6.3329935e-07
- valid_mask: int32 [2, 32, 384], P(None, ('fsdp', 'dp')), may hold values from 0 to 1, as said below
- blocks: int32 [2, 32, 384], P(None, ('fsdp', 'dp')), may hold values from 0 to 2, never falling along the last dimension, each value on 1 to 256 neighbouring positions
- buckets: int32 [384, 384], replicated, may hold values from 0 to 31
- first_gain: bfloat16 [1536], P(('fsdp', 'dp')), may hold values from 0.25 to 1.75
- query_weight: bfloat16 [1536, 768], P('fsdp', 'dp'), may hold values from -0.0390625 to 0.0390625
- key_weight: bfloat16 [1536, 768], P('fsdp', 'dp'), may hold values from -0.15625 to 0.15625
- value_weight: bfloat16 [1536, 768], P('fsdp', 'dp'), may hold values from -0.15625 to 0.15625
- output_weight: bfloat16 [1536, 768], P('fsdp', 'dp'), may hold values from -1.25 to 1.25
- second_gain: bfloat16 [1536], P(('fsdp', 'dp')), may hold values from 0.25 to 1.75
- gate_weight: bfloat16 [1536, 3968], P('fsdp', 'dp'), may hold values from -0.15625 to 0.15625
- up_weight: bfloat16 [1536, 3968], P('fsdp', 'dp'), may hold values from -0.15625 to 0.15625
- down_weight: bfloat16 [1536, 3968], P('fsdp', 'dp'), may hold values from -0.1875 to 0.1875
- bias_table: bfloat16 [32, 12], replicated, may hold values from -5 to 5
Outputs:
- layer_output: bfloat16 [2, 32, 384, 1536], P(None, ('fsdp', 'dp'))
- loss_value: float32 [], replicated
- hidden_grad: bfloat16 [2, 32, 384, 1536], P(None, ('fsdp', 'dp'))
- first_gain_grad: float32 [1536], P(('fsdp', 'dp'))
- query_grad: float32 [1536, 768], P('fsdp', 'dp')
- key_grad: float32 [1536, 768], P('fsdp', 'dp')
- value_grad: float32 [1536, 768], P('fsdp', 'dp')
- output_grad: float32 [1536, 768], P('fsdp', 'dp')
- second_gain_grad: float32 [1536], P(('fsdp', 'dp'))
- gate_grad: float32 [1536, 3968], P('fsdp', 'dp')
- up_grad: float32 [1536, 3968], P('fsdp', 'dp')
- down_grad: float32 [1536, 3968], P('fsdp', 'dp')
- bias_grad: float32 [32, 12], replicated
Inputs may be any that keep to these rules, and one draw needn't show every extreme that they name: `valid_mask`: 1 marks a valid token. `blocks`: never falls along a sequence; every block number up to the largest occurs, each block has 1 to 256 positions and some block has exactly 256.
All inputs are finite; a program needn't handle non-finite values.
Results may differ from a plain program's by a relative error of at most 0.013.
The roundings to bfloat16 on the way count: a program that leaves them out, or rounds other values in their place, can miss the bound.
Values may be sent and summed in bfloat16 or wider, within the bound.
A program may use at most 320 MiB of HBM per device.

v0:
```python
import jax
import jax.numpy as jnp
from jax import lax
from jax.sharding import PartitionSpec as P

EPS = 1e-06
NEG = -1000000000.0
HIGH = lax.Precision.HIGHEST


def times_rows(former, latter):
    return jnp.dot(former, latter, preferred_element_type=jnp.float32)


def times_transpose(former, latter):
    return lax.dot_general(
        former, latter, (((1,), (1,)), ((), ())), preferred_element_type=jnp.float32
    )


def over_tokens(former, latter):
    return lax.dot_general(
        former, latter, (((0,), (0,)), ((), ())), preferred_element_type=jnp.float32
    )


def assemble(gathered, fsdp_count, dp_count):
    row_block = gathered.shape[0] // (fsdp_count * dp_count)
    col_block = gathered.shape[1]
    shaped = gathered.reshape(fsdp_count, dp_count, row_block, col_block)
    return jnp.transpose(shaped, (0, 2, 1, 3)).reshape(fsdp_count * row_block, dp_count * col_block)


def disperse(gradient, fsdp_count, dp_count):
    row_block = gradient.shape[0] // fsdp_count
    col_block = gradient.shape[1] // dp_count
    shaped = gradient.reshape(fsdp_count, row_block, dp_count, col_block)
    return jnp.transpose(shaped, (0, 2, 1, 3)).reshape(fsdp_count * dp_count * row_block, col_block)


def norm_forward(inputs, norm_gain):
    row_scale = lax.rsqrt(jnp.mean(inputs * inputs, axis=-1, keepdims=True) + EPS)
    return (inputs * row_scale * norm_gain, row_scale)


def norm_backward(inputs, row_scale, norm_gain, upstream):
    scaled = upstream * norm_gain
    gain_grad = jnp.sum(upstream * inputs * row_scale, axis=0)
    mean_term = jnp.mean(scaled * inputs, axis=-1, keepdims=True)
    return (
        row_scale * scaled - inputs * (row_scale * row_scale * row_scale) * mean_term,
        gain_grad,
    )


def gelu_tanh(values_in):
    return jax.nn.gelu(values_in, approximate=True)


def masked_scores(queries, key_heads, position_bias, allowed):
    products = jnp.einsum("qhd,khd->hqk", queries, key_heads, preferred_element_type=jnp.float32)
    return jnp.where(allowed[None], products + position_bias, NEG)


def body(
    hidden,
    teacher,
    cotangent,
    valid_mask,
    blocks,
    buckets,
    first_gain,
    query_weight,
    key_weight,
    value_weight,
    output_weight,
    second_gain,
    gate_weight,
    up_weight,
    down_weight,
    bias_table,
):
    fsdp_count = lax.axis_size("fsdp")
    dp_count = lax.axis_size("dp")
    micro_count = hidden.shape[0]
    seq_len = hidden.shape[2]
    model_width = hidden.shape[3]
    bucket_count = bias_table.shape[0]
    head_count = bias_table.shape[1]
    scale_factor = jnp.float32(
        float(micro_count * lax.axis_size(("fsdp", "dp")) * hidden.shape[1] * seq_len * model_width)
    )
    valid_float = valid_mask.astype(jnp.float32)
    valid_total = lax.psum(jnp.sum(valid_float), ("fsdp", "dp"))
    places = lax.broadcasted_iota(jnp.int32, (1, 1, bucket_count), 2)
    onehot = (buckets[:, :, None] == places).astype(jnp.float32)
    position_bias = jnp.einsum(
        "qkb,bh->hqk", onehot, bias_table.astype(jnp.float32), precision=HIGH
    )
    onehot_low = onehot.astype(jnp.bfloat16)
    rows_iota = lax.broadcasted_iota(jnp.int32, (seq_len, seq_len), 0)
    cols_iota = lax.broadcasted_iota(jnp.int32, (seq_len, seq_len), 1)
    diagonal = rows_iota == cols_iota

    def rebuild(gathered):
        return (gathered[0],) + tuple(
            (assemble(matrix, fsdp_count, dp_count) for matrix in gathered[1:])
        )

    def spread_out(grads):
        return (
            (grads[0],)
            + tuple((disperse(matrix, fsdp_count, dp_count) for matrix in grads[1:5]))
            + (grads[5],)
            + tuple((disperse(matrix, fsdp_count, dp_count) for matrix in grads[6:]))
        )

    outputs_list = []
    input_grads = []
    squares = jnp.float32(0.0)
    table_grad = jnp.zeros((bucket_count, head_count), jnp.float32)
    totals = None
    for step_index in range(micro_count):
        inputs = hidden[step_index, 0].astype(jnp.float32)
        target = teacher[step_index, 0].astype(jnp.float32)
        upstream = cotangent[step_index, 0].astype(jnp.float32)
        token_valid = valid_float[step_index, 0]
        block_ids = blocks[step_index, 0]
        allowed = (block_ids[None, :] <= block_ids[:, None]) & (
            valid_mask[step_index, 0][None, :] == 1
        ) | diagonal
        first_block = rebuild(
            (
                lax.all_gather(first_gain, ("fsdp", "dp"), axis=0, tiled=True),
                lax.all_gather(query_weight, ("fsdp", "dp"), axis=0, tiled=True),
                lax.all_gather(key_weight, ("fsdp", "dp"), axis=0, tiled=True),
                lax.all_gather(value_weight, ("fsdp", "dp"), axis=0, tiled=True),
                lax.all_gather(output_weight, ("fsdp", "dp"), axis=0, tiled=True),
            )
        )
        gain_one = first_block[0].astype(jnp.float32)
        normed_full, scale_one = norm_forward(inputs, gain_one)
        normed_one = normed_full.astype(jnp.bfloat16)
        head_size = first_block[1].shape[1] // head_count
        head_split = (seq_len, head_count, head_size)
        queries = times_rows(normed_one, first_block[1]).astype(jnp.bfloat16).reshape(head_split)
        key_heads = times_rows(normed_one, first_block[2]).astype(jnp.bfloat16).reshape(head_split)
        value_heads = (
            times_rows(normed_one, first_block[3]).astype(jnp.bfloat16).reshape(head_split)
        )
        scores = masked_scores(queries, key_heads, position_bias, allowed)
        row_max = jnp.max(scores, axis=-1, keepdims=True)
        exponent = jnp.exp(scores - row_max)
        row_total = jnp.sum(exponent, axis=-1, keepdims=True)
        log_total = row_max + jnp.log(row_total)
        softmax_low = (exponent / row_total).astype(jnp.bfloat16)
        attended = jnp.einsum(
            "hqk,khd->qhd", softmax_low, value_heads, preferred_element_type=jnp.float32
        )
        attended = attended.astype(jnp.bfloat16).reshape(seq_len, head_count * head_size)
        middle = inputs + times_transpose(attended, first_block[4])
        second_block = rebuild(
            (
                lax.all_gather(second_gain, ("fsdp", "dp"), axis=0, tiled=True),
                lax.all_gather(gate_weight, ("fsdp", "dp"), axis=0, tiled=True),
                lax.all_gather(up_weight, ("fsdp", "dp"), axis=0, tiled=True),
                lax.all_gather(down_weight, ("fsdp", "dp"), axis=0, tiled=True),
            )
        )
        gain_two = second_block[0].astype(jnp.float32)
        normed_mid, scale_two = norm_forward(middle, gain_two)
        normed_two = normed_mid.astype(jnp.bfloat16)
        gate_pre = times_rows(normed_two, second_block[1])
        up_pre = times_rows(normed_two, second_block[2])
        gate_act, gelu_pullback = jax.vjp(gelu_tanh, gate_pre)
        hidden_act = (gate_act * up_pre).astype(jnp.bfloat16)
        layer_full = middle + times_transpose(hidden_act, second_block[3])
        outputs_list.append(layer_full.astype(jnp.bfloat16))
        residual_gap = layer_full - target
        weighted_gap = token_valid[:, None] * residual_gap
        squares = squares + jnp.sum(weighted_gap * residual_gap)
        grad_out = scale_factor * upstream + scale_factor * (
            2.0 * weighted_gap / (valid_total * model_width)
        )
        back_second = rebuild(
            (
                lax.all_gather(second_gain, ("fsdp", "dp"), axis=0, tiled=True),
                lax.all_gather(gate_weight, ("fsdp", "dp"), axis=0, tiled=True),
                lax.all_gather(up_weight, ("fsdp", "dp"), axis=0, tiled=True),
                lax.all_gather(down_weight, ("fsdp", "dp"), axis=0, tiled=True),
            )
        )
        grad_ffn = grad_out.astype(jnp.bfloat16)
        down_part = over_tokens(grad_ffn, hidden_act)
        grad_hidden_act = times_rows(grad_ffn, back_second[3])
        grad_gate = gelu_pullback(grad_hidden_act * up_pre)[0].astype(jnp.bfloat16)
        grad_up = (grad_hidden_act * gate_act).astype(jnp.bfloat16)
        gate_part = over_tokens(normed_two, grad_gate)
        up_part = over_tokens(normed_two, grad_up)
        grad_normed_two = times_transpose(grad_gate, back_second[1]) + times_transpose(
            grad_up, back_second[2]
        )
        middle_term, gain_two_part = norm_backward(
            middle, scale_two, back_second[0].astype(jnp.float32), grad_normed_two
        )
        grad_middle = grad_out + middle_term
        grad_attn = grad_middle.astype(jnp.bfloat16)
        back_first = rebuild(
            (
                lax.all_gather(first_gain, ("fsdp", "dp"), axis=0, tiled=True),
                lax.all_gather(query_weight, ("fsdp", "dp"), axis=0, tiled=True),
                lax.all_gather(key_weight, ("fsdp", "dp"), axis=0, tiled=True),
                lax.all_gather(value_weight, ("fsdp", "dp"), axis=0, tiled=True),
                lax.all_gather(output_weight, ("fsdp", "dp"), axis=0, tiled=True),
            )
        )
        output_part = over_tokens(grad_attn, attended)
        grad_attended = (
            times_rows(grad_attn, back_first[4]).astype(jnp.bfloat16).reshape(head_split)
        )
        scores_again = masked_scores(queries, key_heads, position_bias, allowed)
        softmax_again = jnp.exp(scores_again - log_total)
        grad_probs = jnp.einsum(
            "qhd,khd->hqk", grad_attended, value_heads, preferred_element_type=jnp.float32
        )
        grad_scores = softmax_again * (
            grad_probs - jnp.sum(softmax_again * grad_probs, axis=-1, keepdims=True)
        )
        grad_scores = grad_scores.astype(jnp.bfloat16)
        table_grad = table_grad + jnp.einsum(
            "hqk,qkb->bh", grad_scores, onehot_low, preferred_element_type=jnp.float32
        )
        flat_width = head_count * head_size
        grad_queries = (
            jnp.einsum("hqk,khd->qhd", grad_scores, key_heads, preferred_element_type=jnp.float32)
            .astype(jnp.bfloat16)
            .reshape(seq_len, flat_width)
        )
        grad_keys = (
            jnp.einsum("hqk,qhd->khd", grad_scores, queries, preferred_element_type=jnp.float32)
            .astype(jnp.bfloat16)
            .reshape(seq_len, flat_width)
        )
        grad_values = (
            jnp.einsum(
                "hqk,qhd->khd",
                softmax_again.astype(jnp.bfloat16),
                grad_attended,
                preferred_element_type=jnp.float32,
            )
            .astype(jnp.bfloat16)
            .reshape(seq_len, flat_width)
        )
        query_part = over_tokens(normed_one, grad_queries)
        key_part = over_tokens(normed_one, grad_keys)
        value_part = over_tokens(normed_one, grad_values)
        grad_normed_one = (
            times_transpose(grad_queries, back_first[1])
            + times_transpose(grad_keys, back_first[2])
            + times_transpose(grad_values, back_first[3])
        )
        input_term, gain_one_part = norm_backward(
            inputs, scale_one, back_first[0].astype(jnp.float32), grad_normed_one
        )
        input_grads.append((grad_middle + input_term).astype(jnp.bfloat16))
        step_set = spread_out(
            (
                gain_one_part,
                query_part,
                key_part,
                value_part,
                output_part,
                gain_two_part,
                gate_part,
                up_part,
                down_part,
            )
        )
        totals = step_set if totals is None else jax.tree.map(jnp.add, totals, step_set)
    shards = (
        lax.psum_scatter(totals[0], ("fsdp", "dp"), scatter_dimension=0, tiled=True),
        lax.psum_scatter(totals[1], ("fsdp", "dp"), scatter_dimension=0, tiled=True),
        lax.psum_scatter(totals[2], ("fsdp", "dp"), scatter_dimension=0, tiled=True),
        lax.psum_scatter(totals[3], ("fsdp", "dp"), scatter_dimension=0, tiled=True),
        lax.psum_scatter(totals[4], ("fsdp", "dp"), scatter_dimension=0, tiled=True),
        lax.psum_scatter(totals[5], ("fsdp", "dp"), scatter_dimension=0, tiled=True),
        lax.psum_scatter(totals[6], ("fsdp", "dp"), scatter_dimension=0, tiled=True),
        lax.psum_scatter(totals[7], ("fsdp", "dp"), scatter_dimension=0, tiled=True),
        lax.psum_scatter(totals[8], ("fsdp", "dp"), scatter_dimension=0, tiled=True),
    )
    total_squares, table_all = lax.psum((squares, table_grad), ("fsdp", "dp"))
    loss_value = total_squares / (valid_total * model_width)
    layer_output = jnp.stack(outputs_list)[:, None]
    hidden_grad = jnp.stack(input_grads)[:, None]
    return (
        layer_output,
        loss_value,
        hidden_grad,
        shards[0],
        shards[1],
        shards[2],
        shards[3],
        shards[4],
        shards[5],
        shards[6],
        shards[7],
        shards[8],
        table_all,
    )


def solution(mesh):
    in_specs = (
        P(None, ("fsdp", "dp"), None, None),
        P(None, ("fsdp", "dp"), None, None),
        P(None, ("fsdp", "dp"), None, None),
        P(None, ("fsdp", "dp"), None),
        P(None, ("fsdp", "dp"), None),
        P(),
        P(("fsdp", "dp")),
        P("fsdp", "dp"),
        P("fsdp", "dp"),
        P("fsdp", "dp"),
        P("fsdp", "dp"),
        P(("fsdp", "dp")),
        P("fsdp", "dp"),
        P("fsdp", "dp"),
        P("fsdp", "dp"),
        P(),
    )
    out_specs = (
        P(None, ("fsdp", "dp"), None, None),
        P(),
        P(None, ("fsdp", "dp"), None, None),
        P(("fsdp", "dp")),
        P("fsdp", "dp"),
        P("fsdp", "dp"),
        P("fsdp", "dp"),
        P("fsdp", "dp"),
        P(("fsdp", "dp")),
        P("fsdp", "dp"),
        P("fsdp", "dp"),
        P("fsdp", "dp"),
        P(),
    )
    return jax.shard_map(body, mesh=mesh, in_specs=in_specs, out_specs=out_specs, check_vma=False)
```

profile of v0, /device:TPU:0, one launch (start us, length us, event | category | flops | bytes accessed | tf_op | source)
XLA Modules:
  0.0 2003.2 jit_solution(12041364364537936734)
XLA Ops:
  13.3 42.2 %psum.22 = f32[]{:T(128)} all-reduce(f32[]{:T(128)} %convert_reduce_fusion), channel_id=1, replica_groups=mesh['fsdp'=8,'dp'=4] {'fsdp','dp'}, use_global_device_ids=true, to_apply=%region_12.13 | all-reduce | flops 1 | bytes 8 | tf_op jit(solution)/shard_map/psum | solution.py:94
  57.9 40.4 %all-reduce.5 = (bf16[1536]{0:T(1024)(128)(2,1)S(1)}, bf16[1536]{0:T(1024)(128)(2,1)S(1)}) all-reduce(bf16[1536]{0:T(1024)(128)(2,1)S(1)} %dynamic-update-slice, bf16[1536]{0:T(1024)(128)(2,1)S(1)} %dynamic-update-slice.1), channel_id=1, replica_groups=mesh['fsdp'=8,'dp'=4] {'fsdp','dp'}, use_global_device_ids=true, to_apply=%add | all-reduce | flops 3072 | bytes 12288
  145.1 49.3 %all-gather.8.cloned.1.call-done = bf16[6144,192]{1,0:T(8,128)(2,1)} async-done(((bf16[192,192]{1,0:T(8,128)(2,1)}), bf16[6144,192]{1,0:T(8,128)(2,1)}) %all-gather.8.cloned.1.call-update) | async-done | bytes 2359312 | tf_op jit(solution)/shard_map/all_gather | solution.py:137
  205.9 49.1 %all-gather.14.cloned.1.call-done = bf16[6144,192]{1,0:T(8,128)(2,1)} async-done(((bf16[192,192]{1,0:T(8,128)(2,1)}), bf16[6144,192]{1,0:T(8,128)(2,1)}) %all-gather.14.cloned.1.call-update) | async-done | bytes 2359312 | tf_op jit(solution)/shard_map/all_gather | solution.py:138
  327.5 25.1 %all-gather.16.cloned.1.call-done = bf16[6144,992]{1,0:T(8,128)(2,1)} async-done(((bf16[192,992]{1,0:T(8,128)(2,1)}), bf16[6144,992]{1,0:T(8,128)(2,1)}) %all-gather.16.cloned.1.call-update) | async-done | bytes 12189712 | tf_op jit(solution)/shard_map/all_gather | solution.py:165
  352.6 15.6 copy.177
  368.2 25.0 %reshape.544 = bf16[1536,3968]{1,0:T(8,128)(2,1)} reshape(bf16[8,192,4,992]{3,2,1,0:T(4,128)(2,1)} %bitcast.396) | data formatting | bytes 24379392 | tf_op jit(solution)/shard_map/reshape | solution.py:31
  393.2 56.5 %all-gather.18.cloned.1.call-done = bf16[6144,992]{1,0:T(8,128)(2,1)} async-done(((bf16[192,992]{1,0:T(8,128)(2,1)}), bf16[6144,992]{1,0:T(8,128)(2,1)}) %all-gather.18.cloned.1.call-update) | async-done | bytes 12189712 | tf_op jit(solution)/shard_map/all_gather | solution.py:166
  449.7 15.6 copy.176
  465.3 25.1 %reshape.546 = bf16[1536,3968]{1,0:T(8,128)(2,1)} reshape(bf16[8,192,4,992]{3,2,1,0:T(4,128)(2,1)} %bitcast.397) | data formatting | bytes 24379392 | tf_op jit(solution)/shard_map/reshape | solution.py:31
  490.4 56.4 %all-gather.20.cloned.1.call-done = bf16[6144,992]{1,0:T(8,128)(2,1)} async-done(((bf16[192,992]{1,0:T(8,128)(2,1)}), bf16[6144,992]{1,0:T(8,128)(2,1)}) %all-gather.20.cloned.1.call-update) | async-done | bytes 12189712 | tf_op jit(solution)/shard_map/all_gather | solution.py:167
  546.8 15.6 copy.175
  562.4 25.0 %reshape.548 = bf16[1536,3968]{1,0:T(8,128)(2,1)} reshape(bf16[8,192,4,992]{3,2,1,0:T(4,128)(2,1)} %bitcast.398) | data formatting | bytes 24379392 | tf_op jit(solution)/shard_map/reshape | solution.py:31
  655.1 17.2 multiply_convert_fusion.3
  683.1 15.5 multiply_convert_fusion.2
  719.4 19.4 multiply_reduce_fusion.2
  837.4 13.9 fusion.106
  851.4 17.0 convolution_add_fusion
  868.4 32.6 %add.290 = f32[8,192,4,992]{3,2,1,0:T(4,128)} reshape(f32[1536,3968]{1,0:T(8,128)} %convolution_add_fusion) | data formatting | bytes 48758784 | tf_op jit(solution)/shard_map/add | solution.py:279
  900.9 25.3 %copy.140 = f32[8,4,192,992]{3,2,1,0:T(8,128)} copy(f32[8,4,192,992]{3,1,2,0:T(4,128)} %bitcast.393) | data formatting | bytes 48758784 | tf_op jit(solution)/shard_map/add | solution.py:279
  941.1 17.0 convolution_add_fusion.1
  958.1 32.6 %add.286 = f32[8,192,4,992]{3,2,1,0:T(4,128)} reshape(f32[1536,3968]{1,0:T(8,128)} %convolution_add_fusion.1) | data formatting | bytes 48758784 | tf_op jit(solution)/shard_map/add | solution.py:279
  990.7 24.9 %copy.139 = f32[8,4,192,992]{3,2,1,0:T(8,128)} copy(f32[8,4,192,992]{3,1,2,0:T(4,128)} %bitcast.394) | data formatting | bytes 48758784 | tf_op jit(solution)/shard_map/add | solution.py:279
  1016.1 14.0 fusion.131
  1030.1 17.5 convolution_add_fusion.2
  1047.6 32.6 %add.282 = f32[8,192,4,992]{3,2,1,0:T(4,128)} reshape(f32[1536,3968]{1,0:T(8,128)} %convolution_add_fusion.2) | data formatting | bytes 48758784 | tf_op jit(solution)/shard_map/add | solution.py:279
  1080.2 25.1 %copy.138 = f32[8,4,192,992]{3,2,1,0:T(8,128)} copy(f32[8,4,192,992]{3,1,2,0:T(4,128)} %bitcast.395) | data formatting | bytes 48758784 | tf_op jit(solution)/shard_map/add | solution.py:279
  1116.6 40.0 %all-reduce.4 = (f32[]{:T(128)}, f32[1536]{0:T(1024)}, f32[1536]{0:T(1024)}, f32[32,12]{0,1:T(8,128)}) all-reduce(f32[]{:T(128)S(6)} %add.252, f32[1536]{0:T(1024)} %add.267, f32[1536]{0:T(1024)} %add.280, f32[32,12]{0,1:T(8,128)} %fusion.98), channel_id=1, replica_groups=mesh['fsdp'=8,'dp'=4] {'fsdp','dp'}, use_global_device_ids=true, to_apply=%region_10.11 | all-reduce | flops 3457 | bytes 27656 | tf_op jit(solution)/shard_map/psum | solution.py:291
  1168.7 70.0 %reduce-scatter.8.cloned.1.call-done = f32[192,192]{1,0:T(8,128)} async-done(((f32[6144,192]{1,0:T(8,128)}), f32[192,192]{1,0:T(8,128)}) %reduce-scatter.8.cloned.1.call-update) | async-done | bytes 147472 | tf_op jit(solution)/shard_map/reduce_scatter | solution.py:282
  1238.8 251.5 %reduce-scatter.20.cloned.1.call-done = f32[192,992]{1,0:T(8,128)} async-done(((f32[6144,992]{1,0:T(8,128)}), f32[192,992]{1,0:T(8,128)}) %reduce-scatter.20.cloned.1.call-update) | async-done | bytes 761872 | tf_op jit(solution)/shard_map/reduce_scatter | solution.py:289
  1490.3 253.2 %reduce-scatter.18.cloned.1.call-done = f32[192,992]{1,0:T(8,128)} async-done(((f32[6144,992]{1,0:T(8,128)}), f32[192,992]{1,0:T(8,128)}) %reduce-scatter.18.cloned.1.call-update) | async-done | bytes 761872 | tf_op jit(solution)/shard_map/reduce_scatter | solution.py:288
  1743.4 251.9 %reduce-scatter.16.cloned.1.call-done = f32[192,992]{1,0:T(8,128)} async-done(((f32[6144,992]{1,0:T(8,128)}), f32[192,992]{1,0:T(8,128)}) %reduce-scatter.16.cloned.1.call-update) | async-done | bytes 761872 | tf_op jit(solution)/shard_map/reduce_scatter | solution.py:287
  (349 shorter events, 372.0 us)
Async XLA Ops:
  7.2 96.6 %copy-start = (bf16[32,12]{0,1:T(8,128)(2,1)S(1)}, bf16[32,12]{0,1:T(8,128)(2,1)}, u32[]{:S(2)}) copy-start(bf16[32,12]{0,1:T(8,128)(2,1)} %param.31) | copy-start | bytes 2308
  7.2 94.3 %copy-start.75 = (s32[2,1,384]{2,1,0:T(1,128)S(1)}, s32[2,1,384]{2,1,0:T(1,128)}, u32[]{:S(2)}) copy-start(s32[2,1,384]{2,1,0:T(1,128)} %param.19) | copy-start | bytes 9220
  7.2 94.3 %copy-start.89 = (s32[2,1,384]{2,1,0:T(1,128)S(1)}, s32[2,1,384]{2,1,0:T(1,128)}, u32[]{:S(2)}) copy-start(s32[2,1,384]{2,1,0:T(1,128)} %param.20) | copy-start | bytes 9220
  7.2 94.3 %copy-start.4 = (bf16[2,1,384,1536]{3,2,1,0:T(8,128)(2,1)S(1)}, bf16[2,1,384,1536]{3,2,1,0:T(8,128)(2,1)}, u32[]{:S(2)}) copy-start(bf16[2,1,384,1536]{3,2,1,0:T(8,128)(2,1)} %param.16) | copy-start | bytes 7077892
  7.2 101.8 %all-gather.10.cloned.1.call-start = ((), (), s32[]{:S(2)}) async-start(), calls=%async_computation.8 | async-start | bytes 3244032 | tf_op jit(solution)/shard_map/all_gather | solution.py:135
  8.0 125.6 %all-gather.12.cloned.1.call-start = ((), (), s32[]{:S(2)}) async-start(), calls=%async_computation.9 | async-start | bytes 3244032 | tf_op jit(solution)/shard_map/all_gather | solution.py:136
  8.7 185.7 %all-gather.8.cloned.1.call-start = ((), (), s32[]{:S(2)}) async-start(), calls=%async_computation.7 | async-start | bytes 3244032 | tf_op jit(solution)/shard_map/all_gather | solution.py:137
  9.4 245.6 %all-gather.14.cloned.1.call-start = ((), (), s32[]{:S(2)}) async-start(), calls=%async_computation.10 | async-start | bytes 3244032 | tf_op jit(solution)/shard_map/all_gather | solution.py:138
  10.0 342.6 %all-gather.16.cloned.1.call-start = ((), (), s32[]{:S(2)}) async-start(), calls=%async_computation.11 | async-start | bytes 12976128 | tf_op jit(solution)/shard_map/all_gather | solution.py:165
  10.6 439.1 %all-gather.18.cloned.1.call-start = ((), (), s32[]{:S(2)}) async-start(), calls=%async_computation.12 | async-start | bytes 12976128 | tf_op jit(solution)/shard_map/all_gather | solution.py:166
  11.2 535.6 %all-gather.20.cloned.1.call-start = ((), (), s32[]{:S(2)}) async-start(), calls=%async_computation.13 | async-start | bytes 12976128 | tf_op jit(solution)/shard_map/all_gather | solution.py:167
  11.9 1156.8 %reduce-scatter.14.cloned.1.call-start = ((), (), s32[]{:S(2)}) async-start(), calls=%async_computation.17 | async-start | bytes 6488064 | tf_op jit(solution)/shard_map/reduce_scatter | solution.py:285
  98.9 228.1 %copy-start.69 = (f32[1536]{0:T(1024)}, f32[1536]{0:T(1024)S(1)}, u32[]{:S(2)}) copy-start(f32[1536]{0:T(1024)S(1)} %convert_element_type.234) | copy-start | bytes 18436
  102.7 172.5 %copy-start.76 = (f32[384]{0:T(512)}, f32[384]{0:T(512)S(1)}, u32[]{:S(2)}) copy-start(f32[384]{0:T(512)S(1)} %get-tuple-element.103) | copy-start | bytes 4612
  270.0 28.6 %copy-start.34 = (bf16[384,768]{0,1:T(8,128)(2,1)}, bf16[384,768]{0,1:T(8,128)(2,1)S(1)}, u32[]{:S(2)}) copy-start(bf16[384,768]{0,1:T(8,128)(2,1)S(1)} %copy.124) | copy-start | bytes 1769476
  327.5 283.6 %copy-start.24 = (bf16[384,1536]{1,0:T(8,128)(2,1)}, bf16[384,1536]{1,0:T(8,128)(2,1)S(1)}, u32[]{:S(2)}) copy-start(bf16[384,1536]{1,0:T(8,128)(2,1)S(1)} %get-tuple-element.99) | copy-start | bytes 3538948
  327.5 292.8 %copy-start.28 = (bf16[384,1536]{1,0:T(8,128)(2,1)}, bf16[384,1536]{1,0:T(8,128)(2,1)S(1)}, u32[]{:S(2)}) copy-start(bf16[384,1536]{1,0:T(8,128)(2,1)S(1)} %get-tuple-element.98) | copy-start | bytes 3538948
  655.1 83.7 %copy-start.26 = (f32[384,1536]{1,0:T(8,128)}, f32[384,1536]{1,0:T(8,128)S(1)}, u32[]{:S(2)}) copy-start(f32[384,1536]{1,0:T(8,128)S(1)} %get-tuple-element.86) | copy-start | bytes 7077892
  655.1 83.7 %copy-start.30 = (f32[384,1536]{1,0:T(8,128)}, f32[384,1536]{1,0:T(8,128)S(1)}, u32[]{:S(2)}) copy-start(f32[384,1536]{1,0:T(8,128)S(1)} %get-tuple-element.87) | copy-start | bytes 7077892
  754.9 27.1 %copy-start.42 = (bf16[384,768]{0,1:T(8,128)(2,1)}, bf16[384,768]{0,1:T(8,128)(2,1)S(1)}, u32[]{:S(2)}) copy-start(bf16[384,768]{0,1:T(8,128)(2,1)S(1)} %copy.130) | copy-start | bytes 1769476
  764.3 404.4 %reduce-scatter.12.cloned.1.call-start = ((), (), s32[]{:S(2)}) async-start(), calls=%async_computation.16 | async-start | bytes 6488064 | tf_op jit(solution)/shard_map/reduce_scatter | solution.py:284
  822.3 346.4 %reduce-scatter.10.cloned.1.call-start = ((), (), s32[]{:S(2)}) async-start(), calls=%async_computation.15 | async-start | bytes 6488064 | tf_op jit(solution)/shard_map/reduce_scatter | solution.py:283
  829.8 409.0 %reduce-scatter.8.cloned.1.call-start = ((), (), s32[]{:S(2)}) async-start(), calls=%async_computation.14 | async-start | bytes 6488064 | tf_op jit(solution)/shard_map/reduce_scatter | solution.py:282
  837.2 653.0 %reduce-scatter.20.cloned.1.call-start = ((), (), s32[]{:S(2)}) async-start(), calls=%async_computation.20 | async-start | bytes 25952256 | tf_op jit(solution)/shard_map/reduce_scatter | solution.py:289
  926.3 817.1 %reduce-scatter.18.cloned.1.call-start = ((), (), s32[]{:S(2)}) async-start(), calls=%async_computation.19 | async-start | bytes 25952256 | tf_op jit(solution)/shard_map/reduce_scatter | solution.py:288
  1015.6 979.7 %reduce-scatter.16.cloned.1.call-start = ((), (), s32[]{:S(2)}) async-start(), calls=%async_computation.18 | async-start | bytes 25952256 | tf_op jit(solution)/shard_map/reduce_scatter | solution.py:287
  1113.3 47.1 %copy-start.88 = (f32[384]{0:T(512)S(1)}, f32[384]{0:T(512)}, u32[]{:S(2)}) copy-start(f32[384]{0:T(512)} %get-tuple-element.60) | copy-start | bytes 4612
  1113.4 47.1 %copy-start.65 = (bf16[1,384,1536]{2,1,0:T(8,128)(2,1)S(1)}, bf16[1,384,1536]{2,1,0:T(8,128)(2,1)}, u32[]{:S(2)}) copy-start(bf16[1,384,1536]{2,1,0:T(8,128)(2,1)} %get-tuple-element.92) | copy-start | bytes 3538948
  1113.4 50.2 %copy-start.18 = (f32[384,1536]{1,0:T(8,128)S(1)}, f32[384,1536]{1,0:T(8,128)}, u32[]{:S(2)}) copy-start(f32[384,1536]{1,0:T(8,128)} %copy-done.17) | copy-start | bytes 7077892
  1113.4 50.2 %copy-start.73 = (f32[1536]{0:T(1024)S(1)}, f32[1536]{0:T(1024)}, u32[]{:S(2)}) copy-start(f32[1536]{0:T(1024)} %convert_element_type.225) | copy-start | bytes 18436
  1113.4 50.2 %copy-start.81 = (f32[384]{0:T(512)S(1)}, f32[384]{0:T(512)}, u32[]{:S(2)}) copy-start(f32[384]{0:T(512)} %get-tuple-element.125) | copy-start | bytes 4612
  1167.1 828.2 %copy-start.1 = (bf16[32,12]{0,1:T(8,128)(2,1)S(1)}, bf16[32,12]{0,1:T(8,128)(2,1)}, u32[]{:S(2)}) copy-start(bf16[32,12]{0,1:T(8,128)(2,1)} %param.31) | copy-start | bytes 2308
  (85 other events, 527.8 us)
Sparse Core Ops, SparseCore 0:
  11.0 61.7 all-gather.9
  75.6 57.9 all-gather.11
  136.5 57.8 all-gather.7
  197.1 57.8 all-gather.13
  257.8 94.7 all-gather.15
  355.4 94.2 all-gather.17
  452.5 94.2 all-gather.19
  764.4 112.5 reduce-scatter.13
  884.2 113.8 reduce-scatter.11
  1004.1 113.9 reduce-scatter.9
  1125.2 113.4 reduce-scatter.7
  1245.6 244.5 reduce-scatter.19
  1498.4 244.9 reduce-scatter.17
  1750.3 244.9 reduce-scatter.15
where the time goes:
time: 2020 us; the launch traced here: 2000 us
  waiting for transfers between devices  1080 us (53%)
  local copies, waits for them, and re-layouts  382 us (19%)
  matrix products  356 us (18%)
  blocking collectives  123 us (6%)
  other arithmetic  41 us (2%)
    reduce_scatter x1, waiting for transfers between devices, body(): lax.psum_scatter(totals[7], ('fsdp', 'dp'), scatter_dimension=0, tiled=True)  253 us
    reduce_scatter x1, waiting for transfers between devices, body(): lax.psum_scatter(totals[6], ('fsdp', 'dp'), scatter_dimension=0, tiled=True)  252 us
    reduce_scatter x1, waiting for transfers between devices, body(): lax.psum_scatter(totals[8], ('fsdp', 'dp'), scatter_dimension=0, tiled=True)  251 us
    add x6, local copies, waits for them, and re-layouts, body(): jax.tree.map(jnp.add, totals, step_set)  173 us
    dot_general x14, matrix products, over_tokens(): lax.dot_general(former, latter, (((0,), (0,)), ((), ())), preferred_eleme...  122 us
    dot_general x14, matrix products, times_rows(): return jnp.dot(former, latter, preferred_element_type=jnp.float32)  104 us
    reshape x7, local copies, waits for them, and re-layouts, assemble(): jnp.transpose(shaped, (0, 2, 1, 3))  99.5 us
    dot_general x14, matrix products, times_transpose(): lax.dot_general(former, latter, (((1,), (1,)), ((), ())), preferred_eleme...  84.5 us
  transfers between devices with their start and end apart: 14, of which 10 were waited for; matrix products, arithmetic and copies ran while one was open for 27% of the time, Pallas kernels for 0%

commit v1 on v0

--- a/solution.py
+++ b/solution.py
@@ -1,6 +1,9 @@
+import functools
 import jax
 import jax.numpy as jnp
 from jax import lax
+from jax.experimental import pallas as pl
+from jax.experimental.pallas import tpu as pltpu
 from jax.sharding import PartitionSpec as P
 
 EPS = 1e-06
@@ -309,6 +312,612 @@
     )
 
 
+MESH_ID = pl.DeviceIdType.MESH
+LANES = 768
+ROWS = 192
+
+
+def place():
+    f = lax.axis_index("fsdp")
+    d = lax.axis_index("dp")
+    return f // 2, f % 2, d // 2, d % 2
+
+
+def device(z, x, y, c):
+    return (z * 2 + x, y * 2 + c)
+
+
+def start_barrier():
+    f = lax.axis_index("fsdp")
+    d = lax.axis_index("dp")
+    barrier = pltpu.get_barrier_semaphore()
+
+    def tell(step, carry):
+        other = (f * 4 + d + step) % 32
+        pl.semaphore_signal(
+            barrier, inc=1, device_id=(other // 4, other % 4), device_id_type=MESH_ID
+        )
+        return carry
+
+    lax.fori_loop(1, 32, tell, 0)
+    pl.semaphore_wait(barrier, 31)
+
+
+def exchange(tile_of, table, send, recv):
+    f = lax.axis_index("fsdp")
+    d = lax.axis_index("dp")
+    me = f * 4 + d
+
+    def one(step, carry):
+        other = (me + step) % 32
+        pltpu.make_async_remote_copy(
+            tile_of(other), table.at[me], send, recv,
+            device_id=(other // 4, other % 4), device_id_type=MESH_ID,
+        ).start()
+        return carry
+
+    lax.fori_loop(1, 32, one, 0)
+    view = table.at[pl.ds(0, 31)]
+    return pltpu.make_async_remote_copy(
+        view, view, send, recv, device_id=(f, (d + 1) % 4), device_id_type=MESH_ID
+    )
+
+
+def lanes_of(pack):
+    return pl.ds(pl.multiple_of(pack * LANES, 128), LANES)
+
+
+def rows_of(z, x, first, count):
+    return pl.ds(pl.multiple_of((z * 2 + x) * ROWS + first, 32), count)
+
+
+G_Z, G_X0, G_Y0, G_XZ, G_YZ, G_DY, G_DX = 0, 3, 4, 5, 8, 11, 15
+G_XA, G_XB, G_YA, G_YB, G_C = 19, 22, 25, 28, 31
+G_COUNT = 47
+G_ROWS = (
+    [192] * 3 + [192, 192] + [32] * 6 + [96] * 8 + [64] * 3 + [96] * 3 + [64] * 3 + [96] * 3 + [192] * 16
+)
+
+
+class Gather:
+    def __init__(self, own, whole, send, recv, packs):
+        self.own, self.whole, self.send, self.recv, self.packs = own, whole, send, recv, packs
+        self.z, self.x, self.y, self.c = place()
+
+    def put(self, pack, slot, shard, first, count, target, own=False):
+        zz, xx, yy = shard
+        there = self.whole.at[yy * 2 + self.c, rows_of(zz, xx, first, count), lanes_of(pack)]
+        here = self.own.at[pl.ds(first, count), lanes_of(pack)] if own else there
+        pltpu.make_async_remote_copy(
+            here, there, self.send.at[pack, slot], self.recv.at[pack, slot],
+            device_id=device(*target), device_id_type=MESH_ID,
+        ).start()
+
+    def some(self, pack, slot):
+        count = G_ROWS[slot]
+        view = self.whole.at[0, pl.ds(0, count), lanes_of(pack)]
+        return pltpu.make_async_remote_copy(
+            view, view, self.send.at[pack, slot], self.recv.at[pack, slot],
+            device_id=device(self.z, self.x, self.y, 1 - self.c), device_id_type=MESH_ID,
+        )
+
+    def got(self, pack, slot):
+        self.some(pack, slot).wait_recv()
+
+    def launch(self, pack):
+        z, x, y, c = self.z, self.x, self.y, self.c
+        for k in (1, 2, 3):
+            self.put(pack, G_Z + k - 1, (z, x, y), 0, 192, ((z + k) % 4, x, y, c), own=True)
+
+    def first(self, pack, k):
+        z, x, y, c = self.z, self.x, self.y, self.c
+        xn, yn, cn = (z, 1 - x, y, c), (z, x, 1 - y, c), (z, x, y, 1 - c)
+        zz = (z - k + 4) % 4
+        mine = (zz, x, y)
+        if k == 0:
+            self.put(pack, G_X0, mine, 0, 192, xn, own=True)
+            self.put(pack, G_Y0, mine, 0, 192, yn, own=True)
+            self.put(pack, G_C, mine, 0, 192, cn, own=True)
+        else:
+            self.got(pack, G_Z + k - 1)
+            self.put(pack, G_XA + k - 1, mine, 0, 64, xn)
+            self.put(pack, G_YA + k - 1, mine, 128, 64, yn)
+            self.put(pack, G_XB + k - 1, mine, 96, 96, xn)
+            self.put(pack, G_YB + k - 1, mine, 0, 96, yn)
+            self.put(pack, G_C + 4 * k, mine, 0, 192, cn)
+
+    def second(self, pack, k):
+        z, x, y, c = self.z, self.x, self.y, self.c
+        xn, yn, cn = (z, 1 - x, y, c), (z, x, 1 - y, c), (z, x, y, 1 - c)
+        zz = (z - k + 4) % 4
+        across_x, across_y = (zz, 1 - x, y), (zz, x, 1 - y)
+        if k == 0:
+            self.got(pack, G_X0)
+            for j in (1, 2, 3):
+                self.put(pack, G_XZ + j - 1, across_x, 64, 32, ((z + j) % 4, x, y, c))
+            self.put(pack, G_DY, across_x, 0, 96, yn)
+            self.put(pack, G_C + 1, across_x, 0, 192, cn)
+            self.got(pack, G_Y0)
+            for j in (1, 2, 3):
+                self.put(pack, G_YZ + j - 1, across_y, 96, 32, ((z + j) % 4, x, y, c))
+            self.put(pack, G_DX, across_y, 96, 96, xn)
+            self.put(pack, G_C + 2, across_y, 0, 192, cn)
+        else:
+            self.got(pack, G_XZ + k - 1)
+            self.got(pack, G_XA + k - 1)
+            self.put(pack, G_DY + k, across_x, 0, 96, yn)
+            self.got(pack, G_YZ + k - 1)
+            self.got(pack, G_YA + k - 1)
+            self.put(pack, G_DX + k, across_y, 96, 96, xn)
+            self.got(pack, G_XB + k - 1)
+            self.put(pack, G_C + 4 * k + 1, across_x, 0, 192, cn)
+            self.got(pack, G_YB + k - 1)
+            self.put(pack, G_C + 4 * k + 2, across_y, 0, 192, cn)
+
+    def third(self, pack, k):
+        z, x, y, c = self.z, self.x, self.y, self.c
+        zz = (z - k + 4) % 4
+        self.got(pack, G_DY + k)
+        self.got(pack, G_DX + k)
+        self.put(pack, G_C + 4 * k + 3, (zz, 1 - x, 1 - y), 0, 192, (z, x, y, 1 - c))
+
+    def step(self, pack, k):
+        self.first(pack, k)
+        if k == 3:
+            pl.when(pack + 1 < self.packs)(lambda: self.launch(pack + 1))
+        if k >= 1:
+            self.second(pack, k - 1)
+        else:
+            pl.when(pack >= 1)(lambda: self.second(pack - 1, 3))
+        if k >= 2:
+            self.third(pack, k - 2)
+        else:
+            pl.when(pack >= 1)(lambda: self.third(pack - 1, k + 2))
+
+    def drain(self):
+        last = self.packs - 1
+        self.second(last, 3)
+        self.third(last, 2)
+        self.third(last, 3)
+
+    def arrived(self, pack):
+        for slot in range(G_C, G_C + 16):
+            self.got(pack, slot)
+
+    def finish(self):
+        def one(pack, carry):
+            for slot in range(G_COUNT):
+                self.some(pack, slot).wait_send()
+            return carry
+        lax.fori_loop(0, self.packs, one, 0)
+
+
+def gather_kernel(packs, own, tile, whole, table, send, recv, local, tile_send, tile_recv, tile_local):
+    f = lax.axis_index("fsdp")
+    d = lax.axis_index("dp")
+    start_barrier()
+    tiles = exchange(lambda other: tile, table, tile_send, tile_recv)
+    tile_keep = pltpu.make_async_copy(tile, table.at[f * 4 + d], tile_local)
+    tile_keep.start()
+    g = Gather(own, whole, send, recv, packs)
+    keep = pltpu.make_async_copy(
+        own, whole.at[d, pl.ds(pl.multiple_of(f * ROWS, ROWS), ROWS)], local
+    )
+    g.launch(0)
+    keep.start()
+
+    def one(pack, carry):
+        for k in range(4):
+            g.step(pack, k)
+        return carry
+
+    lax.fori_loop(0, packs, one, 0)
+    g.drain()
+    lax.fori_loop(0, packs, lambda p, s: (g.arrived(p), s)[1], 0)
+    g.finish()
+    keep.wait()
+    tiles.wait()
+    tile_keep.wait()
+
+
+def gather(own, tile):
+    packs = own.shape[1] // LANES
+    return pl.pallas_call(
+        functools.partial(gather_kernel, packs),
+        out_shape=(
+            jax.ShapeDtypeStruct((4, 8 * ROWS, own.shape[1]), own.dtype),
+            jax.ShapeDtypeStruct((32, 8, 128), jnp.float32),
+        ),
+        in_specs=[pl.BlockSpec(memory_space=pl.ANY)] * 2,
+        out_specs=[pl.BlockSpec(memory_space=pl.ANY)] * 2,
+        scratch_shapes=[
+            pltpu.SemaphoreType.DMA((packs, G_COUNT)),
+            pltpu.SemaphoreType.DMA((packs, G_COUNT)),
+        ] + [pltpu.SemaphoreType.DMA] * 4,
+        compiler_params=pltpu.CompilerParams(collective_id=1, has_side_effects=True),
+    )(own, tile)
+
+
+R_C, R_V, R_U, R_ZC, R_Z, R_F = 0, 16, 32, 38, 44, 47
+R_COUNT = 49
+R_ROWS = [192] * 16 + [96] * 16 + [64] * 6 + [32] * 6 + [192] * 3 + [96] * 2
+ORDER = (1, 2, 3, 0)
+TILE = 32
+
+
+def add_rows(into, what, count):
+    def one(t, carry):
+        r = pl.ds(pl.multiple_of(t * TILE, TILE), TILE)
+        into[r] = (into[r].astype(jnp.float32) + what[r].astype(jnp.float32)).astype(into.dtype)
+        return carry
+    lax.fori_loop(0, count // TILE, one, 0)
+
+
+class Scatter:
+    def __init__(self, part, out, mine, buf_c, buf_v, buf_u, buf_zc, buf_z, buf_f, send, recv, load, credit, packs):
+        self.part, self.out, self.mine = part, out, mine
+        self.buf_c, self.buf_v, self.buf_u, self.buf_zc, self.buf_z, self.buf_f = buf_c, buf_v, buf_u, buf_zc, buf_z, buf_f
+        self.send, self.recv, self.load, self.credit, self.packs = send, recv, load, credit, packs
+        self.z, self.x, self.y, self.c = place()
+        z, x, y, c = place()
+        self.xn, self.yn, self.cn = (z, 1 - x, y, c), (z, x, 1 - y, c), (z, x, y, 1 - c)
+
+    def at(self, par, shard, first, count):
+        zz, xx, yy = shard
+        return self.mine.at[par, yy, rows_of(zz, xx, first, count)]
+
+    def put(self, par, slot, here, there, target):
+        pltpu.make_async_remote_copy(
+            here, there, self.send.at[par, slot], self.recv.at[par, slot],
+            device_id=device(*target), device_id_type=MESH_ID,
+        ).start()
+
+    def some(self, par, slot):
+        view = self.mine.at[par, 0, pl.ds(0, R_ROWS[slot])]
+        return pltpu.make_async_remote_copy(
+            view, view, self.send.at[par, slot], self.recv.at[par, slot],
+            device_id=device(*self.cn), device_id_type=MESH_ID,
+        )
+
+    def got(self, par, slot):
+        self.some(par, slot).wait_recv()
+
+    def shards(self, k):
+        zz = (self.z + k) % 4
+        return ((zz, 1 - self.x, 1 - self.y), (zz, self.x, 1 - self.y), (zz, 1 - self.x, self.y), (zz, self.x, self.y))
+
+    def loads(self, pack):
+        par = pack % 2
+        return [
+            pltpu.make_async_copy(
+                self.part.at[yy * 2 + self.c, :, lanes_of(pack)], self.mine.at[par, yy], self.load.at[yy]
+            )
+            for yy in range(2)
+        ]
+
+    def launch(self, pack):
+        par = pack % 2
+        pl.when(pack >= 2)(lambda: pl.semaphore_wait(self.credit.at[pack - 2], 6))
+        for r in self.loads(pack):
+            r.start()
+        for k in ORDER:
+            for i, (zz, xx, yy) in enumerate(self.shards(k)):
+                rows = rows_of(zz, xx, 0, 192)
+                self.put(
+                    par, R_C + 4 * k + i,
+                    self.part.at[yy * 2 + 1 - self.c, rows, lanes_of(pack)],
+                    self.buf_c.at[par, yy, rows], self.cn,
+                )
+
+    def core(self, pack, k):
+        par = pack % 2
+        sh = self.shards(k)
+        if k == ORDER[0]:
+            for r in self.loads(pack):
+                r.wait()
+        for i, (zz, xx, yy) in enumerate(sh):
+            self.got(par, R_C + 4 * k + i)
+            add_rows(self.at(par, sh[i], 0, 192), self.buf_c.at[par, yy, rows_of(zz, xx, 0, 192)], 192)
+        v = self.buf_v
+        self.put(par, R_V + 4 * k, self.at(par, sh[0], 0, 96), v.at[par, k, 0], self.yn)
+        self.put(par, R_V + 4 * k + 1, self.at(par, sh[0], 96, 96), v.at[par, k, 1], self.xn)
+        self.put(par, R_V + 4 * k + 2, self.at(par, sh[1], 0, 96), v.at[par, k, 2], self.yn)
+        self.put(par, R_V + 4 * k + 3, self.at(par, sh[2], 96, 96), v.at[par, k, 3], self.xn)
+
+    def vees(self, pack, k):
+        par = pack % 2
+        sh = self.shards(k)
+        zz = (self.z + k) % 4
+        peer = (zz, self.x, self.y, self.c)
+        v = self.buf_v
+        self.got(par, R_V + 4 * k)
+        add_rows(self.at(par, sh[2], 0, 96), v.at[par, k, 0], 96)
+        if k:
+            self.put(par, R_U + 2 * (k - 1), self.at(par, sh[2], 0, 64), self.buf_u.at[par, k - 1, 0], self.xn)
+            self.put(par, R_ZC + 2 * (k - 1), self.at(par, sh[2], 64, 32), self.buf_zc.at[par, k - 1, 0], peer)
+        self.got(par, R_V + 4 * k + 1)
+        add_rows(self.at(par, sh[1], 96, 96), v.at[par, k, 1], 96)
+        if k:
+            self.put(par, R_U + 2 * (k - 1) + 1, self.at(par, sh[1], 128, 64), self.buf_u.at[par, k - 1, 1], self.yn)
+            self.put(par, R_ZC + 2 * (k - 1) + 1, self.at(par, sh[1], 96, 32), self.buf_zc.at[par, k - 1, 1], peer)
+            self.got(par, R_V + 4 * k + 2)
+            add_rows(self.at(par, sh[3], 0, 96), v.at[par, k, 2], 96)
+            self.got(par, R_V + 4 * k + 3)
+            add_rows(self.at(par, sh[3], 96, 96), v.at[par, k, 3], 96)
+
+    def yous(self, pack, k):
+        par = pack % 2
+        sh = self.shards(k)
+        peer = ((self.z + k) % 4, self.x, self.y, self.c)
+        self.got(par, R_U + 2 * (k - 1))
+        add_rows(self.at(par, sh[3], 0, 64), self.buf_u.at[par, k - 1, 0], 64)
+        self.got(par, R_U + 2 * (k - 1) + 1)
+        add_rows(self.at(par, sh[3], 128, 64), self.buf_u.at[par, k - 1, 1], 64)
+        self.put(par, R_Z + k - 1, self.at(par, sh[3], 0, 192), self.buf_z.at[par, k - 1], peer)
+
+    def near(self, pack):
+        par = pack % 2
+        sh = self.shards(0)
+        for j, (shard, first, whole, nb) in enumerate(((sh[2], 64, 0, self.xn), (sh[1], 96, 96, self.yn))):
+            for k in range(3):
+                self.got(par, R_ZC + 2 * k + j)
+            into = self.at(par, shard, first, 32)
+            b = self.buf_zc
+            into[...] = (
+                into[...].astype(jnp.float32)
+                + b[par, 0, j].astype(jnp.float32)
+                + b[par, 1, j].astype(jnp.float32)
+                + b[par, 2, j].astype(jnp.float32)
+            ).astype(into.dtype)
+            self.put(par, R_F + j, self.at(par, shard, whole, 96), self.buf_f.at[par, j], nb)
+
+    def final(self, pack):
+        par = pack % 2
+        own = self.at(par, self.shards(0)[3], 0, 192)
+        self.got(par, R_V + 2)
+        self.got(par, R_V + 3)
+        for k in range(3):
+            self.got(par, R_Z + k)
+        for j in range(2):
+            self.got(par, R_F + j)
+        for j in range(2):
+            def one(t, carry, j=j):
+                r = pl.ds(pl.multiple_of(t * TILE, TILE), TILE)
+                rr = pl.ds(pl.multiple_of(j * 96 + t * TILE, TILE), TILE)
+                total = own[rr].astype(jnp.float32) + self.buf_v[par, 0, 2 + j, r].astype(jnp.float32)
+                total = total + self.buf_f[par, j, r].astype(jnp.float32)
+                for k in range(3):
+                    total = total + self.buf_z[par, k, rr].astype(jnp.float32)
+                self.out[rr, lanes_of(pack)] = total
+                return carry
+            lax.fori_loop(0, 96 // TILE, one, 0)
+        for slot in range(R_COUNT):
+            self.some(par, slot).wait_send()
+
+        @pl.when(pack + 2 < self.packs)
+        def _():
+            z, x, y, c = self.z, self.x, self.y, self.c
+            for t in (self.xn, self.yn, self.cn) + tuple(((z + k) % 4, x, y, c) for k in (1, 2, 3)):
+                pl.semaphore_signal(self.credit.at[pack], inc=1, device_id=device(*t), device_id_type=MESH_ID)
+
+    def step(self, pack, r):
+        self.core(pack, ORDER[r])
+        if r == 0:
+            @pl.when(pack >= 1)
+            def _():
+                self.vees(pack - 1, ORDER[3])
+                self.yous(pack - 1, ORDER[2])
+                self.near(pack - 1)
+        else:
+            self.vees(pack, ORDER[r - 1])
+        if r == 1:
+            pl.when(pack >= 1)(lambda: self.final(pack - 1))
+        if r == 2:
+            pl.when(pack + 1 < self.packs)(lambda: self.launch(pack + 1))
+        if r >= 2:
+            self.yous(pack, ORDER[r - 2])
+
+    def drain(self):
+        last = self.packs - 1
+        self.vees(last, ORDER[3])
+        self.yous(last, ORDER[2])
+        self.near(last)
+        self.final(last)
+
+
+def scatter_scratch(packs):
+    bf = jnp.bfloat16
+    return [
+        pltpu.VMEM((2, 2, 8 * ROWS, LANES), bf),
+        pltpu.VMEM((2, 2, 8 * ROWS, LANES), bf),
+        pltpu.VMEM((2, 4, 4, 96, LANES), bf),
+        pltpu.VMEM((2, 3, 2, 64, LANES), bf),
+        pltpu.VMEM((2, 3, 2, 32, LANES), bf),
+        pltpu.VMEM((2, 3, 192, LANES), bf),
+        pltpu.VMEM((2, 2, 96, LANES), bf),
+        pltpu.SemaphoreType.DMA((2, R_COUNT)),
+        pltpu.SemaphoreType.DMA((2, R_COUNT)),
+        pltpu.SemaphoreType.DMA((2,)),
+        pltpu.SemaphoreType.REGULAR((packs,)),
+    ]
+
+
+def scatter_kernel(packs, part, tile, out, table, tile_send, tile_recv, tile_local, *scratch):
+    start_barrier()
+    me = lax.axis_index("fsdp") * 4 + lax.axis_index("dp")
+    tiles = exchange(lambda other: tile.at[other], table, tile_send, tile_recv)
+    tile_keep = pltpu.make_async_copy(tile.at[me], table.at[me], tile_local)
+    tile_keep.start()
+    s = Scatter(part, out, *scratch, packs)
+    s.launch(0)
+
+    def one(pack, carry):
+        for r in range(4):
+            s.step(pack, r)
+        return carry
+
+    lax.fori_loop(0, packs, one, 0)
+    s.drain()
+    tiles.wait()
+    tile_keep.wait()
+
+
+def scatter(part, tile):
+    packs = part.shape[2] // LANES
+    return pl.pallas_call(
+        functools.partial(scatter_kernel, packs),
+        out_shape=(
+            jax.ShapeDtypeStruct((ROWS, part.shape[2]), jnp.float32),
+            jax.ShapeDtypeStruct((32, 8, 128), jnp.float32),
+        ),
+        in_specs=[pl.BlockSpec(memory_space=pl.ANY)] * 2,
+        out_specs=[pl.BlockSpec(memory_space=pltpu.VMEM), pl.BlockSpec(memory_space=pl.ANY)],
+        scratch_shapes=[pltpu.SemaphoreType.DMA] * 3 + scatter_scratch(packs),
+        compiler_params=pltpu.CompilerParams(
+            collective_id=2, has_side_effects=True, vmem_limit_bytes=60 * 1024 * 1024
+        ),
+    )(part, tile)
+
+
+BF = jnp.bfloat16
+F32 = jnp.float32
+
+
+def tuned_body(
+    hidden, teacher, cotangent, valid_mask, blocks, buckets, first_gain, query_weight, key_weight, value_weight,
+    output_weight, second_gain, gate_weight, up_weight, down_weight, bias_table,
+):
+    micro, _, seq, width = hidden.shape
+    tokens = micro * seq
+    cols = query_weight.shape[1]
+    part = gate_weight.shape[1]
+    wide = -(-part // 128) * 128
+    bucket_count, heads = bias_table.shape
+    scale = F32(float(tokens * 32 * width))
+
+    def pad(m):
+        return jnp.pad(m, ((0, 0), (0, wide - part)))
+
+    own = jnp.concatenate(
+        [query_weight, key_weight, value_weight, output_weight, pad(gate_weight), pad(up_weight), pad(down_weight)], axis=1
+    )
+    valid = valid_mask.reshape(tokens).astype(F32)
+    per = first_gain.shape[0]
+    tile = jnp.zeros((8, 128), F32)
+    tile = tile.at[0, :per].set(first_gain.astype(F32)).at[1, :per].set(second_gain.astype(F32))
+    tile = tile.at[2, 0].set(jnp.sum(valid))
+    packs, table = gather(own, tile)
+    gain_one = table[:, 0, :per].reshape(width)
+    gain_two = table[:, 1, :per].reshape(width)
+    valid_total = jnp.sum(table[:, 2, 0])
+    dp = packs.shape[0]
+
+    def piece(d, name):
+        first, count = {"q": (0, cols), "k": (cols, cols), "v": (2 * cols, cols), "o": (3 * cols, cols),
+                        "gate": (4 * cols, wide), "up": (4 * cols + wide, wide), "down": (4 * cols + 2 * wide, wide)}[name]
+        return lax.slice(packs, (d, 0, first), (d + 1, width, first + count))[0]
+
+    x = hidden.reshape(tokens, width).astype(F32)
+    target = teacher.reshape(tokens, width).astype(F32)
+    upstream = cotangent.reshape(tokens, width).astype(F32)
+    places = lax.broadcasted_iota(jnp.int32, (1, 1, bucket_count), 2)
+    onehot = (buckets[:, :, None] == places).astype(F32)
+    position_bias = jnp.einsum("qkb,bh->hqk", onehot, bias_table.astype(F32), precision=HIGH)
+    onehot_low = onehot.astype(BF)
+    diagonal = lax.broadcasted_iota(jnp.int32, (seq, seq), 0) == lax.broadcasted_iota(jnp.int32, (seq, seq), 1)
+    block_ids = blocks.reshape(micro, seq)
+    allowed = (block_ids[:, None, :] <= block_ids[:, :, None]) & (valid_mask.reshape(micro, seq)[:, None, :] == 1) | diagonal
+    normed_full, scale_one = norm_forward(x, gain_one)
+    normed_one = normed_full.astype(BF)
+    per_dp = heads // dp
+    head = cols // per_dp
+
+    def heads_of(name):
+        return jnp.stack([times_rows(normed_one, piece(d, name)).astype(BF) for d in range(dp)], axis=1).reshape(micro, seq, heads, head)
+
+    queries, key_heads, value_heads = heads_of("q"), heads_of("k"), heads_of("v")
+
+    def masked(queries, key_heads):
+        products = jnp.einsum("mqhd,mkhd->mhqk", queries, key_heads, preferred_element_type=F32)
+        return jnp.where(allowed[:, None], products + position_bias[None], NEG)
+
+    scores = masked(queries, key_heads)
+    row_max = jnp.max(scores, axis=-1, keepdims=True)
+    exponent = jnp.exp(scores - row_max)
+    row_total = jnp.sum(exponent, axis=-1, keepdims=True)
+    probs = exponent / row_total
+    softmax_low = probs.astype(BF)
+    attended = jnp.einsum("mhqk,mkhd->mqhd", softmax_low, value_heads, preferred_element_type=F32).astype(BF)
+    attended = attended.reshape(tokens, dp, cols)
+    middle = x
+    for d in range(dp):
+        middle = middle + times_transpose(attended[:, d], piece(d, "o"))
+    normed_mid, scale_two = norm_forward(middle, gain_two)
+    normed_two = normed_mid.astype(BF)
+    gate_pre = [times_rows(normed_two, piece(d, "gate")) for d in range(dp)]
+    up_pre = [times_rows(normed_two, piece(d, "up")) for d in range(dp)]
+    acts = [jax.vjp(gelu_tanh, g) for g in gate_pre]
+    hidden_act = [(a[0] * u).astype(BF) for a, u in zip(acts, up_pre)]
+    layer_full = middle
+    for d in range(dp):
+        layer_full = layer_full + times_transpose(hidden_act[d], piece(d, "down"))
+    gap = layer_full - target
+    weighted = valid[:, None] * gap
+    squares = jnp.sum(weighted * gap)
+    grad_out = scale * upstream + scale * (2.0 * weighted / (valid_total * width))
+    grad_ffn = grad_out.astype(BF)
+    pieces = [[None] * 7 for _ in range(dp)]
+    grad_normed_two = jnp.zeros((tokens, width), F32)
+    for d in range(dp):
+        pieces[d][6] = over_tokens(grad_ffn, hidden_act[d]).astype(BF)
+        grad_hidden = times_rows(grad_ffn, piece(d, "down"))
+        grad_gate = acts[d][1](grad_hidden * up_pre[d])[0].astype(BF)
+        grad_up = (grad_hidden * acts[d][0]).astype(BF)
+        pieces[d][4] = over_tokens(normed_two, grad_gate).astype(BF)
+        pieces[d][5] = over_tokens(normed_two, grad_up).astype(BF)
+        grad_normed_two = grad_normed_two + times_transpose(grad_gate, piece(d, "gate")) + times_transpose(grad_up, piece(d, "up"))
+    middle_term, gain_two_part = norm_backward(middle, scale_two, gain_two, grad_normed_two)
+    grad_middle = grad_out + middle_term
+    grad_attn = grad_middle.astype(BF)
+    grad_attended = []
+    for d in range(dp):
+        pieces[d][3] = over_tokens(grad_attn, attended[:, d]).astype(BF)
+        grad_attended.append(times_rows(grad_attn, piece(d, "o")).astype(BF))
+    grad_attended = jnp.stack(grad_attended, axis=1).reshape(micro, seq, heads, head)
+    grad_probs = jnp.einsum("mqhd,mkhd->mhqk", grad_attended, value_heads, preferred_element_type=F32)
+    grad_scores = (probs * (grad_probs - jnp.sum(probs * grad_probs, axis=-1, keepdims=True))).astype(BF)
+    table_part = jnp.einsum("mhqk,qkb->bh", grad_scores, onehot_low, preferred_element_type=F32)
+    grads = (
+        jnp.einsum("mhqk,mkhd->mqhd", grad_scores, key_heads, preferred_element_type=F32),
+        jnp.einsum("mhqk,mqhd->mkhd", grad_scores, queries, preferred_element_type=F32),
+        jnp.einsum("mhqk,mqhd->mkhd", softmax_low, grad_attended, preferred_element_type=F32),
+    )
+    grad_normed_one = jnp.zeros((tokens, width), F32)
+    for i, (name, g) in enumerate(zip("qkv", grads)):
+        g = g.astype(BF).reshape(tokens, dp, cols)
+        for d in range(dp):
+            pieces[d][i] = over_tokens(normed_one, g[:, d]).astype(BF)
+            grad_normed_one = grad_normed_one + times_transpose(g[:, d], piece(d, name))
+    input_term, gain_one_part = norm_backward(x, scale_one, gain_one, grad_normed_one)
+    hidden_grad = (grad_middle + input_term).astype(BF)
+    partial = jnp.stack([jnp.concatenate(pieces[d], axis=1) for d in range(dp)])
+    tiles = jnp.zeros((32, 8, 128), F32)
+    tiles = tiles.at[:, 0, :per].set(gain_one_part.reshape(32, per)).at[:, 1, :per].set(gain_two_part.reshape(32, per))
+    lines = bucket_count * heads // 128
+    tiles = tiles.at[:, 3:3 + lines].set(table_part.reshape(1, lines, 128)).at[:, 2, 0].set(squares)
+    shard, sums = scatter(partial, tiles)
+    sums = jnp.sum(sums, axis=0)
+    cuts = (0, cols, 2 * cols, 3 * cols, 4 * cols, 4 * cols + wide, 4 * cols + 2 * wide)
+    sizes = (cols,) * 4 + (part,) * 3
+    grad = [shard[:, a:a + s] for a, s in zip(cuts, sizes)]
+    return (
+        layer_full.astype(BF).reshape(hidden.shape),
+        sums[2, 0] / (valid_total * width),
+        hidden_grad.reshape(hidden.shape),
+        sums[0, :per], grad[0], grad[1], grad[2], grad[3], sums[1, :per], grad[4], grad[5], grad[6],
+        sums[3:3 + lines].reshape(bucket_count, heads),
+    )
+
 def solution(mesh):
     in_specs = (
         P(None, ("fsdp", "dp"), None, None),
@@ -343,4 +952,5 @@
         P("fsdp", "dp"),
         P(),
     )
-    return jax.shard_map(body, mesh=mesh, in_specs=in_specs, out_specs=out_specs, check_vma=False)
+    chosen = tuned_body if dict(mesh.shape) == {"fsdp": 8, "dp": 4} else body
+    return jax.shard_map(chosen, mesh=mesh, in_specs=in_specs, out_specs=out_specs, check_vma=False)

time: 2020 us -> 1130 us (0.56)
  waiting for transfers between devices: 1080 us -> 0 us
  Pallas kernels: 0 us -> 415 us
  local copies, waits for them, and re-layouts: 382 us -> 185 us
  blocking collectives: 123 us -> 0 us
  matrix products: 356 us -> 440 us
  other arithmetic: 41 us -> 74.1 us
    reduce_scatter x7 -> x0, waiting for transfers between devices: 827 us -> none  [the longest x1 253 us: body(): lax.psum_scatter(totals[7], ('fsdp', 'dp'), scatter_dimension=0, tiled=True)]
    pallas_call x0 -> x2, Pallas kernels: none -> 415 us  [the longest x1 209 us: gather(): pl.pallas_call(functools.partial(gather_kernel, packs), out_shape=(jax.Sh...]
    all_gather x7 -> x0, waiting for transfers between devices: 249 us -> none  [the longest x1 56.5 us: body(): lax.all_gather(up_weight, ('fsdp', 'dp'), axis=0, tiled=True)]
    add x6 -> x0, local copies, waits for them, and re-layouts: 173 us -> none  [body(): jax.tree.map(jnp.add, totals, step_set)]
    reshape x14 -> x9, local copies, waits for them, and re-layouts: 168 us -> 11.2 us  [the longest x3 7.09 us: heads_of(): jnp.stack([times_rows(normed_one, piece(d, name)).astype(BF) for d in ran...]
    dot_general x14 -> x28, matrix products: 84.5 us -> 183 us  [times_transpose(): lax.dot_general(former, latter, (((1,), (1,)), ((), ())), preferred_eleme...]
    psum x2 -> x0, blocking collectives: 82.1 us -> none  [the longest x1 42.2 us: body(): valid_total = lax.psum(jnp.sum(valid_float), ('fsdp', 'dp'))]
    concatenate x0 -> x5, local copies, waits for them, and re-layouts: none -> 74.4 us  [the longest x4 71.7 us: tuned_body(): partial = jnp.stack([jnp.concatenate(pieces[d], axis=1) for d in range(dp)])]
  transfers between devices with their start and end apart: 14 -> 0, of which waited for: 10 -> 0; matrix products, arithmetic and copies ran while one was open for 27% -> 0% of each run, Pallas kernels for 0% -> 0%
where the time goes in v1:
time: 1130 us; the launch traced here: 1120 us
  matrix products  440 us (39%)
  Pallas kernels  415 us (37%)
  local copies, waits for them, and re-layouts  185 us (16%)
  other arithmetic  74.1 us (7%)
    pallas_call x1, Pallas kernels, gather(): pl.pallas_call(functools.partial(gather_kernel, packs), out_shape=(jax.Sh...  209 us
    pallas_call x1, Pallas kernels, scatter(): pl.pallas_call(functools.partial(scatter_kernel, packs), out_shape=(jax.S...  205 us
    dot_general x28, matrix products, times_transpose(): lax.dot_general(former, latter, (((1,), (1,)), ((), ())), preferred_eleme...  183 us
    dot_general x28, matrix products, times_rows(): return jnp.dot(former, latter, preferred_element_type=jnp.float32)  116 us
    dot_general x28, matrix products, over_tokens(): lax.dot_general(former, latter, (((0,), (0,)), ((), ())), preferred_eleme...  93.5 us
    concatenate x4, local copies, waits for them, and re-layouts, tuned_body(): partial = jnp.stack([jnp.concatenate(pieces[d], axis=1) for d in range(dp)])  71.7 us
    another operation x1, other arithmetic, tuned_body(): partial = jnp.stack([jnp.concatenate(pieces[d], axis=1) for d in range(dp)])  31.6 us
    eq x1, local copies, waits for them, and re-layouts, tuned_body(): onehot = (buckets[:, :, None] == places).astype(F32)  27.6 us

profile of v1, /device:TPU:0, one launch (start us, length us, event | category | flops | bytes accessed | tf_op | source)
XLA Modules:
  0.0 1119.0 jit_solution(17527890299054422885)
XLA Ops:
  10.1 209.4 %shard_map.255 = (bf16[4,1536,3840]{2,1,0:T(8,128)(2,1)}, f32[32,8,128]{2,1,0:T(8,128)}) custom-call(bf16[192,3840]{1,0:T(8,128)(2,1)} %concatenate.31.own, f32[8,128]{1,0:T(8,128)} %copy-done.42), custom_call_target="tpu_custom_call" | custom-call | tf_op jit(solution)/shard_map/pallas_call | solution.py:525
  259.6 27.6 %copy.180 = pred[384,384,32]{1,2,0:T(32,128)(4,1)} copy(pred[384,384,32]{0,2,1:T(32,128)(4,1)} %iota_compare_fusion) | data formatting | bytes 9437184 | tf_op jit(solution)/shard_map/eq | solution.py:824
  287.2 8.4 convolution_bitcast_fusion
  295.6 9.1 copy.181
  305.9 11.0 fusion.264
  357.9 7.9 multiply_convert_fusion.9
  365.8 6.8 fusion.92
  377.2 7.8 multiply_convert_fusion.8
  385.0 6.7 fusion.80
  396.2 7.8 multiply_convert_fusion.7
  404.0 6.9 fusion.68
  415.4 7.6 multiply_convert_fusion.6
  427.0 12.6 %fusion.260 = (bf16[768,1536]{1,0:T(8,128)(2,1)S(1)}, f32[768,1536]{1,0:T(8,128)}, f32[]{:T(128)}, bf16[768,1536]{1,0:T(8,128)(2,1)}) fusion(f32[]{:T(128)S(6)} %mul.475, bf16[2,1,384,1536]{3,2,1,0:T(8,128)(2,1)S(1)} %copy-done.45, f32[768]{0:T(1024)S(1)} %convert_element_type.340, f32[2,1,384,1536]{3,2,1,0:T(8,128)S(1)} %convert_multiply_fusion.2, ...), kind=kOutput, calls=%fused_computation.377 | convolution fusion | flops 2433613824 | bytes 40111112 | tf_op jit(solution)/shard_map/dot_general | solution.py:19
  439.6 8.5 multiply_convert_fusion.5
  448.1 7.3 fusion.94
  455.3 6.7 fusion.98
  468.6 7.3 fusion.86
  482.2 6.6 fusion.48
  488.8 7.3 fusion.74
  509.1 7.3 fusion.62
  516.4 17.2 %multiply_reduce_fusion.1 = (f32[1536]{0:T(1024)}, f32[768]{0:T(1024)S(1)}, f32[768,1536]{1,0:T(8,128)}) fusion(f32[768,1536]{1,0:T(8,128)} %get-tuple-element.195, f32[768]{0:T(1024)S(1)} %get-tuple-element.191, f32[1536]{0:T(1024)S(1)} %mul.446, bf16[768,1024]{1,0:T(8,128)(2,1)S(1)} %get-tuple-element.172, bf16[4,1536,3840]{2,1,0:T(8,128)(2,1)} %get-tuple-element.102, ...), kind=kOutput, calls=%fused_computation.42 | convolution fusion | flops 2431252224 | bytes 47204352 | tf_op jit(solution)/shard_map/dot_general | solution.py:19
  533.6 8.3 fusion.259
  554.0 7.7 fusion.134
  583.4 9.9 convert_reduce_fusion
  637.4 21.2 %fusion.23 = (f32[768]{0:T(1024)S(1)}, f32[1536]{0:T(1024)}, f32[768,1536]{1,0:T(8,128)}) fusion(bf16[2,1,384,1536]{3,2,1,0:T(8,128)(2,1)S(1)} %copy-done.13, f32[1536]{0:T(1024)S(1)} %copy-done.36, f32[768]{0:T(1024)S(1)} %rsqrt.28, bf16[4,1536,3840]{2,1,0:T(8,128)(2,1)} %get-tuple-element.102, bf16[768,4,192]{0,2,1:T(8,128)(2,1)} %copy-done.14, ...), kind=kOutput, calls=%fused_computation.41 | convolution fusion | flops 474216192 | bytes 60082176 | tf_op jit(solution)/shard_map/dot_general | solution.py:19
  704.6 17.9 %concatenate.32 = bf16[1536,3840]{1,0:T(8,128)(2,1)} concatenate(bf16[1536,192]{1,0:T(8,128)(2,1)} %copy.199, bf16[1536,192]{1,0:T(8,128)(2,1)} %copy.200, bf16[1536,192]{1,0:T(8,128)(2,1)} %copy.201, bf16[1536,192]{1,0:T(8,128)(2,1)} %copy.202, bf16[1536,1024]{1,0:T(8,128)(2,1)} %convolution_convert_fusion.11, bf16[1536,1024]{1,0:T(8,128)(2,1)} %convolution_convert_fusion.10, ...), dimensions={1} | concatenate | bytes 23592960 | tf_op jit(solution)/shard_map/concatenate | solution.py:903
  722.6 6.6 convolution_convert_fusion.6
  755.3 17.9 %concatenate.33 = bf16[1536,3840]{1,0:T(8,128)(2,1)} concatenate(bf16[1536,192]{1,0:T(8,128)(2,1)} %copy.206, bf16[1536,192]{1,0:T(8,128)(2,1)} %copy.207, bf16[1536,192]{1,0:T(8,128)(2,1)} %copy.208, bf16[1536,192]{1,0:T(8,128)(2,1)} %copy.209, bf16[1536,1024]{1,0:T(8,128)(2,1)} %convolution_convert_fusion.8, bf16[1536,1024]{1,0:T(8,128)(2,1)} %convolution_convert_fusion.7, ...), dimensions={1} | concatenate | bytes 23592960 | tf_op jit(solution)/shard_map/concatenate | solution.py:903
  805.5 18.1 %concatenate.34 = bf16[1536,3840]{1,0:T(8,128)(2,1)} concatenate(bf16[1536,192]{1,0:T(8,128)(2,1)} %copy.213, bf16[1536,192]{1,0:T(8,128)(2,1)} %copy.214, bf16[1536,192]{1,0:T(8,128)(2,1)} %copy.215, bf16[1536,192]{1,0:T(8,128)(2,1)} %copy.216, bf16[1536,1024]{1,0:T(8,128)(2,1)} %convolution_convert_fusion.5, bf16[1536,1024]{1,0:T(8,128)(2,1)} %convolution_convert_fusion.4, ...), dimensions={1} | concatenate | bytes 23592960 | tf_op jit(solution)/shard_map/concatenate | solution.py:903
  854.9 17.7 %concatenate.35 = bf16[1536,3840]{1,0:T(8,128)(2,1)} concatenate(bf16[1536,192]{1,0:T(8,128)(2,1)S(1)} %copy.220, bf16[1536,192]{1,0:T(8,128)(2,1)} %copy.221, bf16[1536,192]{1,0:T(8,128)(2,1)} %copy.222, bf16[1536,192]{1,0:T(8,128)(2,1)} %copy.223, bf16[1536,1024]{1,0:T(8,128)(2,1)} %convolution_convert_fusion.2, bf16[1536,1024]{1,0:T(8,128)(2,1)} %convolution_convert_fusion.1, ...), dimensions={1} | concatenate | bytes 23592960 | tf_op jit(solution)/shard_map/concatenate | solution.py:903
  872.7 31.6 %pad_maximum_fusion.part = bf16[4,1536,3840]{2,1,0:T(8,128)(2,1)} fusion(bf16[1,1536,3840]{2,1,0:T(8,128)(2,1)} %bitcast.469, bf16[1,1536,3840]{2,1,0:T(8,128)(2,1)} %bitcast.468, bf16[1,1536,3840]{2,1,0:T(8,128)(2,1)} %bitcast.467, bf16[1,1536,3840]{2,1,0:T(8,128)(2,1)} %bitcast.466), kind=kLoop, calls=%fused_computation.1 | loop fusion | flops 70778880 | bytes 94371840 | tf_op jit(solution)/shard_map/stack | solution.py:903
  904.3 205.4 %shard_map.256 = (f32[192,3840]{1,0:T(8,128)}, f32[32,8,128]{2,1,0:T(8,128)}) custom-call(bf16[4,1536,3840]{2,1,0:T(8,128)(2,1)} %pad_maximum_fusion.part, f32[32,8,128]{2,1,0:T(8,128)} %copy-done.32), custom_call_target="tpu_custom_call" | custom-call | tf_op jit(solution)/shard_map/pallas_call | solution.py:767
  (315 shorter events, 354.4 us)
Async XLA Ops:
  0.6 286.5 %copy-start = (bf16[32,12]{0,1:T(8,128)(2,1)S(1)}, bf16[32,12]{0,1:T(8,128)(2,1)}, u32[]{:S(2)}) copy-start(bf16[32,12]{0,1:T(8,128)(2,1)} %param.45) | copy-start | bytes 2308
  5.1 216.1 %copy-start.10 = (bf16[2,1,384,1536]{3,2,1,0:T(8,128)(2,1)S(1)}, bf16[2,1,384,1536]{3,2,1,0:T(8,128)(2,1)}, u32[]{:S(2)}) copy-start(bf16[2,1,384,1536]{3,2,1,0:T(8,128)(2,1)} %param.30) | copy-start | bytes 7077892
  223.5 99.6 %copy-start.2 = (bf16[2,1,384,1536]{3,2,1,0:T(8,128)(2,1)}, bf16[2,1,384,1536]{3,2,1,0:T(8,128)(2,1)S(1)}, u32[]{:S(2)}) copy-start(bf16[2,1,384,1536]{3,2,1,0:T(8,128)(2,1)S(1)} %fusion.13) | copy-start | bytes 7077892
  236.4 69.5 %copy-start.15 = (bf16[2,384,12,64]{1,0,3,2:T(2,128)(2,1)}, bf16[2,384,12,64]{1,0,3,2:T(2,128)(2,1)S(1)}, u32[]{:S(2)}) copy-start(bf16[2,384,12,64]{1,0,3,2:T(2,128)(2,1)S(1)} %reshape.677) | copy-start | bytes 3538948
  295.6 9.2 copy-start.43
  295.6 9.2 copy-start.44
  335.5 7.9 copy-start.19
  352.5 62.9 %copy-start.21 = (bf16[768,1536]{1,0:T(8,128)(2,1)}, bf16[768,1536]{1,0:T(8,128)(2,1)S(1)}, u32[]{:S(2)}) copy-start(bf16[768,1536]{1,0:T(8,128)(2,1)S(1)} %multiply_convert_fusion.1) | copy-start | bytes 7077892
  357.9 8.0 copy-start.56
  377.2 7.8 copy-start.53
  396.2 7.8 copy-start.50
  415.4 7.7 copy-start.47
  415.4 9.9 copy-start.20
  439.6 63.0 %copy-start.46 = (bf16[768,1536]{1,0:T(8,128)(2,1)}, bf16[768,1536]{1,0:T(8,128)(2,1)S(1)}, u32[]{:S(2)}) copy-start(bf16[768,1536]{1,0:T(8,128)(2,1)S(1)} %get-tuple-element.169) | copy-start | bytes 7077892
  448.0 7.3 copy-start.73
  468.6 7.3 copy-start.67
  468.6 7.3 copy-start.69
  488.8 7.3 copy-start.63
  488.8 7.3 copy-start.65
  509.1 7.3 copy-start.59
  509.1 7.3 copy-start.26
  516.4 17.2 %copy-start.41 = (f32[768]{0:T(1024)S(1)}, f32[768]{0:T(1024)}, u32[]{:S(2)}) copy-start(f32[768]{0:T(1024)} %get-tuple-element.190) | copy-start | bytes 9220
  541.9 8.1 copy-start.4
  563.7 9.1 copy-start.14
  563.7 13.4 %slice-start.2 = ((s8[14155776]{0:T(1024)(128)(4,1)}), s8[4194304]{0:T(1024)(128)(4,1)S(1)}, s32[]{:S(2)}) async-start(s8[14155776]{0:T(1024)(128)(4,1)} %bitcast.464), calls=%async_computation.2 | async-start | bytes 8388608
  563.7 13.3 %slice-start.3 = ((s8[14155776]{0:T(1024)(128)(4,1)}), s8[4194304]{0:T(1024)(128)(4,1)S(1)}, s32[]{:S(2)}) async-start(s8[14155776]{0:T(1024)(128)(4,1)} %bitcast.464), calls=%async_computation.3 | async-start | bytes 8388608
  568.5 8.5 slice-start.4
  583.4 9.9 copy-start.16
  598.1 14.5 %copy-start.18 = (bf16[768,4,192]{0,2,1:T(8,128)(2,1)}, bf16[768,4,192]{0,2,1:T(8,128)(2,1)S(1)}, u32[]{:S(2)}) copy-start(bf16[768,4,192]{0,2,1:T(8,128)(2,1)S(1)} %reshape.683) | copy-start | bytes 3538948
  603.1 14.1 %slice-start = ((s8[7077888]{0:T(1024)(128)(4,1)}), s8[4194304]{0:T(1024)(128)(4,1)S(1)}, s32[]{:S(2)}) async-start(s8[7077888]{0:T(1024)(128)(4,1)} %bitcast.462), calls=%async_computation | async-start | bytes 8388608
  607.9 9.4 slice-start.1
  1109.8 7.9 copy-start.1
  (49 other events, 236.1 us)

commit v2 on v0

--- a/solution.py
+++ b/solution.py
@@ -1,6 +1,9 @@
+import functools
 import jax
 import jax.numpy as jnp
 from jax import lax
+from jax.experimental import pallas as pl
+from jax.experimental.pallas import tpu as pltpu
 from jax.sharding import PartitionSpec as P
 
 EPS = 1e-06
@@ -309,6 +312,1034 @@
     )
 
 
+MESH_ID = pl.DeviceIdType.MESH
+LANES = 768
+ROWS = 192
+
+
+def place():
+    f = lax.axis_index("fsdp")
+    d = lax.axis_index("dp")
+    return f // 2, f % 2, d // 2, d % 2
+
+
+def device(z, x, y, c):
+    return (z * 2 + x, y * 2 + c)
+
+
+def start_barrier():
+    f = lax.axis_index("fsdp")
+    d = lax.axis_index("dp")
+    barrier = pltpu.get_barrier_semaphore()
+
+    def tell(step, carry):
+        other = (f * 4 + d + step) % 32
+        pl.semaphore_signal(
+            barrier, inc=1, device_id=(other // 4, other % 4), device_id_type=MESH_ID
+        )
+        return carry
+
+    lax.fori_loop(1, 32, tell, 0)
+    pl.semaphore_wait(barrier, 31)
+
+
+def exchange(tile_of, table, send, recv):
+    f = lax.axis_index("fsdp")
+    d = lax.axis_index("dp")
+    me = f * 4 + d
+
+    def one(step, carry):
+        other = (me + step) % 32
+        pltpu.make_async_remote_copy(
+            tile_of(other), table.at[me], send, recv,
+            device_id=(other // 4, other % 4), device_id_type=MESH_ID,
+        ).start()
+        return carry
+
+    lax.fori_loop(1, 32, one, 0)
+    view = table.at[pl.ds(0, 31)]
+    return pltpu.make_async_remote_copy(
+        view, view, send, recv, device_id=(f, (d + 1) % 4), device_id_type=MESH_ID
+    )
+
+
+def lanes_of(pack):
+    return pl.ds(pl.multiple_of(pack * LANES, 128), LANES)
+
+
+def rows_of(z, x, first, count):
+    return pl.ds(pl.multiple_of((z * 2 + x) * ROWS + first, 32), count)
+
+
+G_Z, G_X0, G_Y0, G_XZ, G_YZ, G_DY, G_DX = 0, 3, 4, 5, 8, 11, 15
+G_XA, G_XB, G_YA, G_YB, G_C = 19, 22, 25, 28, 31
+G_COUNT = 47
+G_ROWS = (
+    [192] * 3 + [192, 192] + [32] * 6 + [96] * 8 + [64] * 3 + [96] * 3 + [64] * 3 + [96] * 3 + [192] * 16
+)
+
+
+class Gather:
+    def __init__(self, own, whole, send, recv, packs):
+        self.own, self.whole, self.send, self.recv, self.packs = own, whole, send, recv, packs
+        self.z, self.x, self.y, self.c = place()
+
+    def put(self, pack, slot, shard, first, count, target, own=False):
+        zz, xx, yy = shard
+        there = self.whole.at[yy * 2 + self.c, rows_of(zz, xx, first, count), lanes_of(pack)]
+        here = self.own.at[pl.ds(first, count), lanes_of(pack)] if own else there
+        pltpu.make_async_remote_copy(
+            here, there, self.send.at[pack, slot], self.recv.at[pack, slot],
+            device_id=device(*target), device_id_type=MESH_ID,
+        ).start()
+
+    def some(self, pack, slot, count):
+        view = self.whole.at[0, pl.ds(0, count), lanes_of(pack)]
+        return pltpu.make_async_remote_copy(
+            view, view, self.send.at[pack, slot], self.recv.at[pack, slot],
+            device_id=device(self.z, self.x, self.y, 1 - self.c), device_id_type=MESH_ID,
+        )
+
+    def got(self, pack, slot, count):
+        self.some(pack, slot, count).wait_recv()
+
+    def launch(self, pack):
+        z, x, y, c = self.z, self.x, self.y, self.c
+        for k in (1, 2, 3):
+            self.put(pack, G_Z + k - 1, (z, x, y), 0, 192, ((z + k) % 4, x, y, c), own=True)
+
+    def first(self, pack, k):
+        z, x, y, c = self.z, self.x, self.y, self.c
+        xn, yn, cn = (z, 1 - x, y, c), (z, x, 1 - y, c), (z, x, y, 1 - c)
+        mine = ((z - k + 4) % 4, x, y)
+
+        @pl.when(k == 0)
+        def _():
+            self.put(pack, G_X0, (z, x, y), 0, 192, xn, own=True)
+            self.put(pack, G_Y0, (z, x, y), 0, 192, yn, own=True)
+            self.put(pack, G_C, (z, x, y), 0, 192, cn, own=True)
+
+        @pl.when(k > 0)
+        def _():
+            self.got(pack, G_Z + k - 1, 192)
+            self.put(pack, G_XA + k - 1, mine, 0, 64, xn)
+            self.put(pack, G_YA + k - 1, mine, 128, 64, yn)
+            self.put(pack, G_XB + k - 1, mine, 96, 96, xn)
+            self.put(pack, G_YB + k - 1, mine, 0, 96, yn)
+            self.put(pack, G_C + 4 * k, mine, 0, 192, cn)
+
+    def second(self, pack, k):
+        z, x, y, c = self.z, self.x, self.y, self.c
+        xn, yn, cn = (z, 1 - x, y, c), (z, x, 1 - y, c), (z, x, y, 1 - c)
+        zz = (z - k + 4) % 4
+        across_x, across_y = (zz, 1 - x, y), (zz, x, 1 - y)
+
+        @pl.when(k == 0)
+        def _():
+            self.got(pack, G_X0, 192)
+            for j in (1, 2, 3):
+                self.put(pack, G_XZ + j - 1, (z, 1 - x, y), 64, 32, ((z + j) % 4, x, y, c))
+            self.put(pack, G_DY, (z, 1 - x, y), 0, 96, yn)
+            self.put(pack, G_C + 1, (z, 1 - x, y), 0, 192, cn)
+            self.got(pack, G_Y0, 192)
+            for j in (1, 2, 3):
+                self.put(pack, G_YZ + j - 1, (z, x, 1 - y), 96, 32, ((z + j) % 4, x, y, c))
+            self.put(pack, G_DX, (z, x, 1 - y), 96, 96, xn)
+            self.put(pack, G_C + 2, (z, x, 1 - y), 0, 192, cn)
+
+        @pl.when(k > 0)
+        def _():
+            self.got(pack, G_XZ + k - 1, 32)
+            self.got(pack, G_XA + k - 1, 64)
+            self.put(pack, G_DY + k, across_x, 0, 96, yn)
+            self.got(pack, G_YZ + k - 1, 32)
+            self.got(pack, G_YA + k - 1, 64)
+            self.put(pack, G_DX + k, across_y, 96, 96, xn)
+            self.got(pack, G_XB + k - 1, 96)
+            self.put(pack, G_C + 4 * k + 1, across_x, 0, 192, cn)
+            self.got(pack, G_YB + k - 1, 96)
+            self.put(pack, G_C + 4 * k + 2, across_y, 0, 192, cn)
+
+    def third(self, pack, k):
+        z, x, y, c = self.z, self.x, self.y, self.c
+        zz = (z - k + 4) % 4
+        self.got(pack, G_DY + k, 96)
+        self.got(pack, G_DX + k, 96)
+        self.put(pack, G_C + 4 * k + 3, (zz, 1 - x, 1 - y), 0, 192, (z, x, y, 1 - c))
+
+    def step(self, s):
+        total = 4 * self.packs
+
+        @pl.when(s < total)
+        def _():
+            self.first(s // 4, s % 4)
+            pl.when((s % 4 == 3) & (s + 1 < total))(lambda: self.launch(s // 4 + 1))
+
+        pl.when((s >= 1) & (s <= total))(lambda: self.second((s + 3) // 4 - 1, (s + 3) % 4))
+        pl.when((s >= 2) & (s <= total + 1))(lambda: self.third((s + 2) // 4 - 1, (s + 2) % 4))
+
+    def arrived(self, pack):
+        for slot in range(G_C, G_C + 16):
+            self.got(pack, slot, 192)
+
+    def finish(self):
+        def one(pack, carry):
+            for slot in range(G_COUNT):
+                self.some(pack, slot, G_ROWS[slot]).wait_send()
+            return carry
+        lax.fori_loop(0, self.packs, one, 0)
+
+
+R_C, R_V, R_U, R_ZC, R_Z, R_F = 0, 16, 32, 38, 44, 47
+R_COUNT = 49
+R_ROWS = [192] * 16 + [96] * 16 + [64] * 6 + [32] * 6 + [192] * 3 + [96] * 2
+ORDER = (1, 2, 3, 0)
+TILE = 32
+
+
+def add_rows(into, what, count):
+    def one(t, carry):
+        r = pl.ds(pl.multiple_of(t * TILE, TILE), TILE)
+        into[r] = (into[r].astype(jnp.float32) + what[r].astype(jnp.float32)).astype(into.dtype)
+        return carry
+    lax.fori_loop(0, count // TILE, one, 0)
+
+
+class Scatter:
+    def __init__(self, part, out, mine, buf_c, buf_v, buf_u, buf_zc, buf_z, buf_f, send, recv, load, credit, stage, out_sem, packs):
+        self.stage, self.out_sem = stage, out_sem
+        self.part, self.out, self.mine = part, out, mine
+        self.buf_c, self.buf_v, self.buf_u, self.buf_zc, self.buf_z, self.buf_f = buf_c, buf_v, buf_u, buf_zc, buf_z, buf_f
+        self.send, self.recv, self.load, self.credit, self.packs = send, recv, load, credit, packs
+        self.z, self.x, self.y, self.c = place()
+        z, x, y, c = place()
+        self.xn, self.yn, self.cn = (z, 1 - x, y, c), (z, x, 1 - y, c), (z, x, y, 1 - c)
+
+    def at(self, par, shard, first, count):
+        zz, xx, yy = shard
+        return self.mine.at[par, yy, rows_of(zz, xx, first, count)]
+
+    def put(self, par, slot, here, there, target):
+        pltpu.make_async_remote_copy(
+            here, there, self.send.at[par, slot], self.recv.at[par, slot],
+            device_id=device(*target), device_id_type=MESH_ID,
+        ).start()
+
+    def some(self, par, slot, count):
+        view = self.mine.at[par, 0, pl.ds(0, count)]
+        return pltpu.make_async_remote_copy(
+            view, view, self.send.at[par, slot], self.recv.at[par, slot],
+            device_id=device(*self.cn), device_id_type=MESH_ID,
+        )
+
+    def got(self, par, slot, count):
+        self.some(par, slot, count).wait_recv()
+
+    def lane_pack(self, pack):
+        return (pack + 1) % self.packs
+
+    def shards(self, k):
+        zz = (self.z + k) % 4
+        return ((zz, 1 - self.x, 1 - self.y), (zz, self.x, 1 - self.y), (zz, 1 - self.x, self.y), (zz, self.x, self.y))
+
+    def loads(self, pack):
+        par = pack % 2
+        return [
+            pltpu.make_async_copy(
+                self.part.at[yy * 2 + self.c, :, lanes_of(self.lane_pack(pack))], self.mine.at[par, yy], self.load.at[yy]
+            )
+            for yy in range(2)
+        ]
+
+    def launch(self, pack):
+        par = pack % 2
+        pl.when(pack >= 2)(lambda: pl.semaphore_wait(self.credit.at[pack - 2], 6))
+        for r in self.loads(pack):
+            r.start()
+        for k in ORDER:
+            for i, (zz, xx, yy) in enumerate(self.shards(k)):
+                rows = rows_of(zz, xx, 0, 192)
+                self.put(
+                    par, R_C + 4 * k + i,
+                    self.part.at[yy * 2 + 1 - self.c, rows, lanes_of(self.lane_pack(pack))],
+                    self.buf_c.at[par, yy, rows], self.cn,
+                )
+
+    def core(self, pack, k):
+        par = pack % 2
+        sh = self.shards(k)
+
+        @pl.when(k == ORDER[0])
+        def _():
+            for r in self.loads(pack):
+                r.wait()
+
+        for i, (zz, xx, yy) in enumerate(sh):
+            self.got(par, R_C + 4 * k + i, 192)
+            add_rows(self.at(par, sh[i], 0, 192), self.buf_c.at[par, yy, rows_of(zz, xx, 0, 192)], 192)
+        v = self.buf_v
+        self.put(par, R_V + 4 * k, self.at(par, sh[0], 0, 96), v.at[par, k, 0], self.yn)
+        self.put(par, R_V + 4 * k + 1, self.at(par, sh[0], 96, 96), v.at[par, k, 1], self.xn)
+        self.put(par, R_V + 4 * k + 2, self.at(par, sh[1], 0, 96), v.at[par, k, 2], self.yn)
+        self.put(par, R_V + 4 * k + 3, self.at(par, sh[2], 96, 96), v.at[par, k, 3], self.xn)
+
+    def vees(self, pack, k):
+        par = pack % 2
+        sh = self.shards(k)
+        peer = ((self.z + k) % 4, self.x, self.y, self.c)
+        v = self.buf_v
+        self.got(par, R_V + 4 * k, 96)
+        add_rows(self.at(par, sh[2], 0, 96), v.at[par, k, 0], 96)
+
+        @pl.when(k > 0)
+        def _():
+            self.put(par, R_U + 2 * (k - 1), self.at(par, sh[2], 0, 64), self.buf_u.at[par, k - 1, 0], self.xn)
+            self.put(par, R_ZC + 2 * (k - 1), self.at(par, sh[2], 64, 32), self.buf_zc.at[par, k - 1, 0], peer)
+
+        self.got(par, R_V + 4 * k + 1, 96)
+        add_rows(self.at(par, sh[1], 96, 96), v.at[par, k, 1], 96)
+
+        @pl.when(k > 0)
+        def _():
+            self.put(par, R_U + 2 * (k - 1) + 1, self.at(par, sh[1], 128, 64), self.buf_u.at[par, k - 1, 1], self.yn)
+            self.put(par, R_ZC + 2 * (k - 1) + 1, self.at(par, sh[1], 96, 32), self.buf_zc.at[par, k - 1, 1], peer)
+            self.got(par, R_V + 4 * k + 2, 96)
+            add_rows(self.at(par, sh[3], 0, 96), v.at[par, k, 2], 96)
+            self.got(par, R_V + 4 * k + 3, 96)
+            add_rows(self.at(par, sh[3], 96, 96), v.at[par, k, 3], 96)
+
+    def yous(self, pack, k):
+        par = pack % 2
+        sh = self.shards(k)
+        peer = ((self.z + k) % 4, self.x, self.y, self.c)
+        self.got(par, R_U + 2 * (k - 1), 64)
+        add_rows(self.at(par, sh[3], 0, 64), self.buf_u.at[par, k - 1, 0], 64)
+        self.got(par, R_U + 2 * (k - 1) + 1, 64)
+        add_rows(self.at(par, sh[3], 128, 64), self.buf_u.at[par, k - 1, 1], 64)
+        self.put(par, R_Z + k - 1, self.at(par, sh[3], 0, 192), self.buf_z.at[par, k - 1], peer)
+
+    def near(self, pack):
+        par = pack % 2
+        sh = self.shards(0)
+        for j, (shard, first, whole, nb) in enumerate(((sh[2], 64, 0, self.xn), (sh[1], 96, 96, self.yn))):
+            for k in range(3):
+                self.got(par, R_ZC + 2 * k + j, 32)
+            into = self.at(par, shard, first, 32)
+            b = self.buf_zc
+            into[...] = (
+                into[...].astype(jnp.float32)
+                + b[par, 0, j].astype(jnp.float32)
+                + b[par, 1, j].astype(jnp.float32)
+                + b[par, 2, j].astype(jnp.float32)
+            ).astype(into.dtype)
+            self.put(par, R_F + j, self.at(par, shard, whole, 96), self.buf_f.at[par, j], nb)
+
+    def out_copy(self, pack):
+        return pltpu.make_async_copy(self.stage, self.out.at[:, lanes_of(self.lane_pack(pack))], self.out_sem)
+
+    def final(self, pack):
+        par = pack % 2
+        own = self.at(par, self.shards(0)[3], 0, 192)
+        self.got(par, R_V + 2, 96)
+        self.got(par, R_V + 3, 96)
+        for k in range(3):
+            self.got(par, R_Z + k, 192)
+        for j in range(2):
+            self.got(par, R_F + j, 96)
+        pl.when(pack > 0)(lambda: self.out_copy(pack).wait())
+        for j in range(2):
+            def one(t, carry, j=j):
+                r = pl.ds(pl.multiple_of(t * TILE, TILE), TILE)
+                rr = pl.ds(pl.multiple_of(j * 96 + t * TILE, TILE), TILE)
+                total = own[rr].astype(jnp.float32) + self.buf_v[par, 0, 2 + j, r].astype(jnp.float32)
+                total = total + self.buf_f[par, j, r].astype(jnp.float32)
+                for k in range(3):
+                    total = total + self.buf_z[par, k, rr].astype(jnp.float32)
+                self.stage[rr] = total
+                return carry
+            lax.fori_loop(0, 96 // TILE, one, 0)
+        self.out_copy(pack).start()
+        for slot in range(R_COUNT):
+            self.some(par, slot, R_ROWS[slot]).wait_send()
+
+        @pl.when(pack + 2 < self.packs)
+        def _():
+            z, x, y, c = self.z, self.x, self.y, self.c
+            for t in (self.xn, self.yn, self.cn) + tuple(((z + k) % 4, x, y, c) for k in (1, 2, 3)):
+                pl.semaphore_signal(self.credit.at[pack], inc=1, device_id=device(*t), device_id_type=MESH_ID)
+
+    def step(self, s):
+        total = 4 * self.packs
+        pl.when(s < total)(lambda: self.core(s // 4, (s % 4 + 1) % 4))
+
+        @pl.when((s >= 1) & (s <= total))
+        def _():
+            self.vees((s + 3) // 4 - 1, s % 4)
+
+        @pl.when((s >= 2) & (s <= total + 1))
+        def _():
+            before = (s + 2) // 4 - 1
+            k = (s + 3) % 4
+            pl.when(k > 0)(lambda: self.yous(before, k))
+            pl.when(k == 0)(lambda: self.final(before))
+
+        pl.when((s >= 4) & (s % 4 == 0))(lambda: self.near(s // 4 - 1))
+        pl.when((s % 4 == 2) & (s // 4 + 1 < self.packs))(lambda: self.launch(s // 4 + 1))
+
+    def finish(self):
+        self.out_copy(self.packs - 1).wait()
+
+
+def scatter_scratch(packs):
+    bf = jnp.bfloat16
+    return [
+        pltpu.VMEM((2, 2, 8 * ROWS, LANES), bf),
+        pltpu.VMEM((2, 2, 8 * ROWS, LANES), bf),
+        pltpu.VMEM((2, 4, 4, 96, LANES), bf),
+        pltpu.VMEM((2, 3, 2, 64, LANES), bf),
+        pltpu.VMEM((2, 3, 2, 32, LANES), bf),
+        pltpu.VMEM((2, 3, 192, LANES), bf),
+        pltpu.VMEM((2, 2, 96, LANES), bf),
+        pltpu.SemaphoreType.DMA((2, R_COUNT)),
+        pltpu.SemaphoreType.DMA((2, R_COUNT)),
+        pltpu.SemaphoreType.DMA((2,)),
+        pltpu.SemaphoreType.REGULAR((packs,)),
+        pltpu.VMEM((ROWS, LANES), jnp.float32),
+        pltpu.SemaphoreType.DMA,
+    ]
+
+
+BF = jnp.bfloat16
+F32 = jnp.float32
+CHUNK = 256
+
+
+def gain_rows(table, line, into):
+    lines = [None] * 13
+    for i in range(32):
+        first = (48 * i) // 128
+        for j in range(2):
+            got = table[i, line + j : line + j + 1, :]
+            lines[first + j] = got if lines[first + j] is None else lines[first + j] + got
+    for r in range(12):
+        into[:, 128 * r : 128 * (r + 1)] = lines[r]
+
+
+def loop(count, body):
+    def one(t, carry):
+        body(t)
+        return carry
+
+    lax.fori_loop(0, count, one, 0)
+
+
+def tile_rows(t, size):
+    return pl.ds(pl.multiple_of(t * size, size), size)
+
+
+def norm_rows(src, gain, into, tokens):
+    def one(t):
+        r = tile_rows(t, 32)
+        v = src[r].astype(F32)
+        scale = lax.rsqrt(jnp.mean(v * v, axis=-1, keepdims=True) + EPS)
+        into[r] = (v * scale * gain[...]).astype(BF)
+
+    loop(tokens // 32, one)
+
+
+def gelu_parts(u):
+    root = 0.7978845608028654
+    t = jnp.tanh(root * (u + 0.044715 * (u * u * u)))
+    return 0.5 * u * (1.0 + t), t
+
+
+def nt(a, b):
+    return lax.dot_general(a, b, (((1,), (1,)), ((), ())), preferred_element_type=F32)
+
+
+def tn(a, b):
+    return lax.dot_general(a, b, (((0,), (0,)), ((), ())), preferred_element_type=F32)
+
+
+def nn(a, b):
+    return jnp.dot(a, b, preferred_element_type=F32)
+
+
+def forward_kernel(
+    packs, tokens, width, seq, heads, scale,
+    own, tile, x_any, teacher_any, cotangent_any, buckets, bias_smem, blocks_row, blocks_col, valid_row, valid_col,
+    whole, table, n1_out, n2_out, qkv_out, probs_out, pre_out, act_out, middle_out, layer_out, grad_out, gffn_out, loss_out,
+    x, n1, n2, acc, bias, mask, wbuf, qs, ps, pre, act, tabv, gain1, gain2, teach, cot, lossv,
+    send, recv, local, tile_send, tile_recv, tile_local, in_sem, w_sem, p_sem, q_sem, pre_sem, act_sem, out_sem,
+):
+    f = lax.axis_index("fsdp")
+    d = lax.axis_index("dp")
+    micro = tokens // seq
+    per = heads // 4
+    size = 192 // per
+    start_barrier()
+    g = Gather(own, whole, send, recv, packs)
+    g.launch(0)
+    tiles = exchange(lambda other: tile, table, tile_send, tile_recv)
+    tile_keep = pltpu.make_async_copy(tile, table.at[f * 4 + d], tile_local)
+    tile_keep.start()
+    bounce = [
+        pltpu.make_async_copy(own.at[:, pl.ds(p * LANES, LANES)], wbuf.at[1, pl.ds(p * ROWS, ROWS)], local.at[p])
+        for p in range(packs)
+    ]
+    keep = [
+        pltpu.make_async_copy(
+            wbuf.at[1, pl.ds(p * ROWS, ROWS)],
+            whole.at[d, pl.ds(pl.multiple_of(f * ROWS, ROWS), ROWS), pl.ds(p * LANES, LANES)],
+            local.at[p],
+        )
+        for p in range(packs)
+    ]
+    for r in bounce:
+        r.start()
+    load_x = pltpu.make_async_copy(x_any, x, in_sem.at[0])
+    load_x.start()
+    g.step(0)
+    for a, b in zip(bounce, keep):
+        a.wait()
+        b.start()
+    rows_i = lax.broadcasted_iota(jnp.int32, (seq, seq), 0)
+    cols_i = lax.broadcasted_iota(jnp.int32, (seq, seq), 1)
+    for m in range(micro):
+        ok = (blocks_row[m : m + 1, :] <= blocks_col[m * seq : (m + 1) * seq, :]) & (valid_row[m : m + 1, :] == 1)
+        mask[m] = jnp.where(ok | (rows_i == cols_i), 1.0, 0.0)
+
+    def bias_tile(t):
+        r = tile_rows(t, 8)
+        b = buckets[r]
+        totals = [jnp.zeros((8, seq), F32)] * heads
+        for k in range(32):
+            here = b == k
+            totals = [jnp.where(here, bias_smem[k, h], v) for h, v in enumerate(totals)]
+        for h in range(heads):
+            bias[h, r] = totals[h]
+
+    step_tiles = -(-(seq // 8) // 5)
+
+    def early(s):
+        def some(i):
+            t = s * step_tiles + i
+            pl.when(t < seq // 8)(lambda: bias_tile(t))
+
+        loop(step_tiles, some)
+        g.step(s + 1)
+
+    loop(5, early)
+    tile_keep.wait()
+    tiles.wait()
+    load_table = pltpu.make_async_copy(table, tabv, in_sem.at[1])
+    load_table.start()
+    load_x.wait()
+    load_table.wait()
+    gain_rows(tabv, 0, gain1)
+    gain_rows(tabv, 2, gain2)
+    load_t = pltpu.make_async_copy(teacher_any, teach, in_sem.at[2])
+    load_t.start()
+    load_c = pltpu.make_async_copy(cotangent_any, cot, in_sem.at[3])
+    load_c.start()
+    norm_rows(x, gain1, n1, tokens)
+
+    def copy_x(t):
+        r = tile_rows(t, 32)
+        acc[r] = x[r].astype(F32)
+
+    loop(tokens // 32, copy_x)
+    n1_copy = pltpu.make_async_copy(n1, n1_out, out_sem.at[0])
+    n1_copy.start()
+    for r in keep:
+        r.wait()
+    g.arrived(0)
+
+    def load_w(i, slot):
+        return pltpu.make_async_copy(
+            whole.at[i % 4, :, lanes_of(i // 4)], wbuf.at[slot], w_sem.at[slot]
+        )
+
+    load_w(0, 0).start()
+
+    def probs_copy(dd, m, slot):
+        return pltpu.make_async_copy(ps.at[slot], probs_out.at[dd * micro + m], p_sem.at[slot])
+
+    def attention(dd):
+        slot = dd % 2
+        pl.when(dd < 3)(lambda: load_w(dd + 1, 1 - slot).start())
+        load_w(dd, slot).wait()
+        pl.when(dd > 0)(lambda: pltpu.make_async_copy(qs, qkv_out.at[dd], q_sem).wait())
+        qs[:, 0:576] = nn(n1[...], wbuf[slot, :, 0:576]).astype(BF)
+        g.step(6 + 2 * dd)
+        for m in range(micro):
+            r = slice(m * seq, (m + 1) * seq)
+            pl.when(dd > 0)(lambda: probs_copy(dd, m, m).wait())
+            for hh in range(per):
+                a = hh * size
+                s = nt(qs[r, a : a + size], qs[r, 192 + a : 192 + a + size]) + bias[dd * per + hh]
+                s = jnp.where(mask[m] > 0.0, s, NEG)
+                top = jnp.max(s, axis=-1, keepdims=True)
+                e = jnp.exp(s - top)
+                p = e * (1.0 / jnp.sum(e, axis=-1, keepdims=True))
+                ps[m, hh] = p
+                qs[r, 576 + a : 576 + a + size] = nn(p.astype(BF), qs[r, 384 + a : 384 + a + size]).astype(BF)
+            probs_copy(dd, m, m).start()
+        g.step(7 + 2 * dd)
+        for m in range(micro):
+            r = slice(m * seq, (m + 1) * seq)
+            acc[r] += nt(qs[r, 576:768], wbuf[slot, :, 576:768])
+        pltpu.make_async_copy(qs, qkv_out.at[dd], q_sem).start()
+
+    loop(4, attention)
+    pltpu.make_async_copy(qs, qkv_out.at[0], q_sem).wait()
+    for m in range(micro):
+        probs_copy(3, m, m).wait()
+    mid_copy = pltpu.make_async_copy(acc, middle_out, out_sem.at[1])
+    mid_copy.start()
+    norm_rows(acc, gain2, n2, tokens)
+    n2_copy = pltpu.make_async_copy(n2, n2_out, out_sem.at[2])
+    n2_copy.start()
+    mid_copy.wait()
+
+    def pre_copy(t, slot):
+        return pltpu.make_async_copy(pre.at[slot], pre_out.at[t], pre_sem.at[slot])
+
+    def act_copy(t, slot):
+        return pltpu.make_async_copy(act.at[slot], act_out.at[t], act_sem.at[slot])
+
+    def feed(t):
+        slot = t % 2
+
+        @pl.when(t % 4 == 0)
+        def _():
+            g.arrived(1 + t // 4)
+            load_w(4 + t, slot).start()
+
+        pl.when(t % 4 < 3)(lambda: load_w(5 + t, 1 - slot).start())
+        load_w(4 + t, slot).wait()
+
+        @pl.when(t > 1)
+        def _():
+            pre_copy(t, slot).wait()
+            act_copy(t, slot).wait()
+
+        for m in range(micro):
+            r = slice(m * seq, (m + 1) * seq)
+            gu = nn(n2[r], wbuf[slot, :, 0 : 2 * CHUNK])
+            pre[slot, r] = gu
+            ge, _ = gelu_parts(gu[:, 0:CHUNK])
+            act[slot, r] = (ge * gu[:, CHUNK:]).astype(BF)
+        pre_copy(t, slot).start()
+        act_copy(t, slot).start()
+
+        @pl.when(t < 8)
+        def _():
+            pl.when(t % 2 == 0)(lambda: g.step(14 + t // 2))
+
+        pl.when((t >= 8) & (t < 12))(lambda: g.step(10 + t))
+        for m in range(micro):
+            r = slice(m * seq, (m + 1) * seq)
+            acc[r] += nt(act[slot, r], wbuf[slot, :, 2 * CHUNK :])
+
+    loop(16, feed)
+    load_t.wait()
+    load_c.wait()
+    n1_copy.wait()
+    n2_copy.wait()
+    for slot in range(2):
+        pre_copy(14 + slot, slot).wait()
+        act_copy(14 + slot, slot).wait()
+    total = tabv[0, 4:5, 0:1]
+    for i in range(1, 32):
+        total = total + tabv[i, 4:5, 0:1]
+    factor = (2.0 * scale / width) / total
+    lossv[...] = jnp.zeros_like(lossv)
+
+    def ends(t):
+        r = tile_rows(t, 16)
+        full = acc[r]
+        gap = full - teach[r].astype(F32)
+        weighted = valid_col[r] * gap
+        grad = scale * cot[r].astype(F32) + factor * weighted
+        acc[r] = grad
+        x[r] = grad.astype(BF)
+        n1[r] = full.astype(BF)
+        lossv[...] += weighted * gap
+
+    loop(tokens // 16, ends)
+    copies = [
+        pltpu.make_async_copy(n1, layer_out, out_sem.at[0]),
+        pltpu.make_async_copy(acc, grad_out, out_sem.at[1]),
+        pltpu.make_async_copy(x, gffn_out, out_sem.at[2]),
+    ]
+    for r in copies:
+        r.start()
+    loss_out[...] = jnp.zeros_like(loss_out) + jnp.sum(lossv[...])
+    g.finish()
+    for r in copies:
+        r.wait()
+
+
+def forward(own, tile, x, teacher, cotangent, buckets, bias_table, blocks_row, blocks_col, valid_row, valid_col, scale):
+    packs = own.shape[1] // LANES
+    tokens, width = x.shape
+    seq = buckets.shape[0]
+    heads = bias_table.shape[1]
+    micro = tokens // seq
+    any_ = pl.BlockSpec(memory_space=pl.ANY)
+    vmem = pl.BlockSpec(memory_space=pltpu.VMEM)
+    smem = pl.BlockSpec(memory_space=pltpu.SMEM)
+    S = jax.ShapeDtypeStruct
+    dma = pltpu.SemaphoreType.DMA
+    outs = (
+        S((4, 8 * ROWS, own.shape[1]), BF), S((32, 8, 128), F32), S((tokens, width), BF), S((tokens, width), BF),
+        S((4, tokens, 768), BF), S((4 * micro, heads // 4, seq, seq), F32), S((16, tokens, 2 * CHUNK), F32),
+        S((16, tokens, CHUNK), BF), S((tokens, width), F32), S((tokens, width), BF), S((tokens, width), F32), S((tokens, width), BF), S((8, 128), F32),
+    )
+    return pl.pallas_call(
+        functools.partial(forward_kernel, packs, tokens, width, seq, heads, scale),
+        out_shape=outs,
+        in_specs=[any_] * 5 + [vmem, smem] + [vmem] * 4,
+        out_specs=[any_] * 12 + [vmem],
+        scratch_shapes=[
+            pltpu.VMEM((tokens, width), BF), pltpu.VMEM((tokens, width), BF), pltpu.VMEM((tokens, width), BF),
+            pltpu.VMEM((tokens, width), F32), pltpu.VMEM((heads, seq, seq), F32), pltpu.VMEM((micro, seq, seq), F32),
+            pltpu.VMEM((2, 8 * ROWS, LANES), BF), pltpu.VMEM((tokens, 768), BF), pltpu.VMEM((micro, heads // 4, seq, seq), F32),
+            pltpu.VMEM((2, tokens, 2 * CHUNK), F32), pltpu.VMEM((2, tokens, CHUNK), BF), pltpu.VMEM((32, 8, 128), F32),
+            pltpu.VMEM((1, width), F32), pltpu.VMEM((1, width), F32), pltpu.VMEM((tokens, width), BF),
+            pltpu.VMEM((tokens, width), BF), pltpu.VMEM((16, width), F32),
+            dma((packs, G_COUNT)), dma((packs, G_COUNT)), dma((packs,)), dma, dma, dma, dma((4,)), dma((2,)), dma((2,)), dma,
+            dma((2,)), dma((2,)), dma((3,)),
+        ],
+        compiler_params=pltpu.CompilerParams(collective_id=1, has_side_effects=True, vmem_limit_bytes=63 * 1024 * 1024),
+    )(own, tile, x, teacher, cotangent, buckets, bias_table, blocks_row, blocks_col, valid_row, valid_col)
+
+
+def prepare(weights, gain_one, gain_two, valid):
+    part = weights[4].shape[1]
+    pads = [jnp.pad(w, ((0, 0), (0, 4 * CHUNK - part))) for w in weights[4:]]
+    pieces = list(weights[:4])
+    for j in range(4):
+        pieces += [w[:, j * CHUNK : (j + 1) * CHUNK] for w in pads]
+    own = jnp.concatenate(pieces, axis=1)
+    me = lax.axis_index("fsdp") * 4 + lax.axis_index("dp")
+    first = (me * 48) % 128
+
+    def lines(gain):
+        return lax.dynamic_update_slice(jnp.zeros((256,), F32), gain.astype(F32), (first,)).reshape(2, 128)
+
+    count = jnp.zeros((4, 128), F32) + jnp.sum(valid.astype(F32))
+    return own, jnp.concatenate([lines(gain_one), lines(gain_two), count])
+
+
+def gelu_slope(u, t):
+    root = 0.7978845608028654
+    return 0.5 * (1.0 + t) + 0.5 * u * (1.0 - t * t) * root * (1.0 + 3.0 * 0.044715 * (u * u))
+
+
+def norm_back(src_row, up_row, gain, gain_sum):
+    v, u = src_row, up_row
+    scale = lax.rsqrt(jnp.mean(v * v, axis=-1, keepdims=True) + EPS)
+    scaled = u * gain
+    mean = jnp.mean(scaled * v, axis=-1, keepdims=True)
+    term = u * v * scale
+    total = term[0:8]
+    for i in range(1, term.shape[0] // 8):
+        total = total + term[8 * i : 8 * i + 8]
+    gain_sum[...] += total
+    return scale * scaled - v * (scale * scale * scale) * mean
+
+
+def backward_kernel(
+    packs, tokens, width, seq, heads,
+    whole, table, x_any, n1_any, n2_any, qkv_any, probs_any, pre_any, act_any, mid_any, gout_any, gffn_any, buckets, loss,
+    part, out, hidden_out, tiles_out, sums_out,
+    low, src, acc, acc2, wbuf, pre, act, ggu, gst, strm, qs, ps, ga, gqkv, bsum, gain1, gain2, sum1, sum2, tilev, tabv,
+    in_sem, w_sem, pre_sem, act_sem, g_sem, s_sem, q_sem, p_sem, out2_sem, tile_send, tile_recv, tile_local, *scatter_refs,
+):
+    micro = tokens // seq
+    per = heads // 4
+    size = 192 // per
+    me = lax.axis_index("fsdp") * 4 + lax.axis_index("dp")
+    start_barrier()
+    rs = Scatter(part, out, *scatter_refs, packs)
+
+    def fetch(a, b, sem):
+        r = pltpu.make_async_copy(a, b, sem)
+        r.start()
+        return r
+
+    loads = [fetch(gffn_any, low, in_sem.at[0]), fetch(n2_any, src, in_sem.at[1]), fetch(table, tabv, in_sem.at[2])]
+
+    def load_w(i, slot):
+        return pltpu.make_async_copy(whole.at[i % 4, :, lanes_of(i // 4)], wbuf.at[slot], w_sem.at[slot])
+
+    def load_pre(t, slot):
+        return pltpu.make_async_copy(pre_any.at[t], pre.at[slot], pre_sem.at[slot])
+
+    def load_act(t, slot):
+        return pltpu.make_async_copy(act_any.at[t], act.at[slot], act_sem.at[slot])
+
+    def put_g(dd, lane_pack):
+        return pltpu.make_async_copy(gst, part.at[dd, :, lanes_of(lane_pack)], g_sem)
+
+    for r in (load_w(4, 0), load_pre(0, 0), load_act(0, 0)):
+        r.start()
+    sum1[...] = jnp.zeros_like(sum1)
+    sum2[...] = jnp.zeros_like(sum2)
+
+    def clear(t):
+        r = tile_rows(t, 32)
+        acc[r] = jnp.zeros((32, width), F32)
+        acc2[r] = jnp.zeros((32, width), F32)
+
+    loop(tokens // 32, clear)
+    for r in loads:
+        r.wait()
+    gain_rows(tabv, 0, gain1)
+    gain_rows(tabv, 2, gain2)
+    half = width // 2
+
+    def feed(t):
+        slot = t % 2
+
+        @pl.when(t < 15)
+        def _():
+            load_w(5 + t, 1 - slot).start()
+            load_pre(t + 1, 1 - slot).start()
+            load_act(t + 1, 1 - slot).start()
+
+        load_w(4 + t, slot).wait()
+        load_pre(t, slot).wait()
+        load_act(t, slot).wait()
+        for m in range(micro):
+            r = slice(m * seq, (m + 1) * seq)
+            gh = nn(low[r], wbuf[slot, :, 2 * CHUNK :])
+            u = pre[slot, r, 0:CHUNK]
+            ge, th = gelu_parts(u)
+            ggu[r, 0:CHUNK] = (gh * pre[slot, r, CHUNK:] * gelu_slope(u, th)).astype(BF)
+            ggu[r, CHUNK:] = (gh * ge).astype(BF)
+        pl.when((t > 0) & (t != 4))(lambda: put_g(0, 0).wait())
+        for h in range(2):
+            c = slice(h * half, (h + 1) * half)
+            gst[c, 0 : 2 * CHUNK] = tn(src[:, c], ggu[...]).astype(BF)
+            gst[c, 2 * CHUNK :] = tn(low[:, c], act[slot]).astype(BF)
+        put_g(t % 4, 1 + t // 4).start()
+        for m in range(micro):
+            r = slice(m * seq, (m + 1) * seq)
+            acc[r] += nt(ggu[r], wbuf[slot, :, 0 : 2 * CHUNK])
+
+        @pl.when(t == 3)
+        def _():
+            put_g(0, 0).wait()
+            rs.launch(0)
+
+        pl.when((t > 3) & (t % 2 == 1))(lambda: rs.step(t // 2 - 2))
+
+    loop(16, feed)
+    put_g(0, 0).wait()
+    n1_load = fetch(n1_any, src, in_sem.at[1])
+    load_w(0, 0).start()
+
+    def strm_load(t, slot):
+        r = tile_rows(t, 32)
+        return [
+            pltpu.make_async_copy(mid_any.at[r], strm.at[slot, 0], s_sem.at[slot, 0]),
+            pltpu.make_async_copy(gout_any.at[r], strm.at[slot, 1], s_sem.at[slot, 1]),
+        ]
+
+    for r in strm_load(0, 0):
+        r.start()
+
+    def norm_two(t):
+        slot = t % 2
+
+        @pl.when(t + 1 < tokens // 32)
+        def _():
+            for r in strm_load(t + 1, 1 - slot):
+                r.start()
+
+        for r in strm_load(t, slot):
+            r.wait()
+        r = tile_rows(t, 32)
+        grad = strm[slot, 1] + norm_back(strm[slot, 0], acc[r], gain2[...], sum2)
+        acc[r] = grad
+        low[r] = grad.astype(BF)
+
+    loop(tokens // 32, norm_two)
+    n1_load.wait()
+
+    def probs_load(dd, m):
+        return pltpu.make_async_copy(probs_any.at[dd * micro + m], ps.at[m], p_sem.at[m])
+
+    def attention(dd):
+        slot = dd % 2
+        q_load = pltpu.make_async_copy(qkv_any.at[dd], qs, q_sem)
+        q_load.start()
+        for m in range(micro):
+            probs_load(dd, m).start()
+        pl.when(dd < 3)(lambda: load_w(dd + 1, 1 - slot).start())
+        load_w(dd, slot).wait()
+        ga[...] = nn(low[...], wbuf[slot, :, 576:768]).astype(BF)
+        q_load.wait()
+        pl.when(dd > 0)(lambda: put_g(0, 0).wait())
+        gst[:, 576:768] = tn(low[...], qs[:, 576:768]).astype(BF)
+        rs.step(6 + 2 * dd)
+        for m in range(micro):
+            r = slice(m * seq, (m + 1) * seq)
+            probs_load(dd, m).wait()
+            for hh in range(per):
+                a = hh * size
+                p = ps[m, hh]
+                go = ga[r, a : a + size]
+                gp = nt(go, qs[r, 384 + a : 384 + a + size])
+                gs = p * (gp - jnp.sum(p * gp, axis=-1, keepdims=True))
+                gs = gs.astype(BF)
+                gqkv[r, a : a + size] = nn(gs, qs[r, 192 + a : 192 + a + size]).astype(BF)
+                gqkv[r, 192 + a : 192 + a + size] = tn(gs, qs[r, a : a + size]).astype(BF)
+                gqkv[r, 384 + a : 384 + a + size] = tn(p.astype(BF), go).astype(BF)
+                if m == 0:
+                    ps[0, hh] = gs.astype(F32)
+                else:
+                    ps[0, hh] += gs.astype(F32)
+        rs.step(7 + 2 * dd)
+        for h in range(2):
+            c = slice(h * half, (h + 1) * half)
+            gst[c, 0:576] = tn(src[:, c], gqkv[...]).astype(BF)
+        put_g(dd, 0).start()
+        for m in range(micro):
+            r = slice(m * seq, (m + 1) * seq)
+            acc2[r] += nt(gqkv[r], wbuf[slot, :, 0:576])
+
+        def by_bucket(i):
+            hh, group = i // 4, i % 4
+
+            def some(t, totals):
+                r = tile_rows(t, 8)
+                b = buckets[r]
+                v = ps[0, hh, r]
+                return tuple(o + jnp.where(b == group * 8 + j, v, 0.0) for j, o in enumerate(totals))
+
+            totals = lax.fori_loop(0, seq // 8, some, (jnp.zeros((8, seq), F32),) * 8)
+            lines = [jnp.sum(o, axis=0, keepdims=True) for o in totals]
+            bsum[dd * per + hh, pl.ds(pl.multiple_of(group * 8, 8), 8)] = jnp.concatenate(lines, axis=0)
+
+        loop(4 * per, by_bucket)
+
+    loop(4, attention)
+    put_g(0, 0).wait()
+    rs.step(14)
+    x_load = fetch(x_any, src, in_sem.at[1])
+    x_load.wait()
+
+    def norm_one(t):
+        r = tile_rows(t, 32)
+        term = norm_back(src[r].astype(F32), acc2[r], gain1[...], sum1)
+        low[r] = (acc[r] + term).astype(BF)
+
+    loop(tokens // 32, norm_one)
+    hidden_copy = fetch(low, hidden_out, out2_sem)
+    one = jnp.sum(sum1[...], axis=0, keepdims=True)
+    two = jnp.sum(sum2[...], axis=0, keepdims=True)
+    biases = lax.dot_general(
+        jnp.ones((8, seq), F32), bsum[...].reshape(heads * 32, seq), (((1,), (1,)), ((), ())),
+        precision=lax.Precision.HIGHEST, preferred_element_type=F32,
+    )
+    lines = [biases[0:1, 128 * i : 128 * (i + 1)] for i in range(3)]
+    none = jnp.zeros((1, 128), F32)
+    for i in range(32):
+        first = 128 * ((48 * i) // 128)
+        rows = []
+        for v in (one, two):
+            rows.append(v[:, first : first + 128])
+            rows.append(v[:, first + 128 : first + 256] if first + 128 < width else none)
+        tilev[i] = jnp.concatenate(rows + [loss[0:1, :]] + lines, axis=0)
+    tile_copy = fetch(tilev, tiles_out, in_sem.at[0])
+    rs.step(15)
+    tile_copy.wait()
+    tiles = exchange(lambda other: tiles_out.at[other], sums_out, tile_send, tile_recv)
+    tile_keep = fetch(tilev.at[me], sums_out.at[me], tile_local)
+    lax.fori_loop(16, 4 * packs + 2, lambda s, carry: (rs.step(s), carry)[1], 0)
+    rs.finish()
+    hidden_copy.wait()
+    tile_keep.wait()
+    tiles.wait()
+
+
+def backward(whole, table, x, n1, n2, qkv, probs, pre, act, mid, gout, gffn, buckets, loss, heads):
+    packs = whole.shape[2] // LANES
+    tokens, width = x.shape
+    seq = buckets.shape[0]
+    micro = tokens // seq
+    any_ = pl.BlockSpec(memory_space=pl.ANY)
+    vmem = pl.BlockSpec(memory_space=pltpu.VMEM)
+    S = jax.ShapeDtypeStruct
+    V = pltpu.VMEM
+    dma = pltpu.SemaphoreType.DMA
+    outs = (
+        S(whole.shape, BF), S((ROWS, whole.shape[2]), F32), S((tokens, width), BF), S((32, 8, 128), F32), S((32, 8, 128), F32),
+    )
+    return pl.pallas_call(
+        functools.partial(backward_kernel, packs, tokens, width, seq, heads),
+        out_shape=outs,
+        in_specs=[any_] * 12 + [vmem] * 2,
+        out_specs=[any_] * 5,
+        scratch_shapes=[
+            V((tokens, width), BF), V((tokens, width), BF), V((tokens, width), F32), V((tokens, width), F32),
+            V((2, 8 * ROWS, LANES), BF), V((2, tokens, 2 * CHUNK), F32), V((2, tokens, CHUNK), BF), V((tokens, 2 * CHUNK), BF),
+            V((8 * ROWS, LANES), BF), V((2, 2, 32, width), F32), V((tokens, 768), BF), V((micro, heads // 4, seq, seq), F32),
+            V((tokens, 192), BF), V((tokens, 576), BF), V((heads, 32, seq), F32), V((1, width), F32), V((1, width), F32),
+            V((8, width), F32), V((8, width), F32), V((32, 8, 128), F32), V((32, 8, 128), F32),
+            dma((3,)), dma((2,)), dma((2,)), dma((2,)), dma, dma((2, 2)), dma, dma((micro,)), dma, dma, dma, dma,
+        ] + scatter_scratch(packs),
+        compiler_params=pltpu.CompilerParams(collective_id=2, has_side_effects=True, vmem_limit_bytes=67043328),
+    )(whole, table, x, n1, n2, qkv, probs, pre, act, mid, gout, gffn, buckets, loss)
+
+
+def tuned_body(
+    hidden, teacher, cotangent, valid_mask, blocks, buckets, first_gain, query_weight, key_weight, value_weight,
+    output_weight, second_gain, gate_weight, up_weight, down_weight, bias_table,
+):
+    micro, _, seq, width = hidden.shape
+    tokens = micro * seq
+    bucket_count, heads = bias_table.shape
+    part = gate_weight.shape[1]
+    cols = query_weight.shape[1]
+    per = first_gain.shape[0]
+    scale = float(tokens * 32 * width)
+    valid = valid_mask.reshape(micro, seq)
+    block_ids = blocks.reshape(micro, seq)
+    weights = (query_weight, key_weight, value_weight, output_weight, gate_weight, up_weight, down_weight)
+    own, tile = prepare(weights, first_gain, second_gain, valid)
+    x = hidden.reshape(tokens, width)
+    whole, table, n1, n2, qkv, probs, pre, act, mid, layer, gout, gffn, loss = forward(
+        own, tile, x, teacher.reshape(tokens, width), cotangent.reshape(tokens, width), buckets, bias_table.astype(F32),
+        block_ids, block_ids.reshape(tokens, 1), valid, valid.reshape(tokens, 1).astype(F32), scale,
+    )
+    _, shard, hidden_grad, _, sums = backward(
+        whole, table, x, n1, n2, qkv, probs, pre, act, mid, gout, gffn, buckets, loss, heads
+    )
+    sums = jnp.sum(sums, axis=0)
+    me = lax.axis_index("fsdp") * 4 + lax.axis_index("dp")
+    first = (me * per) % 128
+    gain_one = lax.dynamic_slice(sums[0:2].reshape(256), (first,), (per,))
+    gain_two = lax.dynamic_slice(sums[2:4].reshape(256), (first,), (per,))
+    valid_total = jnp.sum(table[:, 4, 0])
+    ff = [
+        jnp.concatenate([shard[:, LANES * (j + 1) + i * CHUNK : LANES * (j + 1) + (i + 1) * CHUNK] for j in range(4)], axis=1)[:, :part]
+        for i in range(3)
+    ]
+    at = [shard[:, i * cols : (i + 1) * cols] for i in range(4)]
+    return (
+        layer.reshape(hidden.shape),
+        sums[4, 0] / (valid_total * width),
+        hidden_grad.reshape(hidden.shape),
+        gain_one, at[0], at[1], at[2], at[3], gain_two, ff[0], ff[1], ff[2],
+        sums[5:8].reshape(heads, bucket_count).T,
+    )
+
+
 def solution(mesh):
     in_specs = (
         P(None, ("fsdp", "dp"), None, None),
@@ -343,4 +1374,5 @@
         P("fsdp", "dp"),
         P(),
     )
-    return jax.shard_map(body, mesh=mesh, in_specs=in_specs, out_specs=out_specs, check_vma=False)
+    chosen = tuned_body if dict(mesh.shape) == {"fsdp": 8, "dp": 4} else body
+    return jax.shard_map(chosen, mesh=mesh, in_specs=in_specs, out_specs=out_specs, check_vma=False)

time: 2020 us -> 557 us (0.28)
  waiting for transfers between devices: 1080 us -> 0 us
  Pallas kernels: 0 us -> 526 us
  local copies, waits for them, and re-layouts: 382 us -> 18.7 us
  matrix products: 356 us -> 0 us
  blocking collectives: 123 us -> 0 us
  other arithmetic: 41 us -> 6.84 us
    reduce_scatter x7 -> x0, waiting for transfers between devices: 827 us -> none  [the longest x1 253 us: body(): lax.psum_scatter(totals[7], ('fsdp', 'dp'), scatter_dimension=0, tiled=True)]
    pallas_call x0 -> x2, Pallas kernels: none -> 526 us  [the longest x1 300 us: backward(): pl.pallas_call(functools.partial(backward_kernel, packs, tokens, width, s...]
    dot_general x57 -> x0, matrix products: 356 us -> none  [the longest x14 122 us: over_tokens(): lax.dot_general(former, latter, (((0,), (0,)), ((), ())), preferred_eleme...]
    all_gather x7 -> x0, waiting for transfers between devices: 249 us -> none  [the longest x1 56.5 us: body(): lax.all_gather(up_weight, ('fsdp', 'dp'), axis=0, tiled=True)]
    add x6 -> x1, local copies, waits for them, and re-layouts: 173 us -> 0.65 us  [prepare(): count = jnp.zeros((4, 128), F32) + jnp.sum(valid.astype(F32))]
    reshape x14 -> x2, local copies, waits for them, and re-layouts: 168 us -> 0.68 us  [the longest x1 0.68 us: tuned_body(): sums[5:8].reshape(heads, bucket_count)]
    psum x2 -> x0, blocking collectives: 82.1 us -> none  [the longest x1 42.2 us: body(): valid_total = lax.psum(jnp.sum(valid_float), ('fsdp', 'dp'))]
    unnamed x1 -> x0, blocking collectives: 40.4 us -> none
  transfers between devices with their start and end apart: 14 -> 0, of which waited for: 10 -> 0; matrix products, arithmetic and copies ran while one was open for 27% -> 0% of each run, Pallas kernels for 0% -> 0%
where the time goes in v2:
time: 557 us; the launch traced here: 555 us
  Pallas kernels  526 us (94%)
  local copies, waits for them, and re-layouts  18.7 us (3%)
  other arithmetic  6.84 us (1%)
    pallas_call x1, Pallas kernels, backward(): pl.pallas_call(functools.partial(backward_kernel, packs, tokens, width, s...  300 us
    pallas_call x1, Pallas kernels, forward(): pl.pallas_call(functools.partial(forward_kernel, packs, tokens, width, se...  226 us

profile of v2, /device:TPU:0, one launch (start us, length us, event | category | flops | bytes accessed | tf_op | source)
XLA Modules:
  0.0 555.0 jit_solution(17521469096447194246)
XLA Ops:
  0.6 0.0 copy-start.2
  0.7 0.0 copy-start.3
  0.7 0.0 copy-start.4
  0.7 1.2 pad_slice_fusion.2
  2.0 1.3 pad_slice_fusion
  3.3 1.9 concatenate.15.own
  5.2 0.1 convert_dynamic-update-slice_fusion
  5.3 0.1 convert_dynamic-update-slice_fusion.1
  5.4 0.6 convert_reduce_fusion
  6.0 0.6 add.27
  6.6 0.1 pad.27.clone
  6.7 0.7 maximum_maximum_fusion.tile
  7.4 0.7 copy.37.bias_smem
  8.1 0.6 copy_bitcast_fusion
  8.7 0.9 copy.38.blocks_col
  9.6 0.9 copy.39.valid_col
  10.6 226.3 %shard_map.255 = (bf16[4,1536,3840]{2,1,0:T(8,128)(2,1)}, f32[32,8,128]{2,1,0:T(8,128)}, bf16[768,1536]{1,0:T(8,128)(2,1)}, bf16[768,1536]{1,0:T(8,128)(2,1)}, b...) custom-call(bf16[192,3840]{1,0:T(8,128)(2,1)} %concatenate.15.own, ...), custom_call_target="tpu_custom_call" | custom-call | tf_op jit(solution)/shard_map/pallas_call | solution.py:1000
  236.8 299.9 %shard_map.256 = (bf16[4,1536,3840]{2,1,0:T(8,128)(2,1)}, f32[192,3840]{1,0:T(8,128)}, bf16[768,1536]{1,0:T(8,128)(2,1)}, f32[32,8,128]{2,1,0:T(8,128)}, f32[32,8,128]{2,1,0:T(8,128)}) custom-call(bf16[4,1536,3840]{2,1,0:T(8,128)(2,1)} %get-tuple-element.30.whole, f32[32,8,128]{2,1,0:T(8,128)} %get-tuple-element.31.table, bf16[768,1536]{1,0:T(8,128)(2,1)} %bitcast.26, ...), custom_call_target="tpu_custom_call" | custom-call | tf_op jit(solution)/shard_map/pallas_call | solution.py:1283
  536.8 0.9 reduce_sum.28
  537.7 0.5 slice.129
  538.2 1.5 slice_reduce_fusion
  541.1 0.6 dynamic_slice.6
  541.7 2.2 fusion.1
  543.9 0.6 dynamic_slice.7
  544.5 1.9 fusion
  546.3 1.0 pad_maximum_fusion.6
  547.3 1.0 pad_maximum_fusion.3
  548.3 1.0 pad_maximum_fusion
  549.3 0.7 reshape.86
  549.9 1.4 copy.53
  551.3 1.1 copy-done.1
  552.5 1.4 copy.54
  (23 shorter events, 0.1 us)
Async XLA Ops:
  0.6 2.6 copy-start.2
  0.7 2.6 copy-start.3
  0.7 2.6 copy-start.4
  0.7 2.6 copy-start.5
  0.7 4.5 copy-start.9
  0.7 4.6 copy-start.10
  0.7 4.7 copy-start.6
  0.7 6.7 %copy-start.8 = (bf16[32,12]{0,1:T(8,128)(2,1)S(1)}, bf16[32,12]{0,1:T(8,128)(2,1)}, u32[]{:S(2)}) copy-start(bf16[32,12]{0,1:T(8,128)(2,1)} %param.31) | copy-start | bytes 2308
  0.7 7.4 %copy-start.7 = (s32[2,1,384]{2,1,0:T(1,128)S(1)}, s32[2,1,384]{2,1,0:T(1,128)}, u32[]{:S(2)}) copy-start(s32[2,1,384]{2,1,0:T(1,128)} %param.20) | copy-start | bytes 9220
  546.3 3.6 copy-start
  549.9 2.5 copy-start.1

commit v3 on v2

--- a/solution.py
+++ b/solution.py
@@ -327,7 +327,7 @@
     return (z * 2 + x, y * 2 + c)
 
 
-def start_barrier():
+def tell_all():
     f = lax.axis_index("fsdp")
     d = lax.axis_index("dp")
     barrier = pltpu.get_barrier_semaphore()
@@ -340,7 +340,15 @@
         return carry
 
     lax.fori_loop(1, 32, tell, 0)
-    pl.semaphore_wait(barrier, 31)
+
+
+def hear_all():
+    pl.semaphore_wait(pltpu.get_barrier_semaphore(), 31)
+
+
+def start_barrier():
+    tell_all()
+    hear_all()
 
 
 def exchange(tile_of, table, send, recv):
@@ -371,12 +379,16 @@
     return pl.ds(pl.multiple_of((z * 2 + x) * ROWS + first, 32), count)
 
 
-G_Z, G_X0, G_Y0, G_XZ, G_YZ, G_DY, G_DX = 0, 3, 4, 5, 8, 11, 15
-G_XA, G_XB, G_YA, G_YB, G_C = 19, 22, 25, 28, 31
-G_COUNT = 47
-G_ROWS = (
-    [192] * 3 + [192, 192] + [32] * 6 + [96] * 8 + [64] * 3 + [96] * 3 + [64] * 3 + [96] * 3 + [192] * 16
-)
+G_Z, G_X0, G_Y0, G_XZ, G_YZ, G_DY, G_DX = 0, 4, 5, 6, 10, 14, 18
+G_XA, G_XB, G_YA, G_YB, G_C, G_BACK = 22, 25, 28, 31, 34, 50
+G_COUNT = 53
+
+
+def on_chain(z, k):
+    end = (3 - z) // 3 + z // 3
+    low = end * k + (1 - end) * (k - (3 - k) // 2)
+    high = z // 2
+    return high * (3 - low) + (1 - high) * low
 
 
 class Gather:
@@ -384,14 +396,25 @@
         self.own, self.whole, self.send, self.recv, self.packs = own, whole, send, recv, packs
         self.z, self.x, self.y, self.c = place()
 
-    def put(self, pack, slot, shard, first, count, target, own=False):
+    def put(self, pack, slot, shard, first, count, target, own=False, send=None):
         zz, xx, yy = shard
         there = self.whole.at[yy * 2 + self.c, rows_of(zz, xx, first, count), lanes_of(pack)]
         here = self.own.at[pl.ds(first, count), lanes_of(pack)] if own else there
         pltpu.make_async_remote_copy(
-            here, there, self.send.at[pack, slot], self.recv.at[pack, slot],
+            here, there, self.send.at[pack, slot if send is None else send], self.recv.at[pack, slot],
             device_id=device(*target), device_id_type=MESH_ID,
         ).start()
+
+    def along(self, pack, slot, back, shard, first, count, own=False):
+        z, x, y, c = self.z, self.x, self.y, self.c
+        pl.when(z < 3)(lambda: self.put(pack, slot + z, shard, first, count, (z + 1, x, y, c), own=own))
+        pl.when(z > 0)(lambda: self.put(pack, slot + z, shard, first, count, (z - 1, x, y, c), own=own, send=back))
+
+    def further(self, pack, slot, shard, first, count):
+        z, x, y, c = self.z, self.x, self.y, self.c
+        zz = shard[0]
+        pl.when((zz < z) & (z < 3))(lambda: self.put(pack, slot + zz, shard, first, count, (z + 1, x, y, c)))
+        pl.when((zz > z) & (z > 0))(lambda: self.put(pack, slot + zz, shard, first, count, (z - 1, x, y, c)))
 
     def some(self, pack, slot, count):
         view = self.whole.at[0, pl.ds(0, count), lanes_of(pack)]
@@ -404,14 +427,11 @@
         self.some(pack, slot, count).wait_recv()
 
     def launch(self, pack):
-        z, x, y, c = self.z, self.x, self.y, self.c
-        for k in (1, 2, 3):
-            self.put(pack, G_Z + k - 1, (z, x, y), 0, 192, ((z + k) % 4, x, y, c), own=True)
+        self.along(pack, G_Z, G_BACK, (self.z, self.x, self.y), 0, 192, own=True)
 
     def first(self, pack, k):
         z, x, y, c = self.z, self.x, self.y, self.c
         xn, yn, cn = (z, 1 - x, y, c), (z, x, 1 - y, c), (z, x, y, 1 - c)
-        mine = ((z - k + 4) % 4, x, y)
 
         @pl.when(k == 0)
         def _():
@@ -421,9 +441,12 @@
 
         @pl.when(k > 0)
         def _():
-            self.got(pack, G_Z + k - 1, 192)
-            self.put(pack, G_XA + k - 1, mine, 0, 64, xn)
-            self.put(pack, G_YA + k - 1, mine, 128, 64, yn)
+            zz = on_chain(z, k)
+            mine = (zz, x, y)
+            self.got(pack, G_Z + zz, 192)
+            self.further(pack, G_Z, mine, 0, 192)
+            self.put(pack, G_XA + k - 1, mine, 0, 32, xn)
+            self.put(pack, G_YA + k - 1, mine, 160, 32, yn)
             self.put(pack, G_XB + k - 1, mine, 96, 96, xn)
             self.put(pack, G_YB + k - 1, mine, 0, 96, yn)
             self.put(pack, G_C + 4 * k, mine, 0, 192, cn)
@@ -431,29 +454,29 @@
     def second(self, pack, k):
         z, x, y, c = self.z, self.x, self.y, self.c
         xn, yn, cn = (z, 1 - x, y, c), (z, x, 1 - y, c), (z, x, y, 1 - c)
-        zz = (z - k + 4) % 4
-        across_x, across_y = (zz, 1 - x, y), (zz, x, 1 - y)
 
         @pl.when(k == 0)
         def _():
             self.got(pack, G_X0, 192)
-            for j in (1, 2, 3):
-                self.put(pack, G_XZ + j - 1, (z, 1 - x, y), 64, 32, ((z + j) % 4, x, y, c))
+            self.along(pack, G_XZ, G_BACK + 1, (z, 1 - x, y), 32, 64)
             self.put(pack, G_DY, (z, 1 - x, y), 0, 96, yn)
             self.put(pack, G_C + 1, (z, 1 - x, y), 0, 192, cn)
             self.got(pack, G_Y0, 192)
-            for j in (1, 2, 3):
-                self.put(pack, G_YZ + j - 1, (z, x, 1 - y), 96, 32, ((z + j) % 4, x, y, c))
+            self.along(pack, G_YZ, G_BACK + 2, (z, x, 1 - y), 96, 64)
             self.put(pack, G_DX, (z, x, 1 - y), 96, 96, xn)
             self.put(pack, G_C + 2, (z, x, 1 - y), 0, 192, cn)
 
         @pl.when(k > 0)
         def _():
-            self.got(pack, G_XZ + k - 1, 32)
-            self.got(pack, G_XA + k - 1, 64)
+            zz = on_chain(z, k)
+            across_x, across_y = (zz, 1 - x, y), (zz, x, 1 - y)
+            self.got(pack, G_XZ + zz, 64)
+            self.further(pack, G_XZ, across_x, 32, 64)
+            self.got(pack, G_YZ + zz, 64)
+            self.further(pack, G_YZ, across_y, 96, 64)
+            self.got(pack, G_XA + k - 1, 32)
             self.put(pack, G_DY + k, across_x, 0, 96, yn)
-            self.got(pack, G_YZ + k - 1, 32)
-            self.got(pack, G_YA + k - 1, 64)
+            self.got(pack, G_YA + k - 1, 32)
             self.put(pack, G_DX + k, across_y, 96, 96, xn)
             self.got(pack, G_XB + k - 1, 96)
             self.put(pack, G_C + 4 * k + 1, across_x, 0, 192, cn)
@@ -462,10 +485,14 @@
 
     def third(self, pack, k):
         z, x, y, c = self.z, self.x, self.y, self.c
-        zz = (z - k + 4) % 4
         self.got(pack, G_DY + k, 96)
         self.got(pack, G_DX + k, 96)
-        self.put(pack, G_C + 4 * k + 3, (zz, 1 - x, 1 - y), 0, 192, (z, x, y, 1 - c))
+
+        def on(zz):
+            self.put(pack, G_C + 4 * k + 3, (zz, 1 - x, 1 - y), 0, 192, (z, x, y, 1 - c))
+
+        pl.when(k == 0)(lambda: on(z))
+        pl.when(k > 0)(lambda: on(on_chain(z, k)))
 
     def step(self, s):
         total = 4 * self.packs
@@ -475,18 +502,34 @@
             self.first(s // 4, s % 4)
             pl.when((s % 4 == 3) & (s + 1 < total))(lambda: self.launch(s // 4 + 1))
 
-        pl.when((s >= 1) & (s <= total))(lambda: self.second((s + 3) // 4 - 1, (s + 3) % 4))
-        pl.when((s >= 2) & (s <= total + 1))(lambda: self.third((s + 2) // 4 - 1, (s + 2) % 4))
+        pl.when((s >= 2) & (s <= total + 1))(lambda: self.second((s + 2) // 4 - 1, (s + 2) % 4))
+        pl.when((s >= 4) & (s <= total + 3))(lambda: self.third(s // 4 - 1, s % 4))
 
     def arrived(self, pack):
         for slot in range(G_C, G_C + 16):
             self.got(pack, slot, 192)
 
     def finish(self):
+        z = self.z
+
+        def sent(pack, slot, count):
+            self.some(pack, slot, count).wait_send()
+
         def one(pack, carry):
-            for slot in range(G_COUNT):
-                self.some(pack, slot, G_ROWS[slot]).wait_send()
+            for slot, count in ((G_X0, 192), (G_Y0, 192)):
+                sent(pack, slot, count)
+            for base, n, count in (
+                (G_DY, 4, 96), (G_DX, 4, 96), (G_XA, 3, 32), (G_XB, 3, 96), (G_YA, 3, 32), (G_YB, 3, 96), (G_C, 16, 192),
+            ):
+                for i in range(n):
+                    sent(pack, base + i, count)
+            for i, (base, count) in enumerate(((G_Z, 192), (G_XZ, 64), (G_YZ, 64))):
+                pl.when(z > 0)(lambda: sent(pack, G_BACK + i, count))
+                for zz in range(4):
+                    pl.when((zz <= z) & (z < 3))(lambda: sent(pack, base + zz, count))
+                    pl.when((zz > z) & (z > 0))(lambda: sent(pack, base + zz, count))
             return carry
+
         lax.fori_loop(0, self.packs, one, 0)
 
 
@@ -498,11 +541,17 @@
 
 
 def add_rows(into, what, count):
+    size = 96 if count % 96 == 0 else count
+
     def one(t, carry):
-        r = pl.ds(pl.multiple_of(t * TILE, TILE), TILE)
-        into[r] = (into[r].astype(jnp.float32) + what[r].astype(jnp.float32)).astype(into.dtype)
+        r = pl.ds(pl.multiple_of(t * size, 32), size)
+        into[r] = into[r] + what[r]
         return carry
-    lax.fori_loop(0, count // TILE, one, 0)
+
+    if count == size:
+        into[...] = into[...] + what[...]
+    else:
+        lax.fori_loop(0, count // size, one, 0)
 
 
 class Scatter:
@@ -510,7 +559,7 @@
         self.stage, self.out_sem = stage, out_sem
         self.part, self.out, self.mine = part, out, mine
         self.buf_c, self.buf_v, self.buf_u, self.buf_zc, self.buf_z, self.buf_f = buf_c, buf_v, buf_u, buf_zc, buf_z, buf_f
-        self.send, self.recv, self.load, self.credit, self.packs = send, recv, load, credit, packs
+        self.send, self.recv, self.load_sem, self.credit, self.packs = send, recv, load, credit, packs
         self.z, self.x, self.y, self.c = place()
         z, x, y, c = place()
         self.xn, self.yn, self.cn = (z, 1 - x, y, c), (z, x, 1 - y, c), (z, x, y, 1 - c)
@@ -546,24 +595,40 @@
         par = pack % 2
         return [
             pltpu.make_async_copy(
-                self.part.at[yy * 2 + self.c, :, lanes_of(self.lane_pack(pack))], self.mine.at[par, yy], self.load.at[yy]
+                self.part.at[yy * 2 + self.c, :, lanes_of(self.lane_pack(pack))], self.mine.at[par, yy], self.load_sem.at[yy]
             )
             for yy in range(2)
         ]
 
-    def launch(self, pack):
+    def ahead(self, s):
+        pack = s // 4
+        k = (s % 4 + 1) % 4
         par = pack % 2
-        pl.when(pack >= 2)(lambda: pl.semaphore_wait(self.credit.at[pack - 2], 6))
+        if not isinstance(s, int):
+            pl.when((pack >= 2) & (s % 4 == 0))(lambda: pl.semaphore_wait(self.credit.at[pack - 2, 0], 1))
+        for i, (zz, xx, yy) in enumerate(self.shards(k)):
+            rows = rows_of(zz, xx, 0, 192)
+            slot = R_C + 4 * k + i
+            if not isinstance(s, int):
+                pl.when(pack >= 2)(lambda: self.some(par, slot, 192).wait_send())
+            self.put(
+                par, slot,
+                self.part.at[yy * 2 + 1 - self.c, rows, lanes_of(self.lane_pack(pack))],
+                self.buf_c.at[par, yy, rows], self.cn,
+            )
+
+    def launch(self):
+        self.ahead(0)
+        self.ahead(1)
+        self.load(0)
+
+    def load(self, pack):
         for r in self.loads(pack):
             r.start()
-        for k in ORDER:
-            for i, (zz, xx, yy) in enumerate(self.shards(k)):
-                rows = rows_of(zz, xx, 0, 192)
-                self.put(
-                    par, R_C + 4 * k + i,
-                    self.part.at[yy * 2 + 1 - self.c, rows, lanes_of(self.lane_pack(pack))],
-                    self.buf_c.at[par, yy, rows], self.cn,
-                )
+
+    def sent(self, pack, first, last):
+        for slot in range(first, last):
+            self.some(pack % 2, slot, R_ROWS[slot]).wait_send()
 
     def core(self, pack, k):
         par = pack % 2
@@ -573,15 +638,22 @@
         def _():
             for r in self.loads(pack):
                 r.wait()
+            pl.when(pack >= 2)(lambda: pl.semaphore_wait(self.credit.at[pack - 2, 1], 5))
 
         for i, (zz, xx, yy) in enumerate(sh):
             self.got(par, R_C + 4 * k + i, 192)
             add_rows(self.at(par, sh[i], 0, 192), self.buf_c.at[par, yy, rows_of(zz, xx, 0, 192)], 192)
+        pl.when((k == ORDER[3]) & (pack + 2 < self.packs))(lambda: self.free(pack, 0, self.cn))
         v = self.buf_v
         self.put(par, R_V + 4 * k, self.at(par, sh[0], 0, 96), v.at[par, k, 0], self.yn)
         self.put(par, R_V + 4 * k + 1, self.at(par, sh[0], 96, 96), v.at[par, k, 1], self.xn)
         self.put(par, R_V + 4 * k + 2, self.at(par, sh[1], 0, 96), v.at[par, k, 2], self.yn)
         self.put(par, R_V + 4 * k + 3, self.at(par, sh[2], 96, 96), v.at[par, k, 3], self.xn)
+
+    def free(self, pack, kind, target):
+        pl.semaphore_signal(
+            self.credit.at[pack, kind], inc=1, device_id=device(*target), device_id_type=MESH_ID
+        )
 
     def vees(self, pack, k):
         par = pack % 2
@@ -659,35 +731,44 @@
                 return carry
             lax.fori_loop(0, 96 // TILE, one, 0)
         self.out_copy(pack).start()
-        for slot in range(R_COUNT):
-            self.some(par, slot, R_ROWS[slot]).wait_send()
+        self.sent(pack, R_V, R_COUNT)
 
         @pl.when(pack + 2 < self.packs)
         def _():
             z, x, y, c = self.z, self.x, self.y, self.c
-            for t in (self.xn, self.yn, self.cn) + tuple(((z + k) % 4, x, y, c) for k in (1, 2, 3)):
-                pl.semaphore_signal(self.credit.at[pack], inc=1, device_id=device(*t), device_id_type=MESH_ID)
+            for t in (self.xn, self.yn) + tuple(((z + k) % 4, x, y, c) for k in (1, 2, 3)):
+                self.free(pack, 1, t)
 
     def step(self, s):
         total = 4 * self.packs
         pl.when(s < total)(lambda: self.core(s // 4, (s % 4 + 1) % 4))
 
-        @pl.when((s >= 1) & (s <= total))
-        def _():
-            self.vees((s + 3) // 4 - 1, s % 4)
-
         @pl.when((s >= 2) & (s <= total + 1))
         def _():
             before = (s + 2) // 4 - 1
             k = (s + 3) % 4
+            self.vees(before, k)
+            pl.when(k == 0)(lambda: self.near(before))
+
+        @pl.when((s >= 4) & (s <= total + 3))
+        def _():
+            before = s // 4 - 1
+            k = (s % 4 + 1) % 4
             pl.when(k > 0)(lambda: self.yous(before, k))
             pl.when(k == 0)(lambda: self.final(before))
 
-        pl.when((s >= 4) & (s % 4 == 0))(lambda: self.near(s // 4 - 1))
-        pl.when((s % 4 == 2) & (s // 4 + 1 < self.packs))(lambda: self.launch(s // 4 + 1))
+        more = s + 2
+        if not isinstance(s, int):
+            pl.when(more < total)(lambda: self.ahead(more))
+        elif more < total:
+            self.ahead(jnp.int32(more))
+        later = s // 4 + 1
+        pl.when((s % 4 == 3) & (later < self.packs))(lambda: self.load(later))
 
     def finish(self):
         self.out_copy(self.packs - 1).wait()
+        for pack in (self.packs - 2, self.packs - 1):
+            self.sent(pack, R_C, R_V)
 
 
 def scatter_scratch(packs):
@@ -703,7 +784,7 @@
         pltpu.SemaphoreType.DMA((2, R_COUNT)),
         pltpu.SemaphoreType.DMA((2, R_COUNT)),
         pltpu.SemaphoreType.DMA((2,)),
-        pltpu.SemaphoreType.REGULAR((packs,)),
+        pltpu.SemaphoreType.REGULAR((packs, 2)),
         pltpu.VMEM((ROWS, LANES), jnp.float32),
         pltpu.SemaphoreType.DMA,
     ]
@@ -747,6 +828,14 @@
     loop(tokens // 32, one)
 
 
+def turn(src, into, tokens):
+    def one(t):
+        r = tile_rows(t, 128)
+        into[:, r] = jnp.transpose(src[r])
+
+    loop(tokens // 128, one)
+
+
 def gelu_parts(u):
     root = 0.7978845608028654
     t = jnp.tanh(root * (u + 0.044715 * (u * u * u)))
@@ -769,7 +858,7 @@
     packs, tokens, width, seq, heads, scale,
     own, tile, x_any, teacher_any, cotangent_any, buckets, bias_smem, blocks_row, blocks_col, valid_row, valid_col,
     whole, table, n1_out, n2_out, qkv_out, probs_out, pre_out, act_out, middle_out, layer_out, grad_out, gffn_out, loss_out,
-    x, n1, n2, acc, bias, mask, wbuf, qs, ps, pre, act, tabv, gain1, gain2, teach, cot, lossv,
+    x, n1, n2, turned, acc, bias, mask, wbuf, qs, ps, pre, act, tabv, gain1, gain2, teach, cot, lossv,
     send, recv, local, tile_send, tile_recv, tile_local, in_sem, w_sem, p_sem, q_sem, pre_sem, act_sem, out_sem,
 ):
     f = lax.axis_index("fsdp")
@@ -819,7 +908,7 @@
         for h in range(heads):
             bias[h, r] = totals[h]
 
-    step_tiles = -(-(seq // 8) // 5)
+    step_tiles = -(-(seq // 8) // 7)
 
     def early(s):
         def some(i):
@@ -829,7 +918,7 @@
         loop(step_tiles, some)
         g.step(s + 1)
 
-    loop(5, early)
+    loop(7, early)
     tile_keep.wait()
     tiles.wait()
     load_table = pltpu.make_async_copy(table, tabv, in_sem.at[1])
@@ -849,7 +938,8 @@
         acc[r] = x[r].astype(F32)
 
     loop(tokens // 32, copy_x)
-    n1_copy = pltpu.make_async_copy(n1, n1_out, out_sem.at[0])
+    turn(n1, turned, tokens)
+    n1_copy = pltpu.make_async_copy(turned, n1_out, out_sem.at[0])
     n1_copy.start()
     for r in keep:
         r.wait()
@@ -871,7 +961,7 @@
         load_w(dd, slot).wait()
         pl.when(dd > 0)(lambda: pltpu.make_async_copy(qs, qkv_out.at[dd], q_sem).wait())
         qs[:, 0:576] = nn(n1[...], wbuf[slot, :, 0:576]).astype(BF)
-        g.step(6 + 2 * dd)
+        g.step(8 + 2 * dd)
         for m in range(micro):
             r = slice(m * seq, (m + 1) * seq)
             pl.when(dd > 0)(lambda: probs_copy(dd, m, m).wait())
@@ -885,7 +975,7 @@
                 ps[m, hh] = p
                 qs[r, 576 + a : 576 + a + size] = nn(p.astype(BF), qs[r, 384 + a : 384 + a + size]).astype(BF)
             probs_copy(dd, m, m).start()
-        g.step(7 + 2 * dd)
+        g.step(9 + 2 * dd)
         for m in range(micro):
             r = slice(m * seq, (m + 1) * seq)
             acc[r] += nt(qs[r, 576:768], wbuf[slot, :, 576:768])
@@ -898,7 +988,9 @@
     mid_copy = pltpu.make_async_copy(acc, middle_out, out_sem.at[1])
     mid_copy.start()
     norm_rows(acc, gain2, n2, tokens)
-    n2_copy = pltpu.make_async_copy(n2, n2_out, out_sem.at[2])
+    n1_copy.wait()
+    turn(n2, turned, tokens)
+    n2_copy = pltpu.make_async_copy(turned, n2_out, out_sem.at[2])
     n2_copy.start()
     mid_copy.wait()
 
@@ -935,9 +1027,9 @@
 
         @pl.when(t < 8)
         def _():
-            pl.when(t % 2 == 0)(lambda: g.step(14 + t // 2))
-
-        pl.when((t >= 8) & (t < 12))(lambda: g.step(10 + t))
+            pl.when(t % 2 == 1)(lambda: g.step(16 + t // 2))
+
+        pl.when((t >= 8) & (t < 12))(lambda: g.step(12 + t))
         for m in range(micro):
             r = slice(m * seq, (m + 1) * seq)
             acc[r] += nt(act[slot, r], wbuf[slot, :, 2 * CHUNK :])
@@ -945,7 +1037,6 @@
     loop(16, feed)
     load_t.wait()
     load_c.wait()
-    n1_copy.wait()
     n2_copy.wait()
     for slot in range(2):
         pre_copy(14 + slot, slot).wait()
@@ -993,7 +1084,7 @@
     S = jax.ShapeDtypeStruct
     dma = pltpu.SemaphoreType.DMA
     outs = (
-        S((4, 8 * ROWS, own.shape[1]), BF), S((32, 8, 128), F32), S((tokens, width), BF), S((tokens, width), BF),
+        S((4, 8 * ROWS, own.shape[1]), BF), S((32, 8, 128), F32), S((width, tokens), BF), S((width, tokens), BF),
         S((4, tokens, 768), BF), S((4 * micro, heads // 4, seq, seq), F32), S((16, tokens, 2 * CHUNK), F32),
         S((16, tokens, CHUNK), BF), S((tokens, width), F32), S((tokens, width), BF), S((tokens, width), F32), S((tokens, width), BF), S((8, 128), F32),
     )
@@ -1004,7 +1095,7 @@
         out_specs=[any_] * 12 + [vmem],
         scratch_shapes=[
             pltpu.VMEM((tokens, width), BF), pltpu.VMEM((tokens, width), BF), pltpu.VMEM((tokens, width), BF),
-            pltpu.VMEM((tokens, width), F32), pltpu.VMEM((heads, seq, seq), F32), pltpu.VMEM((micro, seq, seq), F32),
+            pltpu.VMEM((width, tokens), BF), pltpu.VMEM((tokens, width), F32), pltpu.VMEM((heads, seq, seq), F32), pltpu.VMEM((micro, seq, seq), F32),
             pltpu.VMEM((2, 8 * ROWS, LANES), BF), pltpu.VMEM((tokens, 768), BF), pltpu.VMEM((micro, heads // 4, seq, seq), F32),
             pltpu.VMEM((2, tokens, 2 * CHUNK), F32), pltpu.VMEM((2, tokens, CHUNK), BF), pltpu.VMEM((32, 8, 128), F32),
             pltpu.VMEM((1, width), F32), pltpu.VMEM((1, width), F32), pltpu.VMEM((tokens, width), BF),
@@ -1054,15 +1145,15 @@
 def backward_kernel(
     packs, tokens, width, seq, heads,
     whole, table, x_any, n1_any, n2_any, qkv_any, probs_any, pre_any, act_any, mid_any, gout_any, gffn_any, buckets, loss,
-    part, out, hidden_out, tiles_out, sums_out,
+    part, out, hidden_out, tiles_out, sums_out, gs_out,
     low, src, acc, acc2, wbuf, pre, act, ggu, gst, strm, qs, ps, ga, gqkv, bsum, gain1, gain2, sum1, sum2, tilev, tabv,
-    in_sem, w_sem, pre_sem, act_sem, g_sem, s_sem, q_sem, p_sem, out2_sem, tile_send, tile_recv, tile_local, *scatter_refs,
+    in_sem, w_sem, pre_sem, act_sem, g_sem, s_sem, q_sem, p_sem, out2_sem, gs_sem, tile_send, tile_recv, tile_local, *scatter_refs,
 ):
     micro = tokens // seq
     per = heads // 4
     size = 192 // per
     me = lax.axis_index("fsdp") * 4 + lax.axis_index("dp")
-    start_barrier()
+    tell_all()
     rs = Scatter(part, out, *scatter_refs, packs)
 
     def fetch(a, b, sem):
@@ -1070,6 +1161,7 @@
         r.start()
         return r
 
+    mid_load = fetch(mid_any, acc2, in_sem.at[3])
     loads = [fetch(gffn_any, low, in_sem.at[0]), fetch(n2_any, src, in_sem.at[1]), fetch(table, tabv, in_sem.at[2])]
 
     def load_w(i, slot):
@@ -1092,7 +1184,6 @@
     def clear(t):
         r = tile_rows(t, 32)
         acc[r] = jnp.zeros((32, width), F32)
-        acc2[r] = jnp.zeros((32, width), F32)
 
     loop(tokens // 32, clear)
     for r in loads:
@@ -1123,7 +1214,7 @@
         pl.when((t > 0) & (t != 4))(lambda: put_g(0, 0).wait())
         for h in range(2):
             c = slice(h * half, (h + 1) * half)
-            gst[c, 0 : 2 * CHUNK] = tn(src[:, c], ggu[...]).astype(BF)
+            gst[c, 0 : 2 * CHUNK] = nn(src[c], ggu[...]).astype(BF)
             gst[c, 2 * CHUNK :] = tn(low[:, c], act[slot]).astype(BF)
         put_g(t % 4, 1 + t // 4).start()
         for m in range(micro):
@@ -1133,9 +1224,11 @@
         @pl.when(t == 3)
         def _():
             put_g(0, 0).wait()
-            rs.launch(0)
-
-        pl.when((t > 3) & (t % 2 == 1))(lambda: rs.step(t // 2 - 2))
+            hear_all()
+            rs.launch()
+
+        pl.when((t == 4) | (t == 6))(lambda: rs.step(t // 2 - 2))
+        pl.when(t >= 8)(lambda: rs.step(t - 6))
 
     loop(16, feed)
     put_g(0, 0).wait()
@@ -1143,49 +1236,58 @@
     load_w(0, 0).start()
 
     def strm_load(t, slot):
-        r = tile_rows(t, 32)
-        return [
-            pltpu.make_async_copy(mid_any.at[r], strm.at[slot, 0], s_sem.at[slot, 0]),
-            pltpu.make_async_copy(gout_any.at[r], strm.at[slot, 1], s_sem.at[slot, 1]),
-        ]
-
-    for r in strm_load(0, 0):
-        r.start()
-
-    def norm_two(t):
-        slot = t % 2
-
-        @pl.when(t + 1 < tokens // 32)
-        def _():
-            for r in strm_load(t + 1, 1 - slot):
-                r.start()
-
-        for r in strm_load(t, slot):
-            r.wait()
-        r = tile_rows(t, 32)
-        grad = strm[slot, 1] + norm_back(strm[slot, 0], acc[r], gain2[...], sum2)
-        acc[r] = grad
-        low[r] = grad.astype(BF)
-
-    loop(tokens // 32, norm_two)
-    n1_load.wait()
+        return pltpu.make_async_copy(gout_any.at[tile_rows(t, 128)], strm.at[slot], s_sem.at[slot])
 
     def probs_load(dd, m):
         return pltpu.make_async_copy(probs_any.at[dd * micro + m], ps.at[m], p_sem.at[m])
 
+    def q_load(dd):
+        return pltpu.make_async_copy(qkv_any.at[dd], qs, q_sem)
+
+    strm_load(0, 0).start()
+    q_load(0).start()
+    for m in range(micro):
+        probs_load(0, m).start()
+    mid_load.wait()
+
+    def norm_two(block):
+        slot = block % 2
+        pl.when(block + 1 < tokens // 128)(lambda: strm_load(block + 1, 1 - slot).start())
+        strm_load(block, slot).wait()
+
+        def some(t):
+            r = tile_rows(block * 4 + t, 32)
+            grad = strm[slot, tile_rows(t, 32)] + norm_back(acc2[r], acc[r], gain2[...], sum2)
+            acc[r] = grad
+            acc2[r] = jnp.zeros((32, width), F32)
+            low[r] = grad.astype(BF)
+
+        loop(4, some)
+
+    loop(tokens // 128, norm_two)
+    n1_load.wait()
+    rs.step(10)
+
+    def gs_copy(dd):
+        return pltpu.make_async_copy(ps.at[micro - 1], gs_out.at[dd], gs_sem.at[0])
+
+    def gs_load(dd):
+        return pltpu.make_async_copy(gs_out.at[dd], ps.at[dd % 2], gs_sem.at[dd % 2])
+
     def attention(dd):
         slot = dd % 2
-        q_load = pltpu.make_async_copy(qkv_any.at[dd], qs, q_sem)
-        q_load.start()
-        for m in range(micro):
-            probs_load(dd, m).start()
         pl.when(dd < 3)(lambda: load_w(dd + 1, 1 - slot).start())
         load_w(dd, slot).wait()
         ga[...] = nn(low[...], wbuf[slot, :, 576:768]).astype(BF)
-        q_load.wait()
-        pl.when(dd > 0)(lambda: put_g(0, 0).wait())
+        q_load(dd).wait()
+
+        @pl.when(dd > 0)
+        def _():
+            gs_copy(dd).wait()
+            probs_load(dd, micro - 1).start()
+            put_g(0, 0).wait()
+
         gst[:, 576:768] = tn(low[...], qs[:, 576:768]).astype(BF)
-        rs.step(6 + 2 * dd)
         for m in range(micro):
             r = slice(m * seq, (m + 1) * seq)
             probs_load(dd, m).wait()
@@ -1199,47 +1301,65 @@
                 gqkv[r, a : a + size] = nn(gs, qs[r, 192 + a : 192 + a + size]).astype(BF)
                 gqkv[r, 192 + a : 192 + a + size] = tn(gs, qs[r, a : a + size]).astype(BF)
                 gqkv[r, 384 + a : 384 + a + size] = tn(p.astype(BF), go).astype(BF)
-                if m == 0:
-                    ps[0, hh] = gs.astype(F32)
-                else:
-                    ps[0, hh] += gs.astype(F32)
-        rs.step(7 + 2 * dd)
+                ps[m, hh] = gs.astype(F32) if m == 0 else ps[m - 1, hh] + gs.astype(F32)
+        gs_copy(dd).start()
+
+        @pl.when(dd < 3)
+        def _():
+            q_load(dd + 1).start()
+            probs_load(dd + 1, 0).start()
+
+        pl.when(dd < 3)(lambda: rs.step(11 + dd))
         for h in range(2):
             c = slice(h * half, (h + 1) * half)
-            gst[c, 0:576] = tn(src[:, c], gqkv[...]).astype(BF)
+            gst[c, 0:576] = nn(src[c], gqkv[...]).astype(BF)
         put_g(dd, 0).start()
         for m in range(micro):
             r = slice(m * seq, (m + 1) * seq)
             acc2[r] += nt(gqkv[r], wbuf[slot, :, 0:576])
 
-        def by_bucket(i):
-            hh, group = i // 4, i % 4
-
+
+    loop(4, attention)
+    put_g(0, 0).wait()
+    gs_copy(0).wait()
+    rs.step(14)
+    gs_load(0).start()
+    x_load = fetch(x_any, low, in_sem.at[1])
+    x_load.wait()
+
+    def norm_one(t):
+        r = tile_rows(t, 32)
+        term = norm_back(low[r].astype(F32), acc2[r], gain1[...], sum1)
+        low[r] = (acc[r] + term).astype(BF)
+
+    loop(tokens // 32, norm_one)
+    hidden_copy = fetch(low, hidden_out, out2_sem)
+    rs.step(15)
+
+    def buckets_of(dd):
+        gs_load(dd).wait()
+        pl.when(dd < 3)(lambda: gs_load(dd + 1).start())
+
+        def by_bucket(group):
             def some(t, totals):
                 r = tile_rows(t, 8)
                 b = buckets[r]
-                v = ps[0, hh, r]
-                return tuple(o + jnp.where(b == group * 8 + j, v, 0.0) for j, o in enumerate(totals))
-
-            totals = lax.fori_loop(0, seq // 8, some, (jnp.zeros((8, seq), F32),) * 8)
-            lines = [jnp.sum(o, axis=0, keepdims=True) for o in totals]
-            bsum[dd * per + hh, pl.ds(pl.multiple_of(group * 8, 8), 8)] = jnp.concatenate(lines, axis=0)
-
-        loop(4 * per, by_bucket)
-
-    loop(4, attention)
-    put_g(0, 0).wait()
-    rs.step(14)
-    x_load = fetch(x_any, src, in_sem.at[1])
-    x_load.wait()
-
-    def norm_one(t):
-        r = tile_rows(t, 32)
-        term = norm_back(src[r].astype(F32), acc2[r], gain1[...], sum1)
-        low[r] = (acc[r] + term).astype(BF)
-
-    loop(tokens // 32, norm_one)
-    hidden_copy = fetch(low, hidden_out, out2_sem)
+                v = [ps[dd % 2, hh, r] for hh in range(per)]
+                new = []
+                for j in range(4):
+                    here = b == group * 4 + j
+                    new += [totals[j * per + hh] + jnp.where(here, v[hh], 0.0) for hh in range(per)]
+                return tuple(new)
+
+            totals = lax.fori_loop(0, seq // 8, some, (jnp.zeros((8, seq), F32),) * (4 * per))
+            for j in range(4):
+                for hh in range(per):
+                    bsum[dd * per + hh, pl.ds(group * 4 + j, 1)] = jnp.sum(totals[j * per + hh], axis=0, keepdims=True)
+
+        loop(8, by_bucket)
+        rs.step(16 + dd)
+
+    loop(4, buckets_of)
     one = jnp.sum(sum1[...], axis=0, keepdims=True)
     two = jnp.sum(sum2[...], axis=0, keepdims=True)
     biases = lax.dot_general(
@@ -1256,11 +1376,10 @@
             rows.append(v[:, first + 128 : first + 256] if first + 128 < width else none)
         tilev[i] = jnp.concatenate(rows + [loss[0:1, :]] + lines, axis=0)
     tile_copy = fetch(tilev, tiles_out, in_sem.at[0])
-    rs.step(15)
     tile_copy.wait()
     tiles = exchange(lambda other: tiles_out.at[other], sums_out, tile_send, tile_recv)
     tile_keep = fetch(tilev.at[me], sums_out.at[me], tile_local)
-    lax.fori_loop(16, 4 * packs + 2, lambda s, carry: (rs.step(s), carry)[1], 0)
+    lax.fori_loop(20, 4 * packs + 4, lambda s, carry: (rs.step(s), carry)[1], 0)
     rs.finish()
     hidden_copy.wait()
     tile_keep.wait()
@@ -1279,19 +1398,20 @@
     dma = pltpu.SemaphoreType.DMA
     outs = (
         S(whole.shape, BF), S((ROWS, whole.shape[2]), F32), S((tokens, width), BF), S((32, 8, 128), F32), S((32, 8, 128), F32),
+        S((4, heads // 4, seq, seq), F32),
     )
     return pl.pallas_call(
         functools.partial(backward_kernel, packs, tokens, width, seq, heads),
         out_shape=outs,
         in_specs=[any_] * 12 + [vmem] * 2,
-        out_specs=[any_] * 5,
+        out_specs=[any_] * 6,
         scratch_shapes=[
-            V((tokens, width), BF), V((tokens, width), BF), V((tokens, width), F32), V((tokens, width), F32),
+            V((tokens, width), BF), V((width, tokens), BF), V((tokens, width), F32), V((tokens, width), F32),
             V((2, 8 * ROWS, LANES), BF), V((2, tokens, 2 * CHUNK), F32), V((2, tokens, CHUNK), BF), V((tokens, 2 * CHUNK), BF),
-            V((8 * ROWS, LANES), BF), V((2, 2, 32, width), F32), V((tokens, 768), BF), V((micro, heads // 4, seq, seq), F32),
+            V((8 * ROWS, LANES), BF), V((2, 128, width), F32), V((tokens, 768), BF), V((micro, heads // 4, seq, seq), F32),
             V((tokens, 192), BF), V((tokens, 576), BF), V((heads, 32, seq), F32), V((1, width), F32), V((1, width), F32),
             V((8, width), F32), V((8, width), F32), V((32, 8, 128), F32), V((32, 8, 128), F32),
-            dma((3,)), dma((2,)), dma((2,)), dma((2,)), dma, dma((2, 2)), dma, dma((micro,)), dma, dma, dma, dma,
+            dma((4,)), dma((2,)), dma((2,)), dma((2,)), dma, dma((2,)), dma, dma((micro,)), dma, dma((2,)), dma, dma, dma,
         ] + scatter_scratch(packs),
         compiler_params=pltpu.CompilerParams(collective_id=2, has_side_effects=True, vmem_limit_bytes=67043328),
     )(whole, table, x, n1, n2, qkv, probs, pre, act, mid, gout, gffn, buckets, loss)
@@ -1317,7 +1437,7 @@
         own, tile, x, teacher.reshape(tokens, width), cotangent.reshape(tokens, width), buckets, bias_table.astype(F32),
         block_ids, block_ids.reshape(tokens, 1), valid, valid.reshape(tokens, 1).astype(F32), scale,
     )
-    _, shard, hidden_grad, _, sums = backward(
+    _, shard, hidden_grad, _, sums, _ = backward(
         whole, table, x, n1, n2, qkv, probs, pre, act, mid, gout, gffn, buckets, loss, heads
     )
     sums = jnp.sum(sums, axis=0)

time: 557 us -> 497 us (0.89)
  Pallas kernels: 526 us -> 463 us
    pallas_call x1, Pallas kernels: 300 us -> 250 us  [backward(): pl.pallas_call(functools.partial(backward_kernel, packs, tokens, width, s...]
    pallas_call x1, Pallas kernels: 226 us -> 214 us  [forward(): pl.pallas_call(functools.partial(forward_kernel, packs, tokens, width, se...]
where the time goes in v3:
time: 497 us; the launch traced here: 492 us
  Pallas kernels  463 us (93%)
  local copies, waits for them, and re-layouts  18.7 us (4%)
  other arithmetic  6.84 us (1%)
    pallas_call x1, Pallas kernels, backward(): pl.pallas_call(functools.partial(backward_kernel, packs, tokens, width, s...  250 us
    pallas_call x1, Pallas kernels, forward(): pl.pallas_call(functools.partial(forward_kernel, packs, tokens, width, se...  214 us

profile of v3, /device:TPU:0, one launch (start us, length us, event | category | flops | bytes accessed | tf_op | source)
XLA Modules:
  0.0 492.2 jit_solution(16512075834345316568)
XLA Ops:
  0.6 0.0 copy-start.2
  0.7 0.0 copy-start.3
  0.7 0.0 copy-start.4
  0.7 1.2 pad_slice_fusion.2
  2.0 1.3 pad_slice_fusion
  3.3 1.9 concatenate.15.own
  5.2 0.1 convert_dynamic-update-slice_fusion
  5.3 0.1 convert_dynamic-update-slice_fusion.1
  5.4 0.6 convert_reduce_fusion
  6.0 0.6 add.27
  6.6 0.1 pad.27.clone
  6.7 0.7 maximum_maximum_fusion.tile
  7.4 0.7 copy.37.bias_smem
  8.1 0.6 copy_bitcast_fusion
  8.7 0.9 copy.38.blocks_col
  9.6 0.9 copy.39.valid_col
  10.6 213.8 %shard_map.255 = (bf16[4,1536,3840]{2,1,0:T(8,128)(2,1)}, f32[32,8,128]{2,1,0:T(8,128)}, bf16[1536,768]{1,0:T(8,128)(2,1)}, bf16[1536,768]{1,0:T(8,128)(2,1)}, b...) custom-call(bf16[192,3840]{1,0:T(8,128)(2,1)} %concatenate.15.own, ...), custom_call_target="tpu_custom_call" | custom-call | tf_op jit(solution)/shard_map/pallas_call | solution.py:1091
  224.4 249.6 %shard_map.256 = (bf16[4,1536,3840]{2,1,0:T(8,128)(2,1)}, f32[192,3840]{1,0:T(8,128)}, bf16[768,1536]{1,0:T(8,128)(2,1)}, f32[32,8,128]{2,1,0:T(8,128)}, f32[32,...) custom-call(bf16[4,1536,3840]{2,1,0:T(8,128)(2,1)} %get-tuple-element.30.whole, f32[32,8,128]{2,1,0:T(8,128)} %get-tuple-element.31.table, ...), custom_call_target="tpu_custom_call" | custom-call | tf_op jit(solution)/shard_map/pallas_call | solution.py:1403
  474.0 0.9 reduce_sum.28
  474.9 0.5 slice.129
  475.4 1.5 slice_reduce_fusion
  478.3 0.6 dynamic_slice.6
  478.9 2.2 fusion.1
  481.1 0.6 dynamic_slice.7
  481.7 1.9 fusion
  483.5 1.0 pad_maximum_fusion.6
  484.5 1.0 pad_maximum_fusion.3
  485.5 1.0 pad_maximum_fusion
  486.5 0.7 reshape.86
  487.1 1.4 copy.53
  488.5 1.1 copy-done.1
  489.6 1.4 copy.54
  (23 shorter events, 0.1 us)
Async XLA Ops:
  0.6 2.6 copy-start.2
  0.7 2.6 copy-start.3
  0.7 2.6 copy-start.4
  0.7 2.6 copy-start.5
  0.7 4.5 copy-start.9
  0.7 4.6 copy-start.10
  0.7 4.7 copy-start.6
  0.7 6.7 %copy-start.8 = (bf16[32,12]{0,1:T(8,128)(2,1)S(1)}, bf16[32,12]{0,1:T(8,128)(2,1)}, u32[]{:S(2)}) copy-start(bf16[32,12]{0,1:T(8,128)(2,1)} %param.31) | copy-start | bytes 2308
  0.7 7.4 %copy-start.7 = (s32[2,1,384]{2,1,0:T(1,128)S(1)}, s32[2,1,384]{2,1,0:T(1,128)}, u32[]{:S(2)}) copy-start(s32[2,1,384]{2,1,0:T(1,128)} %param.20) | copy-start | bytes 9220
  483.5 3.6 copy-start
  487.1 2.5 copy-start.1

commit v4 on v3

--- a/solution.py
+++ b/solution.py
@@ -533,10 +533,10 @@
         lax.fori_loop(0, self.packs, one, 0)
 
 
-R_C, R_V, R_U, R_ZC, R_Z, R_F = 0, 16, 32, 38, 44, 47
-R_COUNT = 49
-R_ROWS = [192] * 16 + [96] * 16 + [64] * 6 + [32] * 6 + [192] * 3 + [96] * 2
-ORDER = (1, 2, 3, 0)
+R_C, R_V, R_U, R_ZC, R_Z, R_F = 0, 16, 32, 38, 48, 53
+R_COUNT = 55
+R_ROWS = [192] * 16 + [96] * 16 + [32] * 6 + [64] * 10 + [192] * 5 + [96] * 2
+ORDER = (3, 2, 1, 0)
 TILE = 32
 
 
@@ -587,8 +587,27 @@
     def lane_pack(self, pack):
         return (pack + 1) % self.packs
 
+    def dest(self, k):
+        if isinstance(k, int):
+            return self.z if k == 0 else on_chain(self.z, k)
+        none = (3 - k) // 3
+        return none * self.z + (1 - none) * on_chain(self.z, k)
+
+    def slot_to(self, zz):
+        apart = zz - self.z + 4
+        home = (apart // 3) * (1 - apart // 4)
+        return zz * (1 - home) + 4 * home
+
+    def onward(self, par, base, buf, j, zz, here):
+        z, x, y, c = self.z, self.x, self.y, self.c
+        slot = self.slot_to(zz)
+        there = buf.at[par, slot] if j is None else buf.at[par, slot, j]
+        number = base + (slot if j is None else 2 * slot + j)
+        pl.when(zz > z)(lambda: self.put(par, number, here, there, (z + 1, x, y, c)))
+        pl.when(zz < z)(lambda: self.put(par, number, here, there, (z - 1, x, y, c)))
+
     def shards(self, k):
-        zz = (self.z + k) % 4
+        zz = self.dest(k)
         return ((zz, 1 - self.x, 1 - self.y), (zz, self.x, 1 - self.y), (zz, 1 - self.x, self.y), (zz, self.x, self.y))
 
     def loads(self, pack):
@@ -602,7 +621,7 @@
 
     def ahead(self, s):
         pack = s // 4
-        k = (s % 4 + 1) % 4
+        k = 3 - s % 4
         par = pack % 2
         if not isinstance(s, int):
             pl.when((pack >= 2) & (s % 4 == 0))(lambda: pl.semaphore_wait(self.credit.at[pack - 2, 0], 1))
@@ -658,23 +677,24 @@
     def vees(self, pack, k):
         par = pack % 2
         sh = self.shards(k)
-        peer = ((self.z + k) % 4, self.x, self.y, self.c)
+        zz = self.dest(k)
+        end = (self.z == 0) | (self.z == 3)
         v = self.buf_v
         self.got(par, R_V + 4 * k, 96)
         add_rows(self.at(par, sh[2], 0, 96), v.at[par, k, 0], 96)
 
         @pl.when(k > 0)
         def _():
-            self.put(par, R_U + 2 * (k - 1), self.at(par, sh[2], 0, 64), self.buf_u.at[par, k - 1, 0], self.xn)
-            self.put(par, R_ZC + 2 * (k - 1), self.at(par, sh[2], 64, 32), self.buf_zc.at[par, k - 1, 0], peer)
+            self.put(par, R_U + 2 * (k - 1), self.at(par, sh[2], 0, 32), self.buf_u.at[par, k - 1, 0], self.xn)
+            pl.when(end)(lambda: self.onward(par, R_ZC, self.buf_zc, 0, zz, self.at(par, sh[2], 32, 64)))
 
         self.got(par, R_V + 4 * k + 1, 96)
         add_rows(self.at(par, sh[1], 96, 96), v.at[par, k, 1], 96)
 
         @pl.when(k > 0)
         def _():
-            self.put(par, R_U + 2 * (k - 1) + 1, self.at(par, sh[1], 128, 64), self.buf_u.at[par, k - 1, 1], self.yn)
-            self.put(par, R_ZC + 2 * (k - 1) + 1, self.at(par, sh[1], 96, 32), self.buf_zc.at[par, k - 1, 1], peer)
+            self.put(par, R_U + 2 * (k - 1) + 1, self.at(par, sh[1], 160, 32), self.buf_u.at[par, k - 1, 1], self.yn)
+            pl.when(end)(lambda: self.onward(par, R_ZC, self.buf_zc, 1, zz, self.at(par, sh[1], 96, 64)))
             self.got(par, R_V + 4 * k + 2, 96)
             add_rows(self.at(par, sh[3], 0, 96), v.at[par, k, 2], 96)
             self.got(par, R_V + 4 * k + 3, 96)
@@ -683,27 +703,50 @@
     def yous(self, pack, k):
         par = pack % 2
         sh = self.shards(k)
-        peer = ((self.z + k) % 4, self.x, self.y, self.c)
-        self.got(par, R_U + 2 * (k - 1), 64)
-        add_rows(self.at(par, sh[3], 0, 64), self.buf_u.at[par, k - 1, 0], 64)
-        self.got(par, R_U + 2 * (k - 1) + 1, 64)
-        add_rows(self.at(par, sh[3], 128, 64), self.buf_u.at[par, k - 1, 1], 64)
-        self.put(par, R_Z + k - 1, self.at(par, sh[3], 0, 192), self.buf_z.at[par, k - 1], peer)
+        zz = self.dest(k)
+        end = (self.z == 0) | (self.z == 3)
+
+        @pl.when((self.z > 0) & (self.z < 3))
+        def _():
+            for j, (shard, first) in enumerate(((sh[2], 32), (sh[1], 96))):
+                self.got(par, R_ZC + 2 * zz + j, 64)
+                add_rows(self.at(par, shard, first, 64), self.buf_zc.at[par, zz, j], 64)
+                self.onward(par, R_ZC, self.buf_zc, j, zz, self.at(par, shard, first, 64))
+
+        self.got(par, R_U + 2 * (k - 1), 32)
+        add_rows(self.at(par, sh[3], 0, 32), self.buf_u.at[par, k - 1, 0], 32)
+        self.got(par, R_U + 2 * (k - 1) + 1, 32)
+        add_rows(self.at(par, sh[3], 160, 32), self.buf_u.at[par, k - 1, 1], 32)
+        pl.when(end)(lambda: self.onward(par, R_Z, self.buf_z, None, zz, self.at(par, sh[3], 0, 192)))
+
+    def chain(self, pack, k):
+        par = pack % 2
+        sh = self.shards(k)
+        zz = self.dest(k)
+
+        @pl.when((self.z > 0) & (self.z < 3))
+        def _():
+            self.got(par, R_Z + zz, 192)
+            add_rows(self.at(par, sh[3], 0, 192), self.buf_z.at[par, zz], 192)
+            self.onward(par, R_Z, self.buf_z, None, zz, self.at(par, sh[3], 0, 192))
 
     def near(self, pack):
         par = pack % 2
         sh = self.shards(0)
-        for j, (shard, first, whole, nb) in enumerate(((sh[2], 64, 0, self.xn), (sh[1], 96, 96, self.yn))):
-            for k in range(3):
-                self.got(par, R_ZC + 2 * k + j, 32)
-            into = self.at(par, shard, first, 32)
-            b = self.buf_zc
-            into[...] = (
-                into[...].astype(jnp.float32)
-                + b[par, 0, j].astype(jnp.float32)
-                + b[par, 1, j].astype(jnp.float32)
-                + b[par, 2, j].astype(jnp.float32)
-            ).astype(into.dtype)
+        z = self.z
+        for j, (shard, first, whole, nb) in enumerate(((sh[2], 32, 0, self.xn), (sh[1], 96, 96, self.yn))):
+            into = self.at(par, shard, first, 64)
+
+            @pl.when(z > 0)
+            def _(j=j, into=into):
+                self.got(par, R_ZC + 2 * z + j, 64)
+                add_rows(into, self.buf_zc.at[par, z, j], 64)
+
+            @pl.when(z < 3)
+            def _(j=j, into=into):
+                self.got(par, R_ZC + 8 + j, 64)
+                add_rows(into, self.buf_zc.at[par, 4, j], 64)
+
             self.put(par, R_F + j, self.at(par, shard, whole, 96), self.buf_f.at[par, j], nb)
 
     def out_copy(self, pack):
@@ -714,10 +757,9 @@
         own = self.at(par, self.shards(0)[3], 0, 192)
         self.got(par, R_V + 2, 96)
         self.got(par, R_V + 3, 96)
-        for k in range(3):
-            self.got(par, R_Z + k, 192)
         for j in range(2):
             self.got(par, R_F + j, 96)
+
         pl.when(pack > 0)(lambda: self.out_copy(pack).wait())
         for j in range(2):
             def one(t, carry, j=j):
@@ -725,13 +767,29 @@
                 rr = pl.ds(pl.multiple_of(j * 96 + t * TILE, TILE), TILE)
                 total = own[rr].astype(jnp.float32) + self.buf_v[par, 0, 2 + j, r].astype(jnp.float32)
                 total = total + self.buf_f[par, j, r].astype(jnp.float32)
-                for k in range(3):
-                    total = total + self.buf_z[par, k, rr].astype(jnp.float32)
                 self.stage[rr] = total
                 return carry
             lax.fori_loop(0, 96 // TILE, one, 0)
+        def more(slot):
+            self.got(par, R_Z + slot, 192)
+
+            def one(t, carry):
+                rr = pl.ds(pl.multiple_of(t * TILE, TILE), TILE)
+                self.stage[rr] += self.buf_z[par, slot, rr].astype(jnp.float32)
+                return carry
+
+            lax.fori_loop(0, ROWS // TILE, one, 0)
+
+        pl.when(self.z > 0)(lambda: more(self.z))
+        pl.when(self.z < 3)(lambda: more(4))
         self.out_copy(pack).start()
-        self.sent(pack, R_V, R_COUNT)
+        self.sent(pack, R_V, R_ZC)
+        self.sent(pack, R_F, R_COUNT)
+        for k in (1, 2, 3):
+            slot = self.slot_to(self.dest(k))
+            self.some(par, R_Z + slot, 192).wait_send()
+            for j in range(2):
+                self.some(par, R_ZC + 2 * slot + j, 64).wait_send()
 
         @pl.when(pack + 2 < self.packs)
         def _():
@@ -741,26 +799,28 @@
 
     def step(self, s):
         total = 4 * self.packs
-        pl.when(s < total)(lambda: self.core(s // 4, (s % 4 + 1) % 4))
+        pl.when(s < total)(lambda: self.core(s // 4, 3 - s % 4))
+        pl.when((s >= 1) & (s <= total))(lambda: self.vees((s + 3) // 4 - 1, 3 - (s + 3) % 4))
 
         @pl.when((s >= 2) & (s <= total + 1))
         def _():
             before = (s + 2) // 4 - 1
-            k = (s + 3) % 4
-            self.vees(before, k)
+            k = 3 - (s + 2) % 4
+            pl.when(k > 0)(lambda: self.yous(before, k))
             pl.when(k == 0)(lambda: self.near(before))
 
-        @pl.when((s >= 4) & (s <= total + 3))
-        def _():
-            before = s // 4 - 1
-            k = (s % 4 + 1) % 4
-            pl.when(k > 0)(lambda: self.yous(before, k))
+        @pl.when((s >= 3) & (s <= total + 2))
+        def _():
+            before = (s + 1) // 4 - 1
+            k = 3 - (s + 1) % 4
+            pl.when(k > 0)(lambda: self.chain(before, k))
             pl.when(k == 0)(lambda: self.final(before))
 
         more = s + 2
+        due = (more < total - 4) | ((more >= total - 2) & (more < total))
         if not isinstance(s, int):
-            pl.when(more < total)(lambda: self.ahead(more))
-        elif more < total:
+            pl.when(due)(lambda: self.ahead(more))
+        elif due:
             self.ahead(jnp.int32(more))
         later = s // 4 + 1
         pl.when((s % 4 == 3) & (later < self.packs))(lambda: self.load(later))
@@ -777,9 +837,9 @@
         pltpu.VMEM((2, 2, 8 * ROWS, LANES), bf),
         pltpu.VMEM((2, 2, 8 * ROWS, LANES), bf),
         pltpu.VMEM((2, 4, 4, 96, LANES), bf),
-        pltpu.VMEM((2, 3, 2, 64, LANES), bf),
         pltpu.VMEM((2, 3, 2, 32, LANES), bf),
-        pltpu.VMEM((2, 3, 192, LANES), bf),
+        pltpu.VMEM((2, 5, 2, 64, LANES), bf),
+        pltpu.VMEM((2, 5, 192, LANES), bf),
         pltpu.VMEM((2, 2, 96, LANES), bf),
         pltpu.SemaphoreType.DMA((2, R_COUNT)),
         pltpu.SemaphoreType.DMA((2, R_COUNT)),
@@ -1146,7 +1206,7 @@
     packs, tokens, width, seq, heads,
     whole, table, x_any, n1_any, n2_any, qkv_any, probs_any, pre_any, act_any, mid_any, gout_any, gffn_any, buckets, loss,
     part, out, hidden_out, tiles_out, sums_out, gs_out,
-    low, src, acc, acc2, wbuf, pre, act, ggu, gst, strm, qs, ps, ga, gqkv, bsum, gain1, gain2, sum1, sum2, tilev, tabv,
+    low, src, acc, acc2, wbuf, pre, act, ggu, gst, qs, ps, gqkv, bsum, gain1, gain2, sum1, sum2, tilev,
     in_sem, w_sem, pre_sem, act_sem, g_sem, s_sem, q_sem, p_sem, out2_sem, gs_sem, tile_send, tile_recv, tile_local, *scatter_refs,
 ):
     micro = tokens // seq
@@ -1161,8 +1221,7 @@
         r.start()
         return r
 
-    mid_load = fetch(mid_any, acc2, in_sem.at[3])
-    loads = [fetch(gffn_any, low, in_sem.at[0]), fetch(n2_any, src, in_sem.at[1]), fetch(table, tabv, in_sem.at[2])]
+    loads = [fetch(gffn_any, low, in_sem.at[0]), fetch(n2_any, src, in_sem.at[1]), fetch(table, tilev, in_sem.at[2])]
 
     def load_w(i, slot):
         return pltpu.make_async_copy(whole.at[i % 4, :, lanes_of(i // 4)], wbuf.at[slot], w_sem.at[slot])
@@ -1177,6 +1236,21 @@
         return pltpu.make_async_copy(gst, part.at[dd, :, lanes_of(lane_pack)], g_sem)
 
     for r in (load_w(4, 0), load_pre(0, 0), load_act(0, 0)):
+        r.start()
+    mid_load = fetch(mid_any, acc2, in_sem.at[3])
+    wide = 2 * CHUNK
+    gout_loads = [
+        pltpu.make_async_copy(gout_any.at[:, pl.ds(i * wide, wide)], pre.at[i], s_sem.at[i]) for i in range(2)
+    ]
+    for m in range(micro):
+        rows = pl.ds(m * seq, seq)
+        gout_loads.append(pltpu.make_async_copy(gout_any.at[rows, pl.ds(2 * wide, seq)], ps.at[m, 0], s_sem.at[2 + 2 * m]))
+        gout_loads.append(
+            pltpu.make_async_copy(
+                gout_any.at[rows, pl.ds(2 * wide + seq, 128)], ps.at[m, 1, :, pl.ds(0, 128)], s_sem.at[3 + 2 * m]
+            )
+        )
+    for r in gout_loads[2:]:
         r.start()
     sum1[...] = jnp.zeros_like(sum1)
     sum2[...] = jnp.zeros_like(sum2)
@@ -1188,8 +1262,8 @@
     loop(tokens // 32, clear)
     for r in loads:
         r.wait()
-    gain_rows(tabv, 0, gain1)
-    gain_rows(tabv, 2, gain2)
+    gain_rows(tilev, 0, gain1)
+    gain_rows(tilev, 2, gain2)
     half = width // 2
 
     def feed(t):
@@ -1235,36 +1309,31 @@
     n1_load = fetch(n1_any, src, in_sem.at[1])
     load_w(0, 0).start()
 
-    def strm_load(t, slot):
-        return pltpu.make_async_copy(gout_any.at[tile_rows(t, 128)], strm.at[slot], s_sem.at[slot])
-
     def probs_load(dd, m):
         return pltpu.make_async_copy(probs_any.at[dd * micro + m], ps.at[m], p_sem.at[m])
 
     def q_load(dd):
         return pltpu.make_async_copy(qkv_any.at[dd], qs, q_sem)
 
-    strm_load(0, 0).start()
+    for r in gout_loads[:2]:
+        r.start()
     q_load(0).start()
+    mid_load.wait()
+    for r in gout_loads:
+        r.wait()
     for m in range(micro):
-        probs_load(0, m).start()
-    mid_load.wait()
-
-    def norm_two(block):
-        slot = block % 2
-        pl.when(block + 1 < tokens // 128)(lambda: strm_load(block + 1, 1 - slot).start())
-        strm_load(block, slot).wait()
-
-        def some(t):
-            r = tile_rows(block * 4 + t, 32)
-            grad = strm[slot, tile_rows(t, 32)] + norm_back(acc2[r], acc[r], gain2[...], sum2)
+
+        def norm_two(t, m=m):
+            r = tile_rows(m * (seq // 32) + t, 32)
+            h = tile_rows(t, 32)
+            gout = jnp.concatenate([pre[0, r], pre[1, r], ps[m, 0, h], ps[m, 1, h, 0:128]], axis=1)
+            grad = gout + norm_back(acc2[r], acc[r], gain2[...], sum2)
             acc[r] = grad
             acc2[r] = jnp.zeros((32, width), F32)
             low[r] = grad.astype(BF)
 
-        loop(4, some)
-
-    loop(tokens // 128, norm_two)
+        loop(seq // 32, norm_two)
+        probs_load(0, m).start()
     n1_load.wait()
     rs.step(10)
 
@@ -1278,7 +1347,7 @@
         slot = dd % 2
         pl.when(dd < 3)(lambda: load_w(dd + 1, 1 - slot).start())
         load_w(dd, slot).wait()
-        ga[...] = nn(low[...], wbuf[slot, :, 576:768]).astype(BF)
+        gqkv[:, 576:768] = nn(low[...], wbuf[slot, :, 576:768]).astype(BF)
         q_load(dd).wait()
 
         @pl.when(dd > 0)
@@ -1294,7 +1363,7 @@
             for hh in range(per):
                 a = hh * size
                 p = ps[m, hh]
-                go = ga[r, a : a + size]
+                go = gqkv[r, 576 + a : 576 + a + size]
                 gp = nt(go, qs[r, 384 + a : 384 + a + size])
                 gs = p * (gp - jnp.sum(p * gp, axis=-1, keepdims=True))
                 gs = gs.astype(BF)
@@ -1309,21 +1378,23 @@
             q_load(dd + 1).start()
             probs_load(dd + 1, 0).start()
 
-        pl.when(dd < 3)(lambda: rs.step(11 + dd))
+        rs.step(11 + dd)
         for h in range(2):
             c = slice(h * half, (h + 1) * half)
-            gst[c, 0:576] = nn(src[c], gqkv[...]).astype(BF)
+            gst[c, 0:576] = nn(src[c], gqkv[:, 0:576]).astype(BF)
         put_g(dd, 0).start()
         for m in range(micro):
             r = slice(m * seq, (m + 1) * seq)
-            acc2[r] += nt(gqkv[r], wbuf[slot, :, 0:576])
+            acc2[r] += nt(gqkv[r, 0:576], wbuf[slot, :, 0:576])
 
 
     loop(4, attention)
     put_g(0, 0).wait()
     gs_copy(0).wait()
-    rs.step(14)
+    rs.ahead(jnp.int32(4 * packs - 4))
+    rs.ahead(jnp.int32(4 * packs - 3))
     gs_load(0).start()
+    rs.step(15)
     x_load = fetch(x_any, low, in_sem.at[1])
     x_load.wait()
 
@@ -1334,7 +1405,7 @@
 
     loop(tokens // 32, norm_one)
     hidden_copy = fetch(low, hidden_out, out2_sem)
-    rs.step(15)
+    rs.step(16)
 
     def buckets_of(dd):
         gs_load(dd).wait()
@@ -1357,7 +1428,7 @@
                     bsum[dd * per + hh, pl.ds(group * 4 + j, 1)] = jnp.sum(totals[j * per + hh], axis=0, keepdims=True)
 
         loop(8, by_bucket)
-        rs.step(16 + dd)
+        rs.step(17 + dd)
 
     loop(4, buckets_of)
     one = jnp.sum(sum1[...], axis=0, keepdims=True)
@@ -1379,7 +1450,7 @@
     tile_copy.wait()
     tiles = exchange(lambda other: tiles_out.at[other], sums_out, tile_send, tile_recv)
     tile_keep = fetch(tilev.at[me], sums_out.at[me], tile_local)
-    lax.fori_loop(20, 4 * packs + 4, lambda s, carry: (rs.step(s), carry)[1], 0)
+    lax.fori_loop(21, 4 * packs + 4, lambda s, carry: (rs.step(s), carry)[1], 0)
     rs.finish()
     hidden_copy.wait()
     tile_keep.wait()
@@ -1408,10 +1479,10 @@
         scratch_shapes=[
             V((tokens, width), BF), V((width, tokens), BF), V((tokens, width), F32), V((tokens, width), F32),
             V((2, 8 * ROWS, LANES), BF), V((2, tokens, 2 * CHUNK), F32), V((2, tokens, CHUNK), BF), V((tokens, 2 * CHUNK), BF),
-            V((8 * ROWS, LANES), BF), V((2, 128, width), F32), V((tokens, 768), BF), V((micro, heads // 4, seq, seq), F32),
-            V((tokens, 192), BF), V((tokens, 576), BF), V((heads, 32, seq), F32), V((1, width), F32), V((1, width), F32),
-            V((8, width), F32), V((8, width), F32), V((32, 8, 128), F32), V((32, 8, 128), F32),
-            dma((4,)), dma((2,)), dma((2,)), dma((2,)), dma, dma((2,)), dma, dma((micro,)), dma, dma((2,)), dma, dma, dma,
+            V((8 * ROWS, LANES), BF), V((tokens, 768), BF), V((micro, heads // 4, seq, seq), F32),
+            V((tokens, 768), BF), V((heads, 32, seq), F32), V((1, width), F32), V((1, width), F32),
+            V((8, width), F32), V((8, width), F32), V((32, 8, 128), F32),
+            dma((4,)), dma((2,)), dma((2,)), dma((2,)), dma, dma((6,)), dma, dma((micro,)), dma, dma((2,)), dma, dma, dma,
         ] + scatter_scratch(packs),
         compiler_params=pltpu.CompilerParams(collective_id=2, has_side_effects=True, vmem_limit_bytes=67043328),
     )(whole, table, x, n1, n2, qkv, probs, pre, act, mid, gout, gffn, buckets, loss)

time: 497 us -> 475 us (0.956)
  Pallas kernels: 463 us -> 446 us
    pallas_call x1, Pallas kernels: 250 us -> 232 us  [backward(): pl.pallas_call(functools.partial(backward_kernel, packs, tokens, width, s...]
where the time goes in v4:
time: 475 us
  Pallas kernels  446 us (94%)
  local copies, waits for them, and re-layouts  18.7 us (4%)
  other arithmetic  6.84 us (1%)
    pallas_call x1, Pallas kernels, backward(): pl.pallas_call(functools.partial(backward_kernel, packs, tokens, width, s...  232 us
    pallas_call x1, Pallas kernels, forward(): pl.pallas_call(functools.partial(forward_kernel, packs, tokens, width, se...  214 us

profile of v4, /device:TPU:0, one launch (start us, length us, event | category | flops | bytes accessed | tf_op | source)
XLA Modules:
  0.0 474.6 jit_solution(2246570536434910666)
XLA Ops:
  0.7 1.2 pad_slice_fusion.2
  2.0 1.3 pad_slice_fusion
  3.3 0.0 copy-done.2
  3.3 0.0 copy-done.3
  3.3 0.0 copy-done.4
  3.3 1.9 concatenate.15.own
  5.2 0.1 convert_dynamic-update-slice_fusion
  5.3 0.1 convert_dynamic-update-slice_fusion.1
  5.4 0.6 convert_reduce_fusion
  6.0 0.6 add.27
  6.6 0.1 pad.27.clone
  6.7 0.7 maximum_maximum_fusion.tile
  7.4 0.7 copy.37.bias_smem
  8.1 0.6 copy_bitcast_fusion
  8.7 0.9 copy.38.blocks_col
  9.6 0.9 copy.39.valid_col
  10.6 213.8 %shard_map.255 = (bf16[4,1536,3840]{2,1,0:T(8,128)(2,1)}, f32[32,8,128]{2,1,0:T(8,128)}, bf16[1536,768]{1,0:T(8,128)(2,1)}, bf16[1536,768]{1,0:T(8,128)(2,1)}, b...) custom-call(bf16[192,3840]{1,0:T(8,128)(2,1)} %concatenate.15.own, ...), custom_call_target="tpu_custom_call" | custom-call | tf_op jit(solution)/shard_map/pallas_call | solution.py:1151
  224.4 232.0 %shard_map.256 = (bf16[4,1536,3840]{2,1,0:T(8,128)(2,1)}, f32[192,3840]{1,0:T(8,128)}, bf16[768,1536]{1,0:T(8,128)(2,1)}, f32[32,8,128]{2,1,0:T(8,128)}, f32[32,...) custom-call(bf16[4,1536,3840]{2,1,0:T(8,128)(2,1)} %get-tuple-element.30.whole, f32[32,8,128]{2,1,0:T(8,128)} %get-tuple-element.31.table, ...), custom_call_target="tpu_custom_call" | custom-call | tf_op jit(solution)/shard_map/pallas_call | solution.py:1474
  456.4 0.9 reduce_sum.28
  457.4 0.5 slice.129
  457.9 1.5 slice_reduce_fusion
  460.7 0.6 dynamic_slice.6
  461.3 2.2 fusion.1
  463.5 0.6 dynamic_slice.7
  464.1 1.9 fusion
  466.0 1.0 pad_maximum_fusion.6
  466.9 1.0 pad_maximum_fusion.3
  467.9 1.0 pad_maximum_fusion
  468.9 0.7 reshape.86
  469.6 1.4 copy.53
  471.0 1.1 copy-done.1
  472.1 1.4 copy.54
  (23 shorter events, 0.1 us)
Async XLA Ops:
  0.6 2.6 copy-start.2
  0.7 2.6 copy-start.3
  0.7 2.6 copy-start.4
  0.7 2.6 copy-start.5
  0.7 4.5 copy-start.9
  0.7 4.6 copy-start.10
  0.7 4.7 copy-start.6
  0.7 6.7 %copy-start.8 = (bf16[32,12]{0,1:T(8,128)(2,1)S(1)}, bf16[32,12]{0,1:T(8,128)(2,1)}, u32[]{:S(2)}) copy-start(bf16[32,12]{0,1:T(8,128)(2,1)} %param.31) | copy-start | bytes 2308
  0.7 7.4 %copy-start.7 = (s32[2,1,384]{2,1,0:T(1,128)S(1)}, s32[2,1,384]{2,1,0:T(1,128)}, u32[]{:S(2)}) copy-start(s32[2,1,384]{2,1,0:T(1,128)} %param.20) | copy-start | bytes 9220
  466.0 3.6 copy-start
  469.6 2.5 copy-start.1

commit v5 on v4

--- a/solution.py
+++ b/solution.py
@@ -1169,10 +1169,13 @@
 
 def prepare(weights, gain_one, gain_two, valid):
     part = weights[4].shape[1]
-    pads = [jnp.pad(w, ((0, 0), (0, 4 * CHUNK - part))) for w in weights[4:]]
+    blank = jnp.zeros((ROWS, 4 * CHUNK - part), BF)
     pieces = list(weights[:4])
     for j in range(4):
-        pieces += [w[:, j * CHUNK : (j + 1) * CHUNK] for w in pads]
+        for w in weights[4:]:
+            pieces.append(w[:, j * CHUNK : min((j + 1) * CHUNK, part)])
+            if j == 3:
+                pieces.append(blank)
     own = jnp.concatenate(pieces, axis=1)
     me = lax.axis_index("fsdp") * 4 + lax.axis_index("dp")
     first = (me * 48) % 128

time: 475 us -> 479 us (level)
  no operation moved by 1% of the time
where the time goes in v5:
time: 479 us; the launch traced here: 478 us
  Pallas kernels  445 us (93%)
  local copies, waits for them, and re-layouts  22.5 us (5%)
  other arithmetic  6.86 us (1%)
    pallas_call x1, Pallas kernels, backward(): pl.pallas_call(functools.partial(backward_kernel, packs, tokens, width, s...  232 us
    pallas_call x1, Pallas kernels, forward(): pl.pallas_call(functools.partial(forward_kernel, packs, tokens, width, se...  214 us

profile of v5, /device:TPU:0, one launch (start us, length us, event | category | flops | bytes accessed | tf_op | source)
XLA Modules:
  0.0 478.0 jit_solution(13500620547037068579)
XLA Ops:
  0.7 1.0 fusion.4
  1.7 1.2 fusion.2
  2.9 0.9 slice.117
  3.8 0.9 slice.118
  4.7 0.9 slice.119
  5.6 3.3 concatenate.15.own
  8.9 0.1 convert_dynamic-update-slice_fusion
  9.0 0.1 convert_dynamic-update-slice_fusion.1
  9.1 0.6 convert_reduce_fusion
  9.7 0.6 add.21
  10.4 0.1 pad.14.clone
  10.5 0.7 maximum_maximum_fusion.tile
  11.1 0.7 copy.37.bias_smem
  11.8 0.6 copy_bitcast_fusion
  12.4 0.9 copy.38.blocks_col
  13.4 0.9 copy.39.valid_col
  14.3 213.8 %shard_map.255 = (bf16[4,1536,3840]{2,1,0:T(8,128)(2,1)}, f32[32,8,128]{2,1,0:T(8,128)}, bf16[1536,768]{1,0:T(8,128)(2,1)}, bf16[1536,768]{1,0:T(8,128)(2,1)}, b...) custom-call(bf16[192,3840]{1,0:T(8,128)(2,1)} %concatenate.15.own, ...), custom_call_target="tpu_custom_call" | custom-call | tf_op jit(solution)/shard_map/pallas_call | solution.py:1151
  228.1 231.7 %shard_map.256 = (bf16[4,1536,3840]{2,1,0:T(8,128)(2,1)}, f32[192,3840]{1,0:T(8,128)}, bf16[768,1536]{1,0:T(8,128)(2,1)}, f32[32,8,128]{2,1,0:T(8,128)}, f32[32,...) custom-call(bf16[4,1536,3840]{2,1,0:T(8,128)(2,1)} %get-tuple-element.30.whole, f32[32,8,128]{2,1,0:T(8,128)} %get-tuple-element.31.table, ...), custom_call_target="tpu_custom_call" | custom-call | tf_op jit(solution)/shard_map/pallas_call | solution.py:1477
  459.8 0.9 reduce_sum.28
  460.7 0.5 slice.120
  461.2 1.5 slice_reduce_fusion
  464.1 0.6 dynamic_slice.6
  464.7 2.2 fusion.1
  466.9 0.6 dynamic_slice.7
  467.5 1.9 fusion
  469.3 1.0 pad_maximum_fusion.6
  470.3 1.0 pad_maximum_fusion.3
  471.3 1.0 pad_maximum_fusion
  472.3 0.7 reshape.86
  472.9 1.4 copy.53
  474.3 1.1 copy-done.1
  475.5 1.4 copy.54
  (19 shorter events, 0.1 us)
Async XLA Ops:
  0.6 8.3 %copy-start.5 = (bf16[48]{0:T(256)(128)(2,1)S(1)}, bf16[48]{0:T(256)(128)(2,1)}, u32[]{:S(2)}) copy-start(bf16[48]{0:T(256)(128)(2,1)} %param.27) | copy-start | bytes 292
  0.7 8.4 %copy-start.6 = (bf16[48]{0:T(256)(128)(2,1)S(1)}, bf16[48]{0:T(256)(128)(2,1)}, u32[]{:S(2)}) copy-start(bf16[48]{0:T(256)(128)(2,1)} %param.22) | copy-start | bytes 292
  0.7 8.5 %copy-start.2 = (s32[2,1,384]{2,1,0:T(1,128)S(1)}, s32[2,1,384]{2,1,0:T(1,128)}, u32[]{:S(2)}) copy-start(s32[2,1,384]{2,1,0:T(1,128)} %param.19) | copy-start | bytes 9220
  0.7 10.5 %copy-start.4 = (bf16[32,12]{0,1:T(8,128)(2,1)S(1)}, bf16[32,12]{0,1:T(8,128)(2,1)}, u32[]{:S(2)}) copy-start(bf16[32,12]{0,1:T(8,128)(2,1)} %param.31) | copy-start | bytes 2308
  0.7 11.2 %copy-start.3 = (s32[2,1,384]{2,1,0:T(1,128)S(1)}, s32[2,1,384]{2,1,0:T(1,128)}, u32[]{:S(2)}) copy-start(s32[2,1,384]{2,1,0:T(1,128)} %param.20) | copy-start | bytes 9220
  469.3 3.6 copy-start
  472.9 2.5 copy-start.1
